TPU v7x, 32 devices: a whole 2x2x4 slice. The times are simulated.
32 devices in a mesh: runs: 2 (over x), modes: 16 (over z, y, core).
Axes of the slice: x: 2, y: 2, z: 4, core: 2. Of those that a mesh axis runs over, the one named last changes fastest.
Arguments:
- amplitudes: float32 [8192, 2, 5, 512], P(('runs', 'modes')), parts along dimension 0, may hold values from -6 to 6
- mode_table: int32 [4096, 2], replicated, may hold values from 0 to 127, as said below
- slab_map: int32 [8], replicated, may hold values from 0 to 7, each once
- base_flow: float32 [1024], P('runs'), parts along dimension 0, may hold values from 0 to 1.5
- base_coupling: float32 [50, 512], P('runs'), parts along dimension 0, may hold values from -0.36 to 0.36
- slab_inverse: float32 [8, 64, 64], replicated
- wall_operator: float32 [64, 64], replicated, may hold values from -0.75 to 0.75
Outputs:
- marched: float32 [8192, 2, 5, 512], P(('runs', 'modes')), parts along dimension 0
There are 2 independent parts, one for each index of `runs`. A program takes and returns all parts, laid end to end along the dimension named above; an argument that names none is the same for every part. Nothing has to cross between parts.
Inputs may be any that keep to these rules, and one draw needn't show every extreme that they name: `mode_table`: every cell of the 32 x 128 grid is named by exactly one mode; column 0 lies in 0 to 31. `slab_map`: each subdomain has its own slot.
All inputs are finite; a program needn't handle non-finite values.
Results may differ from a plain program's by a relative error of at most 0.0003.
Values sent between devices are 32-bit elements; how exact they have to be, the bound alone decides.
No kernel may reach another device: no remote copies, remote signals or barrier semaphores. Data moves between devices by JAX's collectives and lax.ppermute only.
A program may use at most 192 MiB of HBM per device.

v0:
```python
import math

import jax
import jax.numpy as jnp
from jax import lax
from jax.sharding import PartitionSpec as P

M = 4096
NB = 128
SWEEPS = 3
NW = 32


precise = lax.Precision.HIGHEST
omega_step = 0.01
phase_gain = 0.2
march_step = 0.2
coupling = 0.3


def twiddle(length):
    counter = jnp.arange(length, dtype=jnp.int32)
    product = counter[:, None] * counter[None, :] % length
    angles = product.astype(jnp.float32) * (2.0 * math.pi / length)
    return (jnp.cos(angles), jnp.sin(angles))


def mode_tables(mode_table):
    omega_index = mode_table[:, 0]
    beta_index = mode_table[:, 1]
    signed = jnp.where(beta_index >= NB // 2, beta_index - NB, beta_index)
    wavenum = 2.0 * signed.astype(jnp.float32) / NB
    frequency = omega_step * omega_index.astype(jnp.float32)
    grid_pos = omega_index * NB + beta_index
    mode_at = jnp.zeros((M,), jnp.int32).at[grid_pos].set(jnp.arange(M, dtype=jnp.int32))
    return (wavenum, frequency, grid_pos, mode_at)


def synthesize(real_part, imag_part, tables, factor):
    cos_omega, sin_omega, cos_beta, sin_beta = tables
    mixed_re = jnp.einsum("...wb,bz->...wz", real_part, cos_beta, precision=precise) - jnp.einsum(
        "...wb,bz->...wz", imag_part, sin_beta, precision=precise
    )
    mixed_im = jnp.einsum("...wb,bz->...wz", real_part, sin_beta, precision=precise) + jnp.einsum(
        "...wb,bz->...wz", imag_part, cos_beta, precision=precise
    )
    physical = jnp.einsum("...wz,wt->...tz", mixed_re, cos_omega, precision=precise) - jnp.einsum(
        "...wz,wt->...tz", mixed_im, sin_omega, precision=precise
    )
    return physical * factor


def analyze(physical, tables, factor):
    cos_omega, sin_omega, cos_beta, sin_beta = tables
    half_re = jnp.einsum("...tz,zb->...tb", physical, cos_beta, precision=precise)
    half_im = -jnp.einsum("...tz,zb->...tb", physical, sin_beta, precision=precise)
    coef_re = jnp.einsum("...tb,tw->...wb", half_re, cos_omega, precision=precise) + jnp.einsum(
        "...tb,tw->...wb", half_im, sin_omega, precision=precise
    )
    coef_im = jnp.einsum("...tb,tw->...wb", half_im, cos_omega, precision=precise) - jnp.einsum(
        "...tb,tw->...wb", half_re, sin_omega, precision=precise
    )
    return (coef_re * factor, coef_im * factor)


def forcing(normal_vel, spanwise_vel, wall_grad, span_grad, tables, factor):
    vel_v = synthesize(normal_vel[0], normal_vel[1], tables, factor)
    vel_w = synthesize(spanwise_vel[0], spanwise_vel[1], tables, factor)
    grad_y = synthesize(wall_grad[0], wall_grad[1], tables, factor)
    grad_z = synthesize(span_grad[0], span_grad[1], tables, factor)
    product = -(vel_v[None] * grad_y + vel_w[None] * grad_z)
    return analyze(product, tables, factor)


def wall_derivative(values, wall_operator):
    slab_width = wall_operator.shape[0]
    slab_count = values.shape[3] // slab_width
    blocks = values.reshape(values.shape[:3] + (slab_count, slab_width))
    return jnp.einsum("ij,abcsj->abcsi", wall_operator, blocks, precision=precise).reshape(
        values.shape
    )


def interface_table(slab_map, slab_count, slab_width):
    inverse = (
        jnp.zeros((slab_count,), jnp.int32)
        .at[slab_map]
        .set(jnp.arange(slab_count, dtype=jnp.int32))
    )
    position = jnp.arange(slab_count * slab_width, dtype=jnp.int32)
    slot_of = position // slab_width
    within = position % slab_width
    domain = inverse[slot_of]
    below = slab_map[jnp.maximum(domain - 1, 0)] * slab_width + (slab_width - 1)
    above = slab_map[jnp.minimum(domain + 1, slab_count - 1)] * slab_width
    lower_ok = (within == 0) & (domain > 0)
    upper_ok = (within == slab_width - 1) & (domain < slab_count - 1)
    source = jnp.where(lower_ok, below, jnp.where(upper_ok, above, 0))
    weight = (lower_ok | upper_ok).astype(jnp.float32)
    return (source, weight)


def relaxation(iterate, right_side, rotation, matrix, slab_inverse, source, weight):
    slab_count = slab_inverse.shape[0]
    slab_width = slab_inverse.shape[1]
    coupled = jnp.einsum("kjy,acjy->acky", matrix, iterate, precision=precise)
    applied = jnp.stack(
        [
            coupled[:, 0] - rotation[:, None, :] * iterate[:, 1],
            coupled[:, 1] + rotation[:, None, :] * iterate[:, 0],
        ],
        1,
    )
    rims = jnp.take(iterate, source, axis=3) * weight
    residual_in = right_side - applied + coupling * rims
    blocks = residual_in.reshape(iterate.shape[:3] + (slab_count, slab_width))
    return jnp.einsum("sij,acvsj->acvsi", slab_inverse, blocks, precision=precise).reshape(
        iterate.shape
    )


def local(amplitudes, mode_table, slab_map, base_flow, base_coupling, slab_inverse, wall_operator):
    local_modes = amplitudes.shape[0]
    wall_points = amplitudes.shape[3]
    groups = lax.axis_size("modes")
    point_share = wall_points // groups
    wavenum, frequency, grid_pos, mode_at = mode_tables(mode_table)
    first_mode = lax.axis_index("modes") * local_modes
    wave_local = lax.dynamic_slice_in_dim(wavenum, first_mode, local_modes)
    freq_local = lax.dynamic_slice_in_dim(frequency, first_mode, local_modes)
    tables = twiddle(NW) + twiddle(NB)
    factor = 1.0 / math.sqrt(M)
    source, weight = interface_table(slab_map, slab_inverse.shape[0], slab_inverse.shape[1])
    matrix = base_coupling.reshape(5, 5, wall_points)
    gradient = wall_derivative(amplitudes, wall_operator)
    span = jnp.stack(
        [
            -wave_local[:, None, None] * amplitudes[:, 1],
            wave_local[:, None, None] * amplitudes[:, 0],
        ],
        1,
    )
    fields = jnp.concatenate([amplitudes[:, :, 2:4], gradient, span], 2)
    field_count = fields.shape[2]
    channels = 2 * field_count
    outgoing = jnp.transpose(
        fields.reshape(local_modes, channels, groups, point_share), (1, 2, 3, 0)
    ).reshape(channels, groups, point_share * local_modes)
    incoming = lax.all_to_all(outgoing, "modes", split_axis=1, concat_axis=1, tiled=True)
    by_mode = jnp.transpose(
        incoming.reshape(channels, groups, point_share, local_modes), (0, 2, 1, 3)
    ).reshape(channels, point_share, M)
    gridded = by_mode[..., mode_at].reshape(2, field_count, point_share, NW, NB)
    normal_vel = gridded[:, 0]
    spanwise_vel = gridded[:, 1]
    wall_grad = gridded[:, 2:7]
    span_grad = gridded[:, 7:12]
    mean_crossflow = lax.all_gather(spanwise_vel[0, :, 0, 0], "modes", axis=0, tiled=True)
    coef_re, coef_im = forcing(normal_vel, spanwise_vel, wall_grad, span_grad, tables, factor)
    packed = jnp.stack([coef_re, coef_im], 0).reshape(10, point_share, M)[..., grid_pos]
    sendback = jnp.transpose(
        packed.reshape(10, point_share, groups, local_modes), (0, 2, 1, 3)
    ).reshape(10, groups, point_share * local_modes)
    returned = lax.all_to_all(sendback, "modes", split_axis=1, concat_axis=1, tiled=True)
    nonlinear = jnp.transpose(
        returned.reshape(10, groups, point_share, local_modes), (3, 0, 1, 2)
    ).reshape(local_modes, 2, 5, wall_points)
    crossflow = base_flow + mean_crossflow
    rotation = phase_gain * wave_local[:, None] * crossflow[None, :] - freq_local[:, None]
    right_side = amplitudes + march_step * nonlinear
    iterate = amplitudes
    for sweep_index in range(SWEEPS):
        iterate = relaxation(iterate, right_side, rotation, matrix, slab_inverse, source, weight)
    return iterate


def solution(mesh):
    return jax.shard_map(
        local,
        mesh=mesh,
        in_specs=(
            P(("runs", "modes"), None, None, None),
            P(),
            P(),
            P("runs"),
            P("runs", None),
            P(),
            P(),
        ),
        out_specs=P(("runs", "modes"), None, None, None),
        check_vma=False,
    )
```

profile of v0, /device:TPU:13, one launch (start us, length us, event | category | flops | bytes accessed | tf_op | source)
XLA Modules:
  0.0 1125.1 jit_solution(16035738039939335785)
XLA Ops:
  0.0 9.0 copy.115
  9.0 8.7 copy.102
  44.1 17.6 %copy.106 = f32[256,2,12,512]{0,3,2,1:T(8,128)} copy(f32[256,2,12,512]{0,2,1,3:T(8,128)} %maximum_maximum_fusion) | data formatting | bytes 25165824 | tf_op jit(solution)/shard_map/concatenate | solution.py:143
  61.7 14.2 %reshape.217 = f32[24,16,8192]{2,1,0:T(8,128)} reshape(f32[24,16,32,256]{3,2,1,0:T(8,128)} %bitcast.293) | data formatting | bytes 25165824 | tf_op jit(solution)/shard_map/reshape | solution.py:148
  75.9 16.4 %copy.107 = f32[24,16,8192]{2,0,1:T(8,128)} copy(f32[24,16,8192]{2,1,0:T(8,128)} %reshape.217) | data formatting | bytes 25165824 | tf_op jit(solution)/shard_map/reshape | solution.py:148
  98.8 15.7 %scatter_custom_fusion = s32[4096]{0:T(1024)S(1)} fusion(s32[4096]{0:T(1024)S(1)} %bitcast.308, s32[4096]{0:T(1024)S(1)} %iota.30, s32[]{:T(128)} %constant.98.clone.1), kind=kCustom, calls=%fused_computation.165 | custom fusion | bytes 16388 | tf_op jit(solution)/shard_map/scatter | solution.py:35
  114.6 256.5 %all-to-all-done = f32[24,16,8192]{2,0,1:T(8,128)} async-done(((f32[24,16,8192]{2,0,1:T(8,128)}), f32[24,16,8192]{2,0,1:T(8,128)}, u32[]{:S(2)}, u32[]{:S(2)}) %all-to-all-start) | async-done | bytes 12582944 | tf_op jit(solution)/shard_map/all_to_all | solution.py:149
  371.0 14.6 %copy.146 = f32[48,8,32,256]{3,2,1,0:T(8,128)} copy(f32[48,8,32,256]{3,1,2,0:T(8,128)} %bitcast.101) | data formatting | bytes 25165824
  385.7 29.6 %copy.138 = f32[24,32,16,256]{1,0,3,2:T(8,128)} copy(f32[24,32,16,256]{3,1,0,2:T(8,128)} %bitcast.294) | data formatting | bytes 25165824 | tf_op jit(solution)/shard_map/reshape | solution.py:152
  415.3 86.4 %gather_fusion = f32[4096,24,32]{2,1,0:T(8,128)} fusion(f32[24,32,4096]{1,0,2:T(8,128)} %bitcast.291, s32[4096]{0:T(1024)S(1)} %fusion.115), kind=kCustom, calls=%fused_computation.3 | custom fusion | bytes 25182208 | tf_op jit(solution)/shard_map/gather | solution.py:153
  501.6 32.3 %copy.110 = f32[24,32,4096]{2,1,0:T(8,128)} copy(f32[24,32,4096]{1,0,2:T(8,128)} %bitcast.292) | data formatting | bytes 25165824 | tf_op jit(solution)/shard_map/gather | solution.py:153
  534.0 12.0 %copy.147 = f32[96,8,32,128]{3,2,1,0:T(8,128)} copy(f32[96,8,32,128]{3,1,2,0:T(8,128)} %bitcast.295) | data formatting | bytes 25165824
  621.5 22.0 %copy.111 = f32[10,32,4096]{1,0,2:T(8,128)} copy(f32[10,32,4096]{2,1,0:T(8,128)} %reshape.221) | data formatting | bytes 10485760 | tf_op jit(solution)/shard_map/reshape | solution.py:160
  643.5 78.3 %gather_fusion.1 = f32[4096,10,32]{2,1,0:T(8,128)} fusion(f32[10,32,4096]{1,0,2:T(8,128)} %copy.111, s32[4096]{0:T(1024)S(1)} %broadcast_clamp_fusion), kind=kCustom, calls=%fused_computation.4 | custom fusion | bytes 10502144 | tf_op jit(solution)/shard_map/gather | solution.py:160
  721.8 21.3 %copy.112 = f32[10,32,16,256]{3,1,2,0:T(8,128)} copy(f32[10,32,16,256]{1,0,3,2:T(8,128)} %bitcast.296) | data formatting | bytes 10485760 | tf_op jit(solution)/shard_map/reshape | solution.py:162
  750.0 9.0 copy.113
  791.9 11.8 %convolution_bitcast_fusion.2 = f32[256,2,5,512]{0,2,1,3:T(8,128)} fusion(f32[256,2,5,512]{0,2,1,3:T(8,128)} %copy.115, f32[5,5,512,1]{1,0,3,2:T(8,128)S(1)} %copy.134), kind=kOutput, calls=%fused_computation.43 | convolution fusion | flops 78643200 | bytes 10536960 | tf_op jit(solution)/shard_map/kjy,acjy->acky/dot_general | solution.py:106
  805.6 157.4 %all-reduce = f32[512]{0:T(512)S(1)} all-reduce(f32[512]{0:T(512)S(1)} %dynamic-update-slice), channel_id=2, replica_groups=mesh['runs'=2,'modes'=16] {'modes'}, use_global_device_ids=true, to_apply=%add | all-reduce | flops 512 | bytes 4096 | tf_op jit(solution)/shard_map/all_gather | solution.py:158
  964.0 10.0 slice_subtract_fusion
  985.5 11.0 fusion
  996.6 8.4 fusion.38
  1011.4 9.8 convolution_bitcast_fusion.1
  1021.2 7.8 gather_fusion.3
  1029.1 8.8 fusion.15
  1040.2 10.4 fusion.1
  1050.6 8.4 fusion.41
  1065.5 9.9 convolution_bitcast_fusion
  1075.4 7.9 gather_fusion.4
  1083.3 8.7 fusion.13
  1094.3 10.5 fusion.2
  1104.8 8.4 fusion.44
  1115.8 8.8 copy.128
  (126 shorter events, 181.9 us)
Async XLA Ops:
  0.0 996.6 %copy-start = (f32[8,64,64]{2,1,0:T(8,128)S(1)}, f32[8,64,64]{2,1,0:T(8,128)}, u32[]{:S(2)}) copy-start(f32[8,64,64]{2,1,0:T(8,128)} %param.14) | copy-start | bytes 393220
  9.0 8.7 copy-start.13
  19.0 8.8 slice-start.4
  23.6 4.1 slice-start.5
  23.6 4.1 copy-start.12
  92.3 278.8 %all-to-all-start = ((f32[24,16,8192]{2,0,1:T(8,128)}), f32[24,16,8192]{2,0,1:T(8,128)}, u32[]{:S(2)}, u32[]{:S(2)}) async-start(f32[24,16,8192]{2,0,1:T(8,128)} %copy.107), calls=%async_computation | async-start | bytes 25165824 | tf_op jit(solution)/shard_map/all_to_all | solution.py:149
  547.8 14.8 %copy-start.3 = (f32[96,8,32,128]{3,2,1,0:T(8,128)S(1)}, f32[96,8,32,128]{3,2,1,0:T(8,128)}, u32[]{:S(2)}) copy-start(f32[96,8,32,128]{3,2,1,0:T(8,128)} %copy.147) | copy-start | bytes 37748740
  759.0 5.0 copy-start.14
  759.0 214.9 %all-to-all-start.1 = ((f32[10,16,8192]{2,0,1:T(8,128)}), f32[10,16,8192]{2,0,1:T(8,128)}, u32[]{:S(2)}, u32[]{:S(2)}) async-start(f32[10,16,8192]{2,0,1:T(8,128)} %copy.113), calls=%async_computation.1 | async-start | bytes 16777216 | tf_op jit(solution)/shard_map/all_to_all | solution.py:164
  781.4 7.8 copy-start.11
  781.4 8.6 copy-start.17
  791.9 171.1 %copy-start.16 = (f32[512]{0:T(512)S(1)}, f32[512]{0:T(512)}, u32[]{:S(2)}) copy-start(f32[512]{0:T(512)} %param.12) | copy-start | bytes 6148
  791.9 171.1 %copy-start.15 = (f32[256]{0:T(256)S(1)}, f32[256]{0:T(256)}, u32[]{:S(2)}) copy-start(f32[256]{0:T(256)} %get-tuple-element.8) | copy-start | bytes 3076
  963.1 0.9 copy-start.9
  980.7 2.2 copy-start.7
  980.7 4.8 copy-start.8
  982.6 14.0 %copy-start.4 = (f32[20,8,32,256]{3,2,1,0:T(8,128)}, f32[20,8,32,256]{3,2,1,0:T(8,128)S(1)}, u32[]{:S(2)}) copy-start(f32[20,8,32,256]{3,2,1,0:T(8,128)S(1)} %copy.148) | copy-start | bytes 15728644
  1008.1 3.3 copy-start.2
  1021.2 16.6 %slice-start = ((s8[5242880]{0:T(1024)(128)(4,1)}), s8[1048576]{0:T(1024)(128)(4,1)S(1)}, s32[]{:S(2)}) async-start(s8[5242880]{0:T(1024)(128)(4,1)} %bitcast.285), calls=%async_computation.2 | async-start | bytes 2097152
  1029.1 8.8 slice-start.1
  1029.1 11.2 copy-start.6
  1062.2 3.3 copy-start.1
  1075.4 7.9 copy-start.10
  1075.4 16.6 %slice-start.2 = ((s8[5242880]{0:T(1024)(128)(4,1)}), s8[1048576]{0:T(1024)(128)(4,1)S(1)}, s32[]{:S(2)}) async-start(s8[5242880]{0:T(1024)(128)(4,1)} %bitcast.288), calls=%async_computation.4 | async-start | bytes 2097152
  1083.3 8.7 slice-start.3
  1083.3 11.0 copy-start.5
where the time goes:
time: 1140 us; the launch traced here: 1130 us
  local copies, waits for them, and re-layouts  472 us (41%)
  waiting for transfers between devices  256 us (22%)
  blocking collectives  157 us (14%)
  matrix products  127 us (11%)
  other arithmetic  98.3 us (9%)
  starting transfers between devices  11.6 us (1%)
    all_to_all x1, waiting for transfers between devices, local(): lax.all_to_all(outgoing, 'modes', split_axis=1, concat_axis=1, tiled=True)  256 us
    all_gather x1, blocking collectives, local(): lax.all_gather(spanwise_vel[0, :, 0, 0], 'modes', axis=0, tiled=True)  157 us
    gather x2, local copies, waits for them, and re-layouts, local(): gridded = by_mode[..., mode_at].reshape(2, field_count, point_share, NW, NB)  119 us
    gather x1, local copies, waits for them, and re-layouts, local(): jnp.stack([coef_re, coef_im], 0).reshape(10, point_share, M)[..., grid_pos]  78.3 us
    unnamed x56, local copies, waits for them, and re-layouts  62 us
    add x3, other arithmetic, relaxation(): residual_in = right_side - applied + coupling * rims  31.9 us
    dot_general x3, matrix products, relaxation(): coupled = jnp.einsum('kjy,acjy->acky', matrix, iterate, precision=precise)  31.5 us
    reshape x2, local copies, waits for them, and re-layouts, local(): outgoing = jnp.transpose(fields.reshape(local_modes, channels, groups, po...  30.6 us
  transfers between devices with their start and end apart: 2, of which 1 were waited for; matrix products, arithmetic and copies ran while one was open for 6% of the time, Pallas kernels for 0%

commit v1 on v0

--- a/solution.py
+++ b/solution.py
@@ -1,8 +1,12 @@
+import functools
 import math
 
 import jax
 import jax.numpy as jnp
+import numpy as np
 from jax import lax
+from jax.experimental import pallas as pl
+from jax.experimental.pallas import tpu as pltpu
 from jax.sharding import PartitionSpec as P
 
 M = 4096
@@ -174,9 +178,594 @@
     return iterate
 
 
+LANES = 128
+SHARE = 32
+SLAB = 64
+HALF = NW // 2
+TIMES = HALF + 1
+BLOCKS = LANES // SHARE
+STRIPES = 4
+PARTS = 10
+TILE = 32
+VMEM_LIMIT = 60 * 1024 * 1024
+
+
+def roll(x, shift):
+    return pltpu.roll(x, shift % LANES, x.ndim - 1)
+
+
+def lane_index(shape):
+    return lax.broadcasted_iota(jnp.int32, shape, len(shape) - 1)
+
+
+def lane_masks(shape):
+    lane = lane_index(shape)
+    return (lane < 64, (lane & 32) == 0)
+
+
+def real_sign(shape):
+    return jnp.where(lane_index(shape) < 64, 1.0, -1.0).astype(jnp.float32)
+
+
+def block_transpose(rows, low, even):
+    r0, r1, r2, r3 = rows
+    t0 = jnp.where(low, r0, roll(r2, 64))
+    t2 = jnp.where(low, roll(r0, 64), r2)
+    t1 = jnp.where(low, r1, roll(r3, 64))
+    t3 = jnp.where(low, roll(r1, 64), r3)
+    return (
+        jnp.where(even, t0, roll(t1, 32)),
+        jnp.where(even, roll(t0, 96), t1),
+        jnp.where(even, t2, roll(t3, 32)),
+        jnp.where(even, roll(t2, 96), t3),
+    )
+
+
+def split(x):
+    high = x.astype(jnp.bfloat16)
+    return high, (x - high.astype(jnp.float32)).astype(jnp.bfloat16)
+
+
+def dot(a, b):
+    return jnp.dot(a, b, preferred_element_type=jnp.float32)
+
+
+def cosine_sine(inputs, length, table, sign, real):
+    if length == 4:
+        first, middle, last = inputs
+        middle_re = middle * real
+        total = first + last
+        return [total + middle_re, (first - last) + (middle - middle_re), total - middle_re]
+    step = NW // length
+    quarter = length // 4
+    even = cosine_sine(inputs[0::2], length // 2, table, sign, real)
+    odd_inputs = [(a, inputs[a]) for a in range(1, length // 2, 2)]
+    odd = []
+    for t in range(quarter + 1):
+        if t == 0:
+            total = odd_inputs[0][1]
+            for _, value in odd_inputs[1:]:
+                total = total + value
+            odd.append(total * real)
+        elif t == quarter:
+            total = odd_inputs[0][1]
+            for a, value in odd_inputs[1:]:
+                total = total + value if a % 4 == 1 else total - value
+            odd.append(total - total * real)
+        else:
+            total = None
+            for a, value in odd_inputs:
+                term = table(a * t * step % NW) * value
+                total = term if total is None else total + term
+            odd.append(total)
+    out = [None] * (length // 2 + 1)
+    for t in range(quarter + 1):
+        out[t] = even[t] + odd[t]
+        out[length // 2 - t] = sign * (even[t] - odd[t])
+    out[quarter] = even[quarter] + odd[quarter]
+    return out
+
+
+def pack_rows(a_ref, o_ref, base, first, second, second_base, count, row, low, even):
+    for stripe in range(STRIPES):
+        rows = []
+        for part in range(2):
+            for variable, start in ((first, base), (second, second_base)):
+                offset = variable * 2 * STRIPES + stripe * 2 + part
+                rows.append(a_ref[pl.ds(start * 2 * STRIPES * 5 + offset, count, stride=2 * STRIPES * 5), :])
+        for block, value in enumerate(block_transpose(rows, low, even)):
+            o_ref[stripe * BLOCKS + block, pl.ds(row, count), :] = value
+
+
+def pack_velocity(a_ref, o_ref):
+    low, even = lane_masks((TILE, LANES))
+
+    def body(i, carry):
+        base = pl.multiple_of(i * TILE, TILE)
+        pack_rows(a_ref, o_ref, base, 2, 3, base, TILE, base, low, even)
+        return carry
+
+    lax.fori_loop(0, o_ref.shape[1] // TILE, body, 0)
+
+
+def pack_others(a_ref, o_ref):
+    low, even = lane_masks((TILE, LANES))
+    modes = o_ref.shape[1] // 3 * 2
+
+    def body(i, carry):
+        base = pl.multiple_of(i * TILE, TILE)
+        pack_rows(a_ref, o_ref, base, 0, 1, base, TILE, base, low, even)
+        return carry
+
+    def last_body(i, carry):
+        base = pl.multiple_of(i * TILE, TILE)
+        pack_rows(a_ref, o_ref, base, 4, 4, base + modes // 2, TILE, modes + base, low, even)
+        return carry
+
+    lax.fori_loop(0, modes // TILE, body, 0)
+    lax.fori_loop(0, modes // 2 // TILE, last_body, 0)
+
+
+UNROLL = 16
+
+
+def synthesis(with_mean, pos_ref, r_ref, w_ref, tab_ref, *refs):
+    if with_mean:
+        f_ref, g_ref, mean_ref, grid_ref, spec_ref = refs
+        last_ref = None
+        modes = r_ref.shape[1]
+    else:
+        f_ref, g_ref, grid_ref, spec_ref, last_ref = refs
+        modes = r_ref.shape[1] // 3 * 2
+    groups = r_ref.shape[0]
+    sign = real_sign((8, LANES))
+    real = jnp.where(lane_index((8, LANES)) < 64, 1.0, 0.0).astype(jnp.float32)
+    wide_sign = real_sign((NB, LANES))
+
+    def table(j):
+        return tab_ref[j]
+
+    def scatter(source):
+        chunks = modes // UNROLL
+
+        def body(i, carry):
+            group = i // chunks
+            start = (i % chunks) * UNROLL
+            for j in range(UNROLL):
+                cell = pos_ref[i * UNROLL + j]
+                grid_ref[pl.ds(cell, 1), :] = source[group, pl.ds(start + j, 1), :]
+            return carry
+
+        lax.fori_loop(0, groups * chunks, body, 0)
+
+    for pair in range(f_ref.shape[0]):
+        if pair == 0:
+            scatter(r_ref)
+        else:
+
+            def unpack(group, carry):
+                rows = r_ref[group, pl.ds(modes, modes // 2), :]
+                last_ref[group, pl.ds(0, modes // 2), :] = rows
+                last_ref[group, pl.ds(modes // 2, modes // 2), :] = roll(rows, 96)
+                return carry
+
+            lax.fori_loop(0, groups, unpack, 0)
+            scatter(last_ref)
+        if with_mean:
+            mean_ref[...] = grid_ref[pl.ds(0, 8), :]
+
+        def beta(i, carry):
+            columns = []
+            for j in range(2):
+                x = grid_ref[pl.ds(pl.multiple_of((2 * i + j) * NB, NB), NB), :]
+                columns.append(jnp.concatenate([x, -wide_sign * roll(x, 64)], 0))
+            high, low_part = split(jnp.concatenate(columns, 1))
+            product = dot(w_ref[...], high)
+            out = product[: 2 * NB] + product[2 * NB :] + dot(w_ref[pl.ds(0, 2 * NB), :], low_part)
+            spec_ref[2 * i] = out[:, :LANES]
+            spec_ref[2 * i + 1] = out[:, LANES:]
+            return carry
+
+        lax.fori_loop(0, NW // 2, beta, 0)
+
+        def omega(out_ref, shift):
+            def body(i, carry):
+                rows = pl.ds(pl.multiple_of(i * 8, 8), 8)
+                source = pl.ds(pl.multiple_of(shift + i * 8, 8), 8)
+                coefs = [spec_ref[a, source, :] for a in range(NW)]
+                inputs = [coefs[0] * real]
+                for a in range(1, HALF):
+                    inputs.append(coefs[a] + sign * coefs[NW - a])
+                inputs.append(coefs[HALF] * real)
+                for t, value in enumerate(cosine_sine(inputs, NW, table, sign, real)):
+                    out_ref[pair, t, rows, :] = value - sign * roll(value, 64)
+                return carry
+
+            lax.fori_loop(0, NB // 8, body, 0)
+
+        omega(f_ref, 0)
+        omega(g_ref, NB)
+
+
+def force_analysis(with_mean, pos_ref, vw_ref, f_ref, s_ref, g_ref, d_ref, w_ref, tab_ref, *refs):
+    if with_mean:
+        mean_ref, o_ref, k_ref, n_ref = refs
+        last_ref = None
+        modes = o_ref.shape[1] - 8
+    else:
+        o_ref, k_ref, n_ref, last_ref = refs
+        modes = o_ref.shape[1] // 3 * 2
+    groups = o_ref.shape[0]
+    sign = real_sign((8, LANES))
+    real = jnp.where(lane_index((8, LANES)) < 64, 1.0, 0.0).astype(jnp.float32)
+    wide_sign = real_sign((NB, LANES))
+    wide_real, even = lane_masks((NB, LANES))
+
+    def table(j):
+        return tab_ref[j]
+
+    def gather(target):
+        chunks = modes // UNROLL
+
+        def body(i, carry):
+            group = i // chunks
+            start = (i % chunks) * UNROLL
+            for j in range(UNROLL):
+                cell = pos_ref[i * UNROLL + j]
+                target[group, pl.ds(start + j, 1), :] = n_ref[pl.ds(cell, 1), :]
+            return carry
+
+        lax.fori_loop(0, groups * chunks, body, 0)
+
+    for pair in range(f_ref.shape[0]):
+
+        def product(t, carry):
+            vw = vw_ref[0, t]
+            v = jnp.where(even, vw, roll(vw, 32))
+            w = jnp.where(even, roll(vw, 96), vw)
+            high, low_part = split(jnp.concatenate([f_ref[pair, t], s_ref[pair, t]], 1))
+            both = dot(high, d_ref[...])
+            grad = both[:, :LANES] + both[:, LANES:] + dot(low_part, d_ref[:, :LANES])
+            force = v * grad + w * g_ref[pair, t]
+            folded = force + wide_sign * roll(force, 64)
+            alone = jnp.logical_or(t == 0, t == HALF)
+            k_ref[t] = jnp.where(alone, jnp.where(wide_real, force, 0.0), folded)
+            return carry
+
+        lax.fori_loop(0, TIMES, product, 0)
+
+        def omega(i, carry):
+            rows = pl.ds(pl.multiple_of(i * 8, 8), 8)
+            inputs = [k_ref[t, rows, :] for t in range(TIMES)]
+            for a, value in enumerate(cosine_sine(inputs, NW, table, sign, real)):
+                k_ref[a, rows, :] = value
+            return carry
+
+        lax.fori_loop(0, NB // 8, omega, 0)
+
+        def beta(frequencies, columns):
+            high, low_part = split(columns)
+            both = dot(w_ref[...], high)
+            out = both[: 2 * NB] + both[2 * NB :] + dot(w_ref[pl.ds(0, 2 * NB), :], low_part)
+            for j, a in enumerate(frequencies):
+                cosine = out[:NB, j * LANES : (j + 1) * LANES]
+                sine = roll(out[NB:, j * LANES : (j + 1) * LANES], 64)
+                mirror = (NW - a) % NW
+                n_ref[pl.ds(pl.multiple_of(mirror * NB, NB), NB), :] = wide_sign * cosine - sine
+                n_ref[pl.ds(pl.multiple_of(a * NB, NB), NB), :] = cosine + wide_sign * sine
+
+        def beta_pair(i, carry):
+            beta((2 * i, 2 * i + 1), jnp.concatenate([k_ref[2 * i], k_ref[2 * i + 1]], 1))
+            return carry
+
+        lax.fori_loop(0, HALF // 2, beta_pair, 0)
+        beta((HALF,), k_ref[HALF])
+
+        if pair == 0:
+            gather(o_ref)
+        else:
+            gather(last_ref)
+
+            def join(group, carry):
+                first = last_ref[group, pl.ds(0, modes // 2), :]
+                second = last_ref[group, pl.ds(modes // 2, modes // 2), :]
+                even_half = (lane_index(first.shape) & 32) == 0
+                o_ref[group, pl.ds(modes, modes // 2), :] = jnp.where(even_half, first, roll(second, 32))
+                return carry
+
+            lax.fori_loop(0, groups, join, 0)
+
+    if with_mean:
+        for group in range(groups):
+            o_ref[group, pl.ds(modes, 8), :] = mean_ref[...]
+
+
+def relax_kernel(a_ref, b1_ref, b2_ref, base_ref, coup_ref, kz_ref, om_ref, sw_ref, o_ref, rhs_ref, x_ref, cf_ref, rh_ref, rl_ref, zh_ref, zl_ref):
+    modes = kz_ref.shape[0]
+    stride = PARTS * STRIPES
+    low, even = lane_masks((TILE, LANES))
+    lane = lane_index((TILE, LANES))
+    edge = ((lane & 63) == 0) | ((lane & 63) == 63)
+    block_of = lane_index((1, LANES)) // SHARE
+
+    def load(start, variable, stripe, part):
+        return a_ref[pl.ds(start * stride + variable * 2 * STRIPES + stripe * 2 + part, TILE, stride=stride), :]
+
+    for stripe in range(STRIPES):
+        total = base_ref[pl.ds(stripe, 1), :]
+        for block in range(BLOCKS):
+            row = b1_ref[stripe * BLOCKS + block, pl.ds(modes, 1), :]
+            total = total + jnp.where(block_of == block, roll(row, SHARE * (block - 1)), 0.0)
+        cf_ref[pl.ds(stripe, 1), :] = total
+
+    def unpack(ref, row, targets):
+        for stripe in range(STRIPES):
+            rows = [ref[stripe * BLOCKS + block, pl.ds(row, TILE), :] for block in range(BLOCKS)]
+            values = block_transpose(rows, low, even)
+            for value, (variable, part, start) in zip(values, targets):
+                rhs_ref[stripe * PARTS + variable * 2 + part, pl.ds(start, TILE), :] = load(start, variable, stripe, part) + march_step * value
+
+    def gather_pairs(i, carry):
+        base = pl.multiple_of(i * TILE, TILE)
+        unpack(b1_ref, base, [(2, 0, base), (3, 0, base), (2, 1, base), (3, 1, base)])
+        unpack(b2_ref, base, [(0, 0, base), (1, 0, base), (0, 1, base), (1, 1, base)])
+        return carry
+
+    def gather_last(i, carry):
+        base = pl.multiple_of(i * TILE, TILE)
+        other = pl.multiple_of(modes // 2 + i * TILE, TILE)
+        unpack(b2_ref, pl.multiple_of(modes + i * TILE, TILE), [(4, 0, base), (4, 0, other), (4, 1, base), (4, 1, other)])
+        return carry
+
+    lax.fori_loop(0, modes // TILE, gather_pairs, 0)
+    lax.fori_loop(0, modes // 2 // TILE, gather_last, 0)
+
+    def tile(i, carry):
+        base = pl.multiple_of(i * TILE, TILE)
+        rows = pl.ds(base, TILE)
+        for stripe in range(STRIPES):
+            for part in range(PARTS):
+                x_ref[stripe * PARTS + part] = load(base, part // 2, stripe, part % 2)
+
+        def sweep(index, sweep_carry):
+            for part in range(PARTS):
+                rims = None
+                for stripe in range(STRIPES):
+                    term = jnp.where(edge, x_ref[stripe * PARTS + part], 0.0)
+                    term = roll(term, 2 * stripe) if stripe else term
+                    rims = term if rims is None else rims + term
+                high, low_part = split(rims)
+                zh_ref[pl.ds(part * TILE, TILE), :] = high
+                zl_ref[pl.ds(part * TILE, TILE), :] = low_part
+            for stripe in range(STRIPES):
+                values = [x_ref[stripe * PARTS + part] for part in range(PARTS)]
+                rotation = kz_ref[rows, :] * cf_ref[pl.ds(stripe, 1), :] - om_ref[rows, :]
+                for k in range(5):
+                    out_re = rhs_ref[stripe * PARTS + 2 * k, rows, :] + rotation * values[2 * k + 1]
+                    out_im = rhs_ref[stripe * PARTS + 2 * k + 1, rows, :] - rotation * values[2 * k]
+                    for j in range(5):
+                        weight = coup_ref[pl.ds((k * 5 + j) * STRIPES + stripe, 1), :]
+                        out_re = out_re - weight * values[2 * j]
+                        out_im = out_im - weight * values[2 * j + 1]
+                    for part, out in ((2 * k, out_re), (2 * k + 1, out_im)):
+                        high, low_part = split(out)
+                        rh_ref[pl.ds(part * TILE, TILE), :] = high
+                        rl_ref[pl.ds(part * TILE, TILE), :] = low_part
+                high = jnp.concatenate([rh_ref[...], zh_ref[...]], 1)
+                low_rows = jnp.concatenate([rl_ref[...], zl_ref[...]], 1)
+                both = dot(high, sw_ref[stripe])
+                new = both[:, :LANES] + both[:, LANES:] + dot(low_rows, sw_ref[stripe, :, pl.ds(0, LANES)])
+                x_ref[pl.ds(stripe * PARTS, PARTS)] = new.reshape(PARTS, TILE, LANES)
+            return sweep_carry
+
+        lax.fori_loop(0, SWEEPS, sweep, 0)
+        for stripe in range(STRIPES):
+            for part in range(PARTS):
+                offset = base * stride + (part // 2) * 2 * STRIPES + stripe * 2 + part % 2
+                o_ref[pl.ds(offset, TILE, stride=stride), :] = x_ref[stripe * PARTS + part]
+        return carry
+
+    lax.fori_loop(0, modes // TILE, tile, 0)
+
+
+def split_host(x):
+    high = x.astype(jnp.bfloat16)
+    low_part = (x - high.astype(np.float64)).astype(jnp.bfloat16)
+    return high, low_part
+
+
+def beta_matrices():
+    index = np.arange(NB)
+    angles = (index[:, None] * index[None, :] % NB) * (2.0 * math.pi / NB)
+    cosine = np.cos(angles)
+    sine = np.sin(angles)
+    wave = 2.0 * np.where(index >= NB // 2, index - NB, index) / NB
+    factor = 1.0 / math.sqrt(M)
+    forward = factor * np.block([[cosine, sine], [-sine * wave, cosine * wave]])
+    backward = -factor * np.concatenate([cosine, sine], 0)
+    return tuple(np.concatenate(split_host(matrix), 0) for matrix in (forward, backward))
+
+
+def omega_table():
+    angles = np.arange(NW) * (2.0 * math.pi / NW)
+    rows = np.concatenate([np.repeat(np.cos(angles)[:, None], 64, 1), np.repeat(np.sin(angles)[:, None], 64, 1)], 1)
+    return np.repeat(rows[:, None, :], 8, 1).astype(np.float32)
+
+
+def split_device(x):
+    high = lax.reduce_precision(x, 8, 7)
+    return high.astype(jnp.bfloat16), (x - high).astype(jnp.bfloat16)
+
+
+def derivative_matrix(wall_operator, half):
+    own = lax.dynamic_slice(wall_operator, (half * SHARE, 0), (SHARE, SLAB)).T
+    mine = lax.dynamic_slice(own, (half * SHARE, 0), (SHARE, SHARE))
+    other = lax.dynamic_slice(own, ((1 - half) * SHARE, 0), (SHARE, SHARE))
+    same = jnp.eye(BLOCKS, dtype=jnp.float32)
+    stacked = jnp.stack([mine, other], 0)
+    full = same[None, :, None, :, None] * stacked[:, None, :, None, :]
+    full = full.reshape(2 * LANES, LANES)
+    return jnp.concatenate(split_device(full), 1)
+
+
+def solve_matrices(slab_map, slab_inverse):
+    count = slab_inverse.shape[0]
+    slots = jnp.arange(count, dtype=jnp.int32)
+    holds = slab_map[:, None] == slots[None, :]
+    below_of = jnp.concatenate([slab_map[:1] * 0 - 1, slab_map[:-1]])
+    above_of = jnp.concatenate([slab_map[1:], slab_map[:1] * 0 - 1])
+    below = jnp.sum(jnp.where(holds, below_of[:, None], 0), 0)
+    above = jnp.sum(jnp.where(holds, above_of[:, None], 0), 0)
+    lane = jnp.arange(LANES, dtype=jnp.int32)
+
+    def one_hot(slot, position):
+        where = (slot % 2 * SLAB + position + 2 * (slot // 2)) % LANES
+        return ((slot >= 0)[:, None] & (where[:, None] == lane[None, :])).astype(jnp.float32)
+
+    low_rim = one_hot(below, SLAB - 1)
+    high_rim = one_hot(above, 0)
+    rims = coupling * (
+        low_rim[:, :, None] * slab_inverse[:, None, :, 0] + high_rim[:, :, None] * slab_inverse[:, None, :, SLAB - 1]
+    )
+    rims = rims.reshape(STRIPES, 2, LANES, SLAB).transpose(0, 2, 1, 3).reshape(STRIPES, LANES, LANES)
+    same = jnp.eye(2, dtype=jnp.float32)
+    turned = slab_inverse.transpose(0, 2, 1).reshape(STRIPES, 2, SLAB, SLAB)
+    blocks = same[None, :, None, :, None] * turned[:, :, :, None, :]
+    blocks = blocks.reshape(STRIPES, LANES, LANES)
+    return jnp.concatenate(split_device(jnp.concatenate([blocks, rims], 1)), 2)
+
+
+def call(kernel, inputs, outputs, scratch, scalars=0, cost=0):
+    specs = [pl.BlockSpec(memory_space=pltpu.SMEM)] * scalars
+    specs += [pl.BlockSpec(memory_space=pltpu.VMEM)] * (len(inputs) - scalars)
+    single = isinstance(outputs, tuple)
+    shapes = [outputs] if single else list(outputs)
+    out = pl.pallas_call(
+        kernel,
+        out_shape=[jax.ShapeDtypeStruct(shape, jnp.float32) for shape in shapes],
+        in_specs=specs,
+        out_specs=[pl.BlockSpec(memory_space=pltpu.VMEM)] * len(shapes),
+        scratch_shapes=scratch,
+        compiler_params=pltpu.CompilerParams(vmem_limit_bytes=VMEM_LIMIT),
+        cost_estimate=pl.CostEstimate(flops=cost, bytes_accessed=8 << 20, transcendentals=0),
+    )(*inputs)
+    return out[0] if single else out
+
+
+def vmem(*shape, dtype=jnp.float32):
+    return pltpu.VMEM(shape, dtype)
+
+
+def local_halves(amplitudes, mode_table, slab_map, base_flow, base_coupling, slab_inverse, wall_operator):
+    modes = amplitudes.shape[0]
+    points = amplitudes.shape[3]
+    groups = lax.axis_size("modes")
+    index = lax.axis_index("modes")
+    exchange = functools.partial(lax.all_to_all, axis_name="modes", split_axis=0, concat_axis=0, tiled=True)
+    neighbours = [(j, j ^ 1) for j in range(groups)]
+
+    rows = amplitudes.transpose(0, 2, 1, 3).reshape(modes, 5, 2, STRIPES, LANES)
+    rows = rows.transpose(0, 1, 3, 2, 4).reshape(modes * PARTS * STRIPES, LANES)
+    positions = mode_table[:, 0] * NB + mode_table[:, 1]
+    forward, backward = (jnp.asarray(matrix) for matrix in beta_matrices())
+    table = jnp.asarray(omega_table())
+    derivative = derivative_matrix(wall_operator, index % 2)
+    solve = solve_matrices(slab_map, slab_inverse)
+    beta_index = lax.dynamic_slice_in_dim(mode_table[:, 1], index * modes, modes)
+    omega_index = lax.dynamic_slice_in_dim(mode_table[:, 0], index * modes, modes)
+    signed = jnp.where(beta_index >= NB // 2, beta_index - NB, beta_index)
+    wave = phase_gain * (2.0 * signed.astype(jnp.float32) / NB)
+    frequency = omega_step * omega_index.astype(jnp.float32)
+    wave = jnp.broadcast_to(wave[:, None], (modes, LANES))
+    frequency = jnp.broadcast_to(frequency[:, None], (modes, LANES))
+
+    sent_first = call(pack_velocity, [rows], (groups, modes, LANES), [])
+    first = exchange(sent_first)
+    sent_second = call(pack_others, [rows], (groups, modes // 2 * 3, LANES), [])
+    second = exchange(sent_second)
+
+    grid = vmem(M, LANES)
+    spectrum = vmem(NW, 2 * NB, LANES)
+    folded = vmem(TIMES, NB, LANES)
+    unpacked = vmem(groups, modes, LANES)
+    physical = (TIMES, NB, LANES)
+    f1, g1, mean = call(
+        functools.partial(synthesis, True),
+        [positions, first, forward, table],
+        [(1,) + physical, (1,) + physical, (8, LANES)],
+        [grid, spectrum],
+        scalars=1,
+        cost=2 * 10**9,
+    )
+    s1 = lax.ppermute(f1, "modes", neighbours)
+    back_first = call(
+        functools.partial(force_analysis, True),
+        [positions, f1, f1, s1, g1, derivative, backward, table, mean],
+        (groups, modes + 8, LANES),
+        [folded, grid],
+        scalars=1,
+        cost=2 * 10**9,
+    )
+    got_first = exchange(back_first)
+    f2, g2 = call(
+        functools.partial(synthesis, False),
+        [positions, second, forward, table],
+        [(2,) + physical, (2,) + physical],
+        [grid, spectrum, unpacked],
+        scalars=1,
+        cost=4 * 10**9,
+    )
+    s2 = lax.ppermute(f2, "modes", neighbours)
+    back_second = call(
+        functools.partial(force_analysis, False),
+        [positions, f1, f2, s2, g2, derivative, backward, table],
+        (groups, modes // 2 * 3, LANES),
+        [folded, grid, unpacked],
+        scalars=1,
+        cost=4 * 10**9,
+    )
+    got_second = exchange(back_second)
+
+    stacked = TILE * PARTS
+    out = call(
+        relax_kernel,
+        [
+            rows,
+            got_first,
+            got_second,
+            base_flow.reshape(STRIPES, LANES),
+            base_coupling.reshape(25 * STRIPES, LANES),
+            wave,
+            frequency,
+            solve,
+        ],
+        (modes * PARTS * STRIPES, LANES),
+        [
+            vmem(STRIPES * PARTS, modes, LANES),
+            vmem(STRIPES * PARTS, TILE, LANES),
+            vmem(8, LANES),
+            vmem(stacked, LANES, dtype=jnp.bfloat16),
+            vmem(stacked, LANES, dtype=jnp.bfloat16),
+            vmem(stacked, LANES, dtype=jnp.bfloat16),
+            vmem(stacked, LANES, dtype=jnp.bfloat16),
+        ],
+        cost=4 * 10**9,
+    )
+    out = out.reshape(modes, 5, STRIPES, 2, LANES).transpose(0, 1, 3, 2, 4).reshape(modes, 5, 2, points)
+    return out.transpose(0, 2, 1, 3)
+
+
+def local_any(amplitudes, mode_table, slab_map, base_flow, base_coupling, slab_inverse, wall_operator):
+    points = amplitudes.shape[3]
+    fits = points == STRIPES * LANES and points // lax.axis_size("modes") == SHARE
+    fits = fits and slab_inverse.shape == (2 * STRIPES, SLAB, SLAB) and amplitudes.shape[0] % (2 * TILE) == 0
+    chosen = local_halves if fits else local
+    return chosen(amplitudes, mode_table, slab_map, base_flow, base_coupling, slab_inverse, wall_operator)
+
+
 def solution(mesh):
     return jax.shard_map(
-        local,
+        local_any,
         mesh=mesh,
         in_specs=(
             P(("runs", "modes"), None, None, None),

time: 1140 us -> 329 us (0.29); the launches traced: 1130 us -> 329 us
  local copies, waits for them, and re-layouts: 472 us -> 21.6 us
  blocking collectives: 157 us -> 0 us
  Pallas kernels: 0 us -> 152 us
  waiting for transfers between devices: 256 us -> 126 us
  matrix products: 127 us -> 0 us
  other arithmetic: 98.3 us -> 6.26 us
  starting transfers between devices: 11.6 us -> 23.1 us
    gather x8 -> x0, local copies, waits for them, and re-layouts: 222 us -> none  [the longest x2 119 us: local(): gridded = by_mode[..., mode_at].reshape(2, field_count, point_share, NW, NB)]
    all_gather x1 -> x0, blocking collectives: 157 us -> none  [local(): lax.all_gather(spanwise_vel[0, :, 0, 0], 'modes', axis=0, tiled=True)]
    pallas_call x0 -> x7, Pallas kernels: none -> 152 us  [call(): pl.pallas_call(kernel, out_shape=[jax.ShapeDtypeStruct(shape, jnp.float32...]
    reshape x12 -> x1, local copies, waits for them, and re-layouts: 139 us -> 1.47 us  [local_halves(): base_coupling.reshape(25 * STRIPES, LANES)]
    all_to_all x2 -> x4, waiting for transfers between devices: 256 us -> 121 us  [the longest x1 51.8 us: local_halves(): got_second = exchange(back_second)]
    dot_general x37 -> x0, matrix products: 127 us -> none  [the longest x3 31.5 us: relaxation(): coupled = jnp.einsum('kjy,acjy->acky', matrix, iterate, precision=precise)]
    unnamed x56 -> x18, local copies, waits for them, and re-layouts: 62 us -> 4.4 us
    add x4 -> x0, other arithmetic: 31.9 us -> none  [the longest x3 31.9 us: relaxation(): residual_in = right_side - applied + coupling * rims]
  transfers between devices with their start and end apart: 2 -> 6, of which waited for: 1 -> 4; matrix products, arithmetic and copies ran while one was open for 6% -> 7% of each run, Pallas kernels for 0% -> 35%
where the time goes in v1:
time: 329 us
  Pallas kernels  152 us (46%)
  waiting for transfers between devices  126 us (38%)
  starting transfers between devices  23.1 us (7%)
  local copies, waits for them, and re-layouts  21.6 us (7%)
  other arithmetic  6.26 us (2%)
    pallas_call x7, Pallas kernels, call(): pl.pallas_call(kernel, out_shape=[jax.ShapeDtypeStruct(shape, jnp.float32...  152 us
    all_to_all x1, waiting for transfers between devices, local_halves(): got_second = exchange(back_second)  51.8 us
    all_to_all x1, waiting for transfers between devices, local_halves(): first = exchange(sent_first)  39.9 us
    all_to_all x1, waiting for transfers between devices, local_halves(): second = exchange(sent_second)  29.7 us
  transfers between devices with their start and end apart: 6, of which 4 were waited for; matrix products, arithmetic and copies ran while one was open for 7% of the time, Pallas kernels for 35%

profile of v1, /device:TPU:13, one launch (start us, length us, event | category | flops | bytes accessed | tf_op | source)
XLA Modules:
  0.0 328.7 jit_solution(14556784481488265813)
XLA Ops:
  0.0 6.1 %shard_map.100 = f32[16,256,128]{2,1,0:T(8,128)} custom-call(f32[10240,128]{1,0:T(8,128)} %bitcast.31), custom_call_target="tpu_custom_call" | custom-call | bytes 8388608 | tf_op jit(solution)/shard_map/pallas_call | solution.py:643
  6.1 6.6 %all-to-all-start = ((f32[16,256,128]{2,1,0:T(8,128)}), f32[16,256,128]{2,1,0:T(8,128)S(1)}, u32[]{:S(2)}, u32[]{:S(2)}) async-start(f32[16,256,128]{2,1,0:T(8,128)} %shard_map.100), calls=%async_computation | async-start | bytes 4194304 | tf_op jit(solution)/shard_map/all_to_all | solution.py:683
  12.6 7.5 %shard_map.103 = f32[16,384,128]{2,1,0:T(8,128)} custom-call(f32[10240,128]{1,0:T(8,128)} %bitcast.32), custom_call_target="tpu_custom_call" | custom-call | bytes 8388608 | tf_op jit(solution)/shard_map/pallas_call | solution.py:643
  20.1 39.9 %all-to-all-done.r_ref = f32[16,256,128]{2,1,0:T(8,128)S(1)} async-done(((f32[16,256,128]{2,1,0:T(8,128)}), f32[16,256,128]{2,1,0:T(8,128)S(1)}, u32[]{:S(2)}, u32[]{:S(2)}) %all-to-all-start) | async-done | bytes 2097184 | tf_op jit(solution)/shard_map/all_to_all | solution.py:683
  60.0 1.3 copy-done.4
  61.4 4.9 %all-to-all-start.2 = ((f32[16,384,128]{2,1,0:T(8,128)}), f32[16,384,128]{2,1,0:T(8,128)S(1)}, u32[]{:S(2)}, u32[]{:S(2)}) async-start(f32[16,384,128]{2,1,0:T(8,128)} %shard_map.103), calls=%async_computation.2 | async-start | bytes 6291456 | tf_op jit(solution)/shard_map/all_to_all | solution.py:685
  66.9 18.4 %shard_map.101 = (f32[1,17,128,128]{3,2,1,0:T(8,128)}, f32[1,17,128,128]{3,2,1,0:T(8,128)}, f32[8,128]{1,0:T(8,128)}) custom-call(s32[4096]{0:T(1024)} %bitcast.37, f32[16,256,128]{2,1,0:T(8,128)} %copy-done.4, bf16[512,256]{1,0:T(8,128)(2,1)} %constant.125.clone.w_ref, f32[32,8,128]{2,1,0:T(8,128)} %constant.127.clone.tab_ref), custom_call_target="tpu_custom_call" | custom-call | flops 2000000000 | bytes 8388608 | tf_op jit(solution)/shard_map/pallas_call | solution.py:643
  85.8 0.9 broadcast_multiply_fusion
  86.8 1.3 mul.162
  88.8 17.7 %shard_map.102 = f32[16,264,128]{2,1,0:T(8,128)} custom-call(s32[4096]{0:T(1024)} %bitcast.38, f32[1,17,128,128]{3,2,1,0:T(8,128)} %get-tuple-element.10.vw_ref.f_ref, f32[1,17,128,128]{3,2,1,0:T(8,128)} %get-tuple-element.10.vw_ref.f_ref, f32[1,17,128,128]{3,2,1,0:T(8,128)} %collective-permute-done.s_ref, f32[1,17,128,128]{3,2,1,0:T(8,128)} %get-tuple-element.11.g_ref, ...), custom_call_target="tpu_custom_call" | custom-call | flops 2000000000 | bytes 8388608 | tf_op jit(solution)/shard_map/pallas_call | solution.py:643
  106.5 29.7 %all-to-all-done.2.r_ref = f32[16,384,128]{2,1,0:T(8,128)S(1)} async-done(((f32[16,384,128]{2,1,0:T(8,128)}), f32[16,384,128]{2,1,0:T(8,128)S(1)}, u32[]{:S(2)}, u32[]{:S(2)}) %all-to-all-start.2) | async-done | bytes 3145760 | tf_op jit(solution)/shard_map/all_to_all | solution.py:685
  136.2 1.7 copy-done.2
  137.8 4.9 %all-to-all-start.1 = ((f32[16,264,128]{2,1,0:T(8,128)}), f32[16,264,128]{2,1,0:T(8,128)S(1)}, u32[]{:S(2)}, u32[]{:S(2)}) async-start(f32[16,264,128]{2,1,0:T(8,128)} %shard_map.102), calls=%async_computation.1 | async-start | bytes 4325376 | tf_op jit(solution)/shard_map/all_to_all | solution.py:709
  142.7 36.2 %shard_map.104 = (f32[2,17,128,128]{3,2,1,0:T(8,128)}, f32[2,17,128,128]{3,2,1,0:T(8,128)}) custom-call(s32[4096]{0:T(1024)} %bitcast.39, f32[16,384,128]{2,1,0:T(8,128)} %copy-done.2, bf16[512,256]{1,0:T(8,128)(2,1)} %constant.125.clone.w_ref, f32[32,8,128]{2,1,0:T(8,128)} %constant.127.clone.tab_ref), custom_call_target="tpu_custom_call" | custom-call | flops 4000000000 | bytes 8388608 | tf_op jit(solution)/shard_map/pallas_call | solution.py:643
  179.3 4.3 %collective-permute-done.1.s_ref = f32[2,17,128,128]{3,2,1,0:T(8,128)} collective-permute-done((f32[2,17,128,128]{3,2,1,0:T(8,128)}, f32[2,17,128,128]{3,2,1,0:T(8,128)}, u32[]{:S(2)}, u32[]{:S(2)}) %collective-permute-start.1) | collective-permute-done | bytes 2228256 | tf_op jit(solution)/shard_map/ppermute | solution.py:718
  183.6 34.2 %shard_map.105 = f32[16,384,128]{2,1,0:T(8,128)} custom-call(s32[4096]{0:T(1024)} %bitcast.40, f32[1,17,128,128]{3,2,1,0:T(8,128)} %get-tuple-element.10.vw_ref.f_ref, f32[2,17,128,128]{3,2,1,0:T(8,128)} %get-tuple-element.13.f_ref, f32[2,17,128,128]{3,2,1,0:T(8,128)} %collective-permute-done.1.s_ref, f32[2,17,128,128]{3,2,1,0:T(8,128)} %get-tuple-element.14.g_ref, ...), custom_call_target="tpu_custom_call" | custom-call | flops 4000000000 | bytes 8388608 | tf_op jit(solution)/shard_map/pallas_call | solution.py:643
  217.9 1.4 copy-done.1
  219.3 6.0 %all-to-all-start.3 = ((f32[16,384,128]{2,1,0:T(8,128)}), f32[16,384,128]{2,1,0:T(8,128)S(1)}, u32[]{:S(2)}, u32[]{:S(2)}) async-start(f32[16,384,128]{2,1,0:T(8,128)} %shard_map.105), calls=%async_computation.3 | async-start | bytes 6291456 | tf_op jit(solution)/shard_map/all_to_all | solution.py:727
  226.5 1.8 copy.22
  229.2 1.8 copy.23
  232.6 0.8 copy.21
  233.4 2.0 mul.172
  235.4 2.0 mul.173
  237.6 0.8 mul.169
  238.3 1.5 reshape.247.coup_ref
  240.5 1.0 broadcast_multiply_fusion.1
  241.5 1.0 add_multiply_fusion
  242.6 0.9 pad_maximum_fusion.1.sw_ref
  243.4 51.8 %all-to-all-done.3.b2_ref = f32[16,384,128]{2,1,0:T(8,128)S(1)} async-done(((f32[16,384,128]{2,1,0:T(8,128)}), f32[16,384,128]{2,1,0:T(8,128)S(1)}, u32[]{:S(2)}, u32[]{:S(2)}) %all-to-all-start.3) | async-done | bytes 3145760 | tf_op jit(solution)/shard_map/all_to_all | solution.py:727
  295.2 0.9 broadcast_in_dim.27.kz_ref
  296.1 0.8 broadcast_in_dim.29.om_ref
  296.9 31.8 %shard_map.106 = f32[10240,128]{1,0:T(8,128)} custom-call(f32[10240,128]{1,0:T(8,128)} %bitcast.33, f32[16,264,128]{2,1,0:T(8,128)} %copy-done.1, f32[16,384,128]{2,1,0:T(8,128)} %copy-done, f32[4,128]{1,0:T(4,128)} %bitcast.43, f32[100,128]{1,0:T(8,128)} %reshape.247.coup_ref, f32[256,128]{1,0:T(8,128)} %broadcast_in_dim.27.kz_ref, ...), custom_call_target="tpu_custom_call" | custom-call | flops 4000000000 | bytes 8388608 | tf_op jit(solution)/shard_map/pallas_call | solution.py:643
  (46 shorter events, 6.8 us)
Async XLA Ops:
  6.1 54.0 %all-to-all-start = ((f32[16,256,128]{2,1,0:T(8,128)}), f32[16,256,128]{2,1,0:T(8,128)S(1)}, u32[]{:S(2)}, u32[]{:S(2)}) async-start(f32[16,256,128]{2,1,0:T(8,128)} %shard_map.100), calls=%async_computation | async-start | bytes 4194304 | tf_op jit(solution)/shard_map/all_to_all | solution.py:683
  20.1 46.2 %copy-start.6 = (s32[4096,2]{0,1:T(2,128)S(1)}, s32[4096,2]{0,1:T(2,128)}, u32[]{:S(2)}) copy-start(s32[4096,2]{0,1:T(2,128)} %param.11) | copy-start | bytes 98308
  60.0 1.3 copy-start.4
  61.4 74.8 %all-to-all-start.2 = ((f32[16,384,128]{2,1,0:T(8,128)}), f32[16,384,128]{2,1,0:T(8,128)S(1)}, u32[]{:S(2)}, u32[]{:S(2)}) async-start(f32[16,384,128]{2,1,0:T(8,128)} %shard_map.103), calls=%async_computation.2 | async-start | bytes 6291456 | tf_op jit(solution)/shard_map/all_to_all | solution.py:685
  66.9 18.7 %copy-start.7 = (f32[64,64]{1,0:T(8,128)S(1)}, f32[64,64]{1,0:T(8,128)}, u32[]{:S(2)}) copy-start(f32[64,64]{1,0:T(8,128)} %param.16) | copy-start | bytes 49156
  85.3 3.5 %collective-permute-start = (f32[1,17,128,128]{3,2,1,0:T(8,128)}, f32[1,17,128,128]{3,2,1,0:T(8,128)}, u32[]{:S(2)}, u32[]{:S(2)}) collective-permute-start(f32[1,17,128,128]{3,2,1,0:T(8,128)} %get-tuple-element.10.vw_ref.f_ref), channel_id=1, source_target_pairs={{0,1},{1,0},{2,3},{3,2},{4,5},{5,4},{6,7},{7,6},{8,9},{9,8},{10,11... | collective-permute-start | bytes 3342344 | tf_op jit(solution)/shard_map/ppermute | solution.py:700
  136.2 1.7 copy-start.2
  137.8 80.0 %all-to-all-start.1 = ((f32[16,264,128]{2,1,0:T(8,128)}), f32[16,264,128]{2,1,0:T(8,128)S(1)}, u32[]{:S(2)}, u32[]{:S(2)}) async-start(f32[16,264,128]{2,1,0:T(8,128)} %shard_map.102), calls=%async_computation.1 | async-start | bytes 4325376 | tf_op jit(solution)/shard_map/all_to_all | solution.py:709
  178.9 4.7 %collective-permute-start.1 = (f32[2,17,128,128]{3,2,1,0:T(8,128)}, f32[2,17,128,128]{3,2,1,0:T(8,128)}, u32[]{:S(2)}, u32[]{:S(2)}) collective-permute-start(f32[2,17,128,128]{3,2,1,0:T(8,128)} %get-tuple-element.13.f_ref), channel_id=1, source_target_pairs={{0,1},{1,0},{2,3},{3,2},{4,5},{5,4},{6,7},{7,6},{8,9},{9,8},{10,11... | collective-permute-start | bytes 6684680 | tf_op jit(solution)/shard_map/ppermute | solution.py:718
  217.9 7.4 %copy-start.8 = (s32[8]{0:T(128)S(1)}, s32[8]{0:T(128)}, u32[]{:S(2)}) copy-start(s32[8]{0:T(128)} %param.12) | copy-start | bytes 100
  217.9 13.1 %copy-start.3 = (f32[8,64,64]{2,1,0:T(8,128)S(1)}, f32[8,64,64]{2,1,0:T(8,128)}, u32[]{:S(2)}) copy-start(f32[8,64,64]{2,1,0:T(8,128)} %param.15) | copy-start | bytes 393220
  217.9 1.4 copy-start.1
  219.3 75.9 %all-to-all-start.3 = ((f32[16,384,128]{2,1,0:T(8,128)}), f32[16,384,128]{2,1,0:T(8,128)S(1)}, u32[]{:S(2)}, u32[]{:S(2)}) async-start(f32[16,384,128]{2,1,0:T(8,128)} %shard_map.105), calls=%async_computation.3 | async-start | bytes 6291456 | tf_op jit(solution)/shard_map/all_to_all | solution.py:727
  233.4 8.0 %copy-start.5 = (f32[4,128,128]{2,1,0:T(8,128)S(1)}, f32[4,128,128]{2,1,0:T(8,128)}, u32[]{:S(2)}) copy-start(f32[4,128,128]{2,1,0:T(8,128)} %copy.22) | copy-start | bytes 786436
  295.2 1.7 copy-start

commit v2 on v0

--- a/solution.py
+++ b/solution.py
@@ -1,8 +1,12 @@
+import functools
 import math
 
 import jax
 import jax.numpy as jnp
+import numpy as np
 from jax import lax
+from jax.experimental import pallas as pl
+from jax.experimental.pallas import tpu as pltpu
 from jax.sharding import PartitionSpec as P
 
 M = 4096
@@ -174,9 +178,756 @@
     return iterate
 
 
+LANES = 128
+SHARE = 32
+SLAB = 64
+HALF = NW // 2
+TIMES = HALF + 1
+BLOCKS = LANES // SHARE
+STRIPES = 4
+PARTS = 10
+TILE = 32
+MIB = 1024 * 1024
+
+
+def roll(x, shift):
+    return pltpu.roll(x, shift % LANES, x.ndim - 1)
+
+
+def lane_index(shape):
+    return lax.broadcasted_iota(jnp.int32, shape, len(shape) - 1)
+
+
+def lane_masks(shape):
+    lane = lane_index(shape)
+    return (lane < 64, (lane & 32) == 0)
+
+
+def real_sign(shape):
+    return jnp.where(lane_index(shape) < 64, 1.0, -1.0).astype(jnp.float32)
+
+
+def block_transpose(rows, low, even):
+    r0, r1, r2, r3 = rows
+    t0 = jnp.where(low, r0, roll(r2, 64))
+    t2 = jnp.where(low, roll(r0, 64), r2)
+    t1 = jnp.where(low, r1, roll(r3, 64))
+    t3 = jnp.where(low, roll(r1, 64), r3)
+    return (
+        jnp.where(even, t0, roll(t1, 32)),
+        jnp.where(even, roll(t0, 96), t1),
+        jnp.where(even, t2, roll(t3, 32)),
+        jnp.where(even, roll(t2, 96), t3),
+    )
+
+
+def split(x):
+    high = x.astype(jnp.bfloat16)
+    return high, (x - high.astype(jnp.float32)).astype(jnp.bfloat16)
+
+
+def dot(a, b):
+    return jnp.dot(a, b, preferred_element_type=jnp.float32)
+
+
+def cosine_sine(inputs, length, table, sign, real):
+    if length == 4:
+        first, middle, last = inputs
+        middle_re = middle * real
+        total = first + last
+        return [total + middle_re, (first - last) + (middle - middle_re), total - middle_re]
+    step = NW // length
+    quarter = length // 4
+    even = cosine_sine(inputs[0::2], length // 2, table, sign, real)
+    odd_inputs = [(a, inputs[a]) for a in range(1, length // 2, 2)]
+    odd = []
+    for t in range(quarter + 1):
+        if t == 0:
+            total = odd_inputs[0][1]
+            for _, value in odd_inputs[1:]:
+                total = total + value
+            odd.append(total * real)
+        elif t == quarter:
+            total = odd_inputs[0][1]
+            for a, value in odd_inputs[1:]:
+                total = total + value if a % 4 == 1 else total - value
+            odd.append(total - total * real)
+        else:
+            total = None
+            for a, value in odd_inputs:
+                term = table(a * t * step % NW) * value
+                total = term if total is None else total + term
+            odd.append(total)
+    out = [None] * (length // 2 + 1)
+    for t in range(quarter + 1):
+        out[t] = even[t] + odd[t]
+        out[length // 2 - t] = sign * (even[t] - odd[t])
+    out[quarter] = even[quarter] + odd[quarter]
+    return out
+
+
+def spread(ref, offset):
+    flat = ref.reshape(ref.shape[0] * ref.shape[1], LANES)
+    return flat[pl.ds(offset, ref.shape[0], stride=ref.shape[1]), :]
+
+
+def pack_pair(first, first_offset, second, second_offset, low, even):
+    out = []
+    for stripe in range(STRIPES):
+        rows = []
+        for part in range(2):
+            rows.append(spread(first, first_offset + stripe * 2 + part))
+            rows.append(spread(second, second_offset + stripe * 2 + part))
+        out.extend(block_transpose(rows, low, even))
+    return out
+
+
+def pack_first(near_ref, far_ref, near_last_ref, far_last_ref, o_ref):
+    low, even = lane_masks((TILE, LANES))
+    pieces = (
+        (near_ref, 0, near_ref, 2 * STRIPES),
+        (far_ref, 0, far_ref, 2 * STRIPES),
+        (near_last_ref, 0, far_last_ref, 0),
+    )
+    for place, piece in enumerate(pieces):
+        for group, value in enumerate(pack_pair(*piece, low, even)):
+            o_ref[group, place] = value
+
+
+def pack_second(near_ref, o_ref):
+    low, even = lane_masks((TILE, LANES))
+    for group, value in enumerate(pack_pair(near_ref, 0, near_ref, 2 * STRIPES, low, even)):
+        o_ref[group] = value
+
+
+ROWS = 128
+
+
+def loop(count, unroll, body):
+    def step(i, carry):
+        for j in range(unroll):
+            body(i * unroll + j)
+        return carry
+
+    lax.fori_loop(0, count // unroll, step, 0)
+    for i in range(count // unroll * unroll, count):
+        body(i)
+
+
+def lanes_constants():
+    sign = real_sign((8, LANES))
+    real = jnp.where(lane_index((8, LANES)) < 64, 1.0, 0.0).astype(jnp.float32)
+    even = (lane_index((8, LANES)) & 32) == 0
+    return sign, real, even
+
+
+def pair_left(even, near, far):
+    return jnp.where(even, near, roll(far, 32))
+
+
+def pair_right(even, near, far):
+    return jnp.where(even, roll(near, 96), far)
+
+
+def synthesis(with_last, pos_ref, r_ref, w_ref, tab_ref, *refs):
+    if with_last:
+        f_ref, g_ref, f_last_ref, g_last_ref, mean_ref, grid_ref, spec_ref, turned_ref = refs
+    else:
+        f_ref, g_ref, grid_ref, spec_ref = refs
+    groups = r_ref.shape[0]
+    modes = M // groups
+    sign, real, even = lanes_constants()
+    wide_sign = real_sign((NB, LANES))
+    wide_even = (lane_index((NB, LANES)) & 32) == 0
+
+    def table(j):
+        return tab_ref[j]
+
+    def scatter(group, mode, source, row):
+        for j in range(ROWS):
+            cell = pos_ref[group * modes + mode + j]
+            grid_ref[pl.ds(cell, 1), :] = source[group, pl.ds(row + j, 1), :]
+
+    def beta(first, second):
+        columns = [jnp.concatenate([x, -wide_sign * roll(x, 64)], 0) for x in (first, second)]
+        high, low_part = split(jnp.concatenate(columns, 1))
+        product = dot(w_ref[...], high)
+        out = product[: 2 * NB] + product[2 * NB :] + dot(w_ref[pl.ds(0, 2 * NB), :], low_part)
+        return out[:, :LANES], out[:, LANES:]
+
+    def grid(a):
+        return grid_ref[pl.ds(pl.multiple_of(a * NB, NB), NB), :]
+
+    def both_halves(i):
+        group = i // (modes // ROWS)
+        start = pl.multiple_of(i % (modes // ROWS) * ROWS, ROWS)
+        scatter(group, start, r_ref, start)
+
+    loop(groups * (modes // ROWS), 1, both_halves)
+    if with_last:
+        mean_ref[...] = grid_ref[pl.ds(0, 8), :]
+
+    def full_beta(i):
+        spec_ref[2 * i], spec_ref[2 * i + 1] = beta(grid(2 * i), grid(2 * i + 1))
+
+    loop(NW // 2, 2, full_beta)
+
+    def full_omega(out_ref, shift):
+        def body(i):
+            rows = pl.ds(pl.multiple_of(i * 8, 8), 8)
+            source = pl.ds(pl.multiple_of(shift + i * 8, 8), 8)
+            inputs = [spec_ref[0, source, :] * real]
+            for a in range(1, HALF):
+                inputs.append(spec_ref[a, source, :] + sign * spec_ref[NW - a, source, :])
+            inputs.append(spec_ref[HALF, source, :] * real)
+            for t, value in enumerate(cosine_sine(inputs, NW, table, sign, real)):
+                out_ref[t, rows, :] = value - sign * roll(value, 64)
+
+        loop(NB // 8, 2, body)
+
+    full_omega(f_ref, 0)
+    full_omega(g_ref, NB)
+    if not with_last:
+        return
+
+    def turn(group):
+        turned_ref[group] = roll(r_ref[group, pl.ds(modes, modes // 2), :], 96)
+        for block in range(modes // 2 // ROWS):
+            scatter(group, block * ROWS, r_ref, modes + block * ROWS)
+            scatter(group, modes // 2 + block * ROWS, turned_ref, block * ROWS)
+
+    loop(groups, 1, turn)
+
+    def half_beta(i):
+        columns = [pair_left(wide_even, grid(a), grid(a + HALF)) for a in (2 * i, 2 * i + 1)]
+        spec_ref[2 * i], spec_ref[2 * i + 1] = beta(*columns)
+
+    loop(HALF // 2, 2, half_beta)
+
+    def half_omega(out_ref, shift):
+        def body(i):
+            rows = pl.ds(pl.multiple_of(i * 8, 8), 8)
+            near = pl.ds(pl.multiple_of(shift + i * 8, 8), 8)
+            far = pl.ds(pl.multiple_of(shift + NB // 2 + i * 8, 8), 8)
+            firsts = []
+            seconds = []
+            for a in range(HALF):
+                pieces = (even, spec_ref[a, near, :], spec_ref[a, far, :])
+                firsts.append(pair_left(*pieces))
+                seconds.append(pair_right(*pieces))
+            inputs = [firsts[0] * real]
+            for a in range(1, HALF):
+                inputs.append(firsts[a] + sign * seconds[HALF - a])
+            inputs.append(seconds[0] * real)
+            for t, value in enumerate(cosine_sine(inputs, NW, table, sign, real)):
+                out_ref[t, rows, :] = value - sign * roll(value, 64)
+
+        loop(NB // 16, 2, body)
+
+    half_omega(f_last_ref, 0)
+    half_omega(g_last_ref, NB)
+
+
+def force_analysis(with_last, pos_ref, vw_ref, f_ref, s_ref, g_ref, d_ref, w_ref, tab_ref, *refs):
+    if with_last:
+        f_last_ref, s_last_ref, g_last_ref, mean_ref, o_ref, k_ref, r_ref, n_ref, turned_ref = refs
+    else:
+        o_ref, k_ref, r_ref, n_ref = refs
+    groups = o_ref.shape[0]
+    modes = M // groups
+    sign, real, _ = lanes_constants()
+    wide_sign = real_sign((NB, LANES))
+    wide_real, wide_even = lane_masks((NB, LANES))
+    half_rows = NB // 2
+
+    def table(j):
+        return tab_ref[j]
+
+    def gather(group, mode, target, row):
+        for j in range(ROWS):
+            cell = pos_ref[group * modes + mode + j]
+            target[group, pl.ds(row + j, 1), :] = n_ref[pl.ds(cell, 1), :]
+
+    def force_of(t, rows, v, w, f, s, g):
+        high, low_part = split(jnp.concatenate([f, s], 1))
+        both = dot(high, d_ref[...])
+        grad = both[:, :LANES] + both[:, LANES:] + dot(low_part, d_ref[:, :LANES])
+        force = v * grad + w * g
+        if t is None:
+            return jnp.where(wide_real[:rows], force, 0.0)
+        return force + wide_sign[:rows] * roll(force, 64)
+
+    def full_product(t, alone=False):
+        vw = vw_ref[t]
+        v = pair_left(wide_even, vw, vw)
+        w = pair_right(wide_even, vw, vw)
+        k_ref[t] = force_of(None if alone else t, NB, v, w, f_ref[t], s_ref[t], g_ref[t])
+
+    def products(product):
+        product(0, True)
+        product(HALF, True)
+        loop(HALF - 1, 3, lambda i: product(i + 1))
+
+    def omegas(tiles):
+        def body(i):
+            rows = pl.ds(pl.multiple_of(i * 8, 8), 8)
+            inputs = [k_ref[t, rows, :] for t in range(TIMES)]
+            for a, value in enumerate(cosine_sine(inputs, NW, table, sign, real)):
+                r_ref[a, rows, :] = value
+
+        loop(tiles, 2, body)
+
+    def beta(columns):
+        high, low_part = split(jnp.concatenate(columns, 1) if len(columns) > 1 else columns[0])
+        both = dot(w_ref[...], high)
+        out = both[: 2 * NB] + both[2 * NB :] + dot(w_ref[pl.ds(0, 2 * NB), :], low_part)
+        result = []
+        for j in range(len(columns)):
+            cosine = out[:NB, j * LANES : (j + 1) * LANES]
+            sine = roll(out[NB:, j * LANES : (j + 1) * LANES], 64)
+            result.append((cosine + wide_sign * sine, wide_sign * cosine - sine))
+        return result
+
+    def store(a, plus, minus):
+        mirror = (NW - a) % NW
+        n_ref[pl.ds(pl.multiple_of(mirror * NB, NB), NB), :] = minus
+        n_ref[pl.ds(pl.multiple_of(a * NB, NB), NB), :] = plus
+
+    products(full_product)
+    omegas(NB // 8)
+
+    def full_beta(i):
+        for j, (plus, minus) in enumerate(beta([r_ref[2 * i], r_ref[2 * i + 1]])):
+            store(2 * i + j, plus, minus)
+
+    loop(HALF // 2, 2, full_beta)
+    store(HALF, *beta([r_ref[HALF]])[0])
+
+    def both_halves(i):
+        group = i // (modes // ROWS)
+        start = pl.multiple_of(i % (modes // ROWS) * ROWS, ROWS)
+        gather(group, start, o_ref, start)
+
+    loop(groups * (modes // ROWS), 1, both_halves)
+    if not with_last:
+        return
+
+    def half_product(t, alone=False):
+        vw = vw_ref[t]
+        near = vw[:half_rows]
+        far = vw[half_rows:]
+        v = pair_left(wide_even[:half_rows], near, far)
+        w = pair_right(wide_even[:half_rows], near, far)
+        k_ref[t, pl.ds(0, half_rows), :] = force_of(
+            None if alone else t, half_rows, v, w, f_last_ref[t], s_last_ref[t], g_last_ref[t]
+        )
+
+    products(half_product)
+    omegas(NB // 16)
+
+    def half_columns(a):
+        even = wide_even[:half_rows]
+        pieces = (even, r_ref[a, pl.ds(0, half_rows), :], r_ref[a + 1, pl.ds(0, half_rows), :])
+        return jnp.concatenate([pair_left(*pieces), pair_right(*pieces)], 0)
+
+    def half_beta(i):
+        for j, (plus, minus) in enumerate(beta([half_columns(4 * i), half_columns(4 * i + 2)])):
+            a = 4 * i + 2 * j
+            store(a, plus, minus)
+            store(a + 1, roll(plus, 96), roll(minus, 96))
+
+    loop(HALF // 4, 1, half_beta)
+    last = r_ref[HALF, pl.ds(0, half_rows), :]
+    store(HALF, *beta([jnp.concatenate([last, roll(last, 96)], 0)])[0])
+
+    def turn(group):
+        for block in range(modes // 2 // ROWS):
+            gather(group, block * ROWS, o_ref, modes + block * ROWS)
+            gather(group, modes // 2 + block * ROWS, turned_ref, block * ROWS)
+        here = pl.ds(modes, modes // 2)
+        near = o_ref[group, here, :]
+        o_ref[group, here, :] = pair_left((lane_index(near.shape) & 32) == 0, near, turned_ref[group])
+        o_ref[group, pl.ds(modes // 2 * 3, 8), :] = mean_ref[...]
+
+    loop(groups, 1, turn)
+
+
+def find_rims(x_of, zh_ref, zl_ref):
+    lane = lane_index((TILE, LANES))
+    edge = ((lane & 63) == 0) | ((lane & 63) == 63)
+    for part in range(PARTS):
+        rims = None
+        for stripe in range(STRIPES):
+            term = jnp.where(edge, x_of(stripe, part), 0.0)
+            term = roll(term, 2 * stripe) if stripe else term
+            rims = term if rims is None else rims + term
+        rows = pl.ds(part * TILE, TILE)
+        zh_ref[rows, :], zl_ref[rows, :] = split(rims)
+
+
+def three_pass(high, low_part, weights):
+    both = dot(high, weights)
+    return both[:, :LANES] + both[:, LANES:] + dot(low_part, weights[:, :LANES])
+
+
+def relax(stripe, x_of, cross, kz_ref, om_ref, coup_ref, sw_ref, rh_ref, rl_ref, zh_ref, zl_ref):
+    values = [x_of(stripe, part) for part in range(PARTS)]
+    rotation = kz_ref[...] * cross - om_ref[...]
+    for k in range(5):
+        out_re = rotation * values[2 * k + 1]
+        out_im = -(rotation * values[2 * k])
+        for j in range(5):
+            weight = coup_ref[pl.ds((k * 5 + j) * STRIPES + stripe, 1), :]
+            out_re = out_re - weight * values[2 * j]
+            out_im = out_im - weight * values[2 * j + 1]
+        for part, out in ((2 * k, out_re), (2 * k + 1, out_im)):
+            rows = pl.ds(part * TILE, TILE)
+            rh_ref[stripe, rows, :], rl_ref[stripe, rows, :] = split(out)
+    high = jnp.concatenate([rh_ref[stripe], zh_ref[...]], 1)
+    low_rows = jnp.concatenate([rl_ref[stripe], zl_ref[...]], 1)
+    return three_pass(high, low_rows, sw_ref[stripe])
+
+
+def relax_first(a_ref, b_ref, t_ref, mean_ref, base_ref, coup_ref, kz_ref, om_ref, sw_ref, start_ref, x_ref, cf_ref, rh_ref, rl_ref, zh_ref, zl_ref):
+    low, even = lane_masks((TILE, LANES))
+    block_of = lane_index((1, LANES)) // SHARE
+    far = pl.program_id(0) >= pl.num_programs(0) // 2
+    for stripe in range(STRIPES):
+        total = base_ref[pl.ds(stripe, 1), :]
+        for block in range(BLOCKS):
+            row = mean_ref[stripe * BLOCKS + block, pl.ds(0, 1), :]
+            total = total + jnp.where(block_of == block, roll(row, SHARE * (block - 1)), 0.0)
+        cf_ref[pl.ds(stripe, 1), :] = total
+
+    def x_of(stripe, part):
+        return spread(a_ref, part // 2 * 2 * STRIPES + stripe * 2 + part % 2)
+
+    for stripe in range(STRIPES):
+        groups = [stripe * BLOCKS + block for block in range(BLOCKS)]
+        velocity = block_transpose([b_ref[group] for group in groups], low, even)
+        last = block_transpose([t_ref[group] for group in groups], low, even)
+        gained = {
+            4: velocity[0],
+            6: velocity[1],
+            5: velocity[2],
+            7: velocity[3],
+            8: jnp.where(far, last[1], last[0]),
+            9: jnp.where(far, last[3], last[2]),
+        }
+        for part in range(PARTS):
+            right = x_of(stripe, part)
+            if part in gained:
+                right = right + march_step * gained[part]
+            rows = pl.ds(part * TILE, TILE)
+            rh_ref[stripe, rows, :], rl_ref[stripe, rows, :] = split(right)
+        solved = three_pass(rh_ref[stripe], rl_ref[stripe], sw_ref[stripe, pl.ds(0, LANES), :])
+        start_ref[pl.ds(stripe * PARTS, PARTS)] = solved.reshape(PARTS, TILE, LANES)
+    find_rims(x_of, zh_ref, zl_ref)
+    for stripe in range(STRIPES):
+        here = pl.ds(stripe * PARTS, PARTS)
+        cross = cf_ref[pl.ds(stripe, 1), :]
+        new = relax(stripe, x_of, cross, kz_ref, om_ref, coup_ref, sw_ref, rh_ref, rl_ref, zh_ref, zl_ref)
+        x_ref[here] = start_ref[here] + new.reshape(PARTS, TILE, LANES)
+
+
+def relax_last(start_ref, first_ref, b_ref, cf_ref, coup_ref, kz_ref, om_ref, sw_ref, o_ref, right_ref, x_ref, rh_ref, rl_ref, zh_ref, zl_ref):
+    low, even = lane_masks((TILE, LANES))
+    gained = 4
+    for stripe in range(STRIPES):
+        here = pl.ds(stripe * PARTS, PARTS)
+        rows = [b_ref[stripe * BLOCKS + block] for block in range(BLOCKS)]
+        first_re, second_re, first_im, second_im = block_transpose(rows, low, even)
+        for part, value in enumerate((first_re, first_im, second_re, second_im)):
+            place = pl.ds(part * TILE, TILE)
+            rh_ref[stripe, place, :], rl_ref[stripe, place, :] = split(march_step * value)
+        place = pl.ds(0, gained * TILE)
+        weights = sw_ref[stripe, pl.ds(0, LANES), :]
+        added = three_pass(rh_ref[stripe, place, :], rl_ref[stripe, place, :], weights).reshape(gained, TILE, LANES)
+        with_added = pl.ds(stripe * PARTS, gained)
+        others = pl.ds(stripe * PARTS + gained, PARTS - gained)
+        right_ref[with_added] = start_ref[with_added] + added
+        x_ref[with_added] = first_ref[with_added] + added
+        right_ref[others] = start_ref[others]
+        x_ref[others] = first_ref[others]
+
+    def x_of(stripe, part):
+        return x_ref[stripe * PARTS + part]
+
+    flat = o_ref.reshape(TILE * PARTS * STRIPES, LANES)
+    for sweep in range(1, SWEEPS):
+        find_rims(x_of, zh_ref, zl_ref)
+        for stripe in range(STRIPES):
+            here = pl.ds(stripe * PARTS, PARTS)
+            cross = cf_ref[pl.ds(stripe, 1), :]
+            new = relax(stripe, x_of, cross, kz_ref, om_ref, coup_ref, sw_ref, rh_ref, rl_ref, zh_ref, zl_ref)
+            new = right_ref[here] + new.reshape(PARTS, TILE, LANES)
+            if sweep < SWEEPS - 1:
+                x_ref[here] = new
+                continue
+            for part in range(PARTS):
+                offset = part // 2 * 2 * STRIPES + stripe * 2 + part % 2
+                flat[pl.ds(offset, TILE, stride=PARTS * STRIPES), :] = new[part]
+
+
+def split_host(x):
+    high = x.astype(jnp.bfloat16)
+    low_part = (x - high.astype(np.float64)).astype(jnp.bfloat16)
+    return high, low_part
+
+
+def beta_matrices():
+    index = np.arange(NB)
+    angles = (index[:, None] * index[None, :] % NB) * (2.0 * math.pi / NB)
+    cosine = np.cos(angles)
+    sine = np.sin(angles)
+    wave = 2.0 * np.where(index >= NB // 2, index - NB, index) / NB
+    factor = 1.0 / math.sqrt(M)
+    forward = factor * np.block([[cosine, sine], [-sine * wave, cosine * wave]])
+    backward = -factor * np.concatenate([cosine, sine], 0)
+    return tuple(np.concatenate(split_host(matrix), 0) for matrix in (forward, backward))
+
+
+def omega_table():
+    angles = np.arange(NW) * (2.0 * math.pi / NW)
+    rows = np.concatenate([np.repeat(np.cos(angles)[:, None], 64, 1), np.repeat(np.sin(angles)[:, None], 64, 1)], 1)
+    return np.repeat(rows[:, None, :], 8, 1).astype(np.float32)
+
+
+def split_device(x):
+    high = lax.reduce_precision(x, 8, 7)
+    return high.astype(jnp.bfloat16), (x - high).astype(jnp.bfloat16)
+
+
+def derivative_matrix(wall_operator, half):
+    own = lax.dynamic_slice(wall_operator, (half * SHARE, 0), (SHARE, SLAB)).T
+    mine = lax.dynamic_slice(own, (half * SHARE, 0), (SHARE, SHARE))
+    other = lax.dynamic_slice(own, ((1 - half) * SHARE, 0), (SHARE, SHARE))
+    same = jnp.eye(BLOCKS, dtype=jnp.float32)
+    stacked = jnp.stack([mine, other], 0)
+    full = same[None, :, None, :, None] * stacked[:, None, :, None, :]
+    full = full.reshape(2 * LANES, LANES)
+    return jnp.concatenate(split_device(full), 1)
+
+
+def solve_matrices(slab_map, slab_inverse):
+    count = slab_inverse.shape[0]
+    slots = jnp.arange(count, dtype=jnp.int32)
+    holds = slab_map[:, None] == slots[None, :]
+    below_of = jnp.concatenate([slab_map[:1] * 0 - 1, slab_map[:-1]])
+    above_of = jnp.concatenate([slab_map[1:], slab_map[:1] * 0 - 1])
+    below = jnp.sum(jnp.where(holds, below_of[:, None], 0), 0)
+    above = jnp.sum(jnp.where(holds, above_of[:, None], 0), 0)
+    lane = jnp.arange(LANES, dtype=jnp.int32)
+
+    def one_hot(slot, position):
+        where = (slot % 2 * SLAB + position + 2 * (slot // 2)) % LANES
+        return ((slot >= 0)[:, None] & (where[:, None] == lane[None, :])).astype(jnp.float32)
+
+    low_rim = one_hot(below, SLAB - 1)
+    high_rim = one_hot(above, 0)
+    rims = coupling * (
+        low_rim[:, :, None] * slab_inverse[:, None, :, 0] + high_rim[:, :, None] * slab_inverse[:, None, :, SLAB - 1]
+    )
+    rims = rims.reshape(STRIPES, 2, LANES, SLAB).transpose(0, 2, 1, 3).reshape(STRIPES, LANES, LANES)
+    same = jnp.eye(2, dtype=jnp.float32)
+    turned = slab_inverse.transpose(0, 2, 1).reshape(STRIPES, 2, SLAB, SLAB)
+    blocks = same[None, :, None, :, None] * turned[:, :, :, None, :]
+    blocks = blocks.reshape(STRIPES, LANES, LANES)
+    return jnp.concatenate(split_device(jnp.concatenate([blocks, rims], 1)), 2)
+
+
+def call(kernel, inputs, outputs, scratch, scalars=0, cost=0, limit=60, grid=None, in_specs=None, out_specs=None):
+    whole = pl.BlockSpec(memory_space=pltpu.VMEM)
+    if in_specs is None:
+        in_specs = [pl.BlockSpec(memory_space=pltpu.SMEM)] * scalars + [whole] * (len(inputs) - scalars)
+    if out_specs is None:
+        out_specs = [whole] * len(outputs)
+    extra = {} if grid is None else {"grid": grid}
+    return pl.pallas_call(
+        kernel,
+        out_shape=[jax.ShapeDtypeStruct(shape, jnp.float32) for shape in outputs],
+        in_specs=in_specs,
+        out_specs=out_specs,
+        scratch_shapes=scratch,
+        compiler_params=pltpu.CompilerParams(vmem_limit_bytes=limit * MIB),
+        cost_estimate=pl.CostEstimate(flops=cost, bytes_accessed=8 << 20, transcendentals=0),
+        **extra,
+    )(*inputs)
+
+
+def vmem(*shape, dtype=jnp.float32):
+    return pltpu.VMEM(shape, dtype)
+
+
+def fixed(*shape):
+    return pl.BlockSpec(shape, lambda i: (0,) * len(shape))
+
+
+def local_halves(amplitudes, mode_table, slab_map, base_flow, base_coupling, slab_inverse, wall_operator):
+    modes = amplitudes.shape[0]
+    points = amplitudes.shape[3]
+    groups = lax.axis_size("modes")
+    index = lax.axis_index("modes")
+    exchange = functools.partial(lax.all_to_all, axis_name="modes", split_axis=0, concat_axis=0, tiled=True)
+    neighbours = [(j, j ^ 1) for j in range(groups)]
+    stride = PARTS * STRIPES
+    tiles = modes // TILE
+    first_rows = modes // 2 * 3
+
+    rows = amplitudes.transpose(0, 2, 1, 3).reshape(modes, 5, 2, STRIPES, LANES)
+    rows = rows.transpose(0, 1, 3, 2, 4).reshape(modes, stride, LANES)
+    positions = mode_table[:, 0] * NB + mode_table[:, 1]
+    forward, backward = (jnp.asarray(matrix) for matrix in beta_matrices())
+    table = jnp.asarray(omega_table())
+    derivative = derivative_matrix(wall_operator, index % 2)
+    solve = solve_matrices(slab_map, slab_inverse)
+    beta_index = lax.dynamic_slice_in_dim(mode_table[:, 1], index * modes, modes)
+    omega_index = lax.dynamic_slice_in_dim(mode_table[:, 0], index * modes, modes)
+    signed = jnp.where(beta_index >= NB // 2, beta_index - NB, beta_index)
+    wave = phase_gain * (2.0 * signed.astype(jnp.float32) / NB)
+    frequency = omega_step * omega_index.astype(jnp.float32)
+    wave = jnp.broadcast_to(wave[:, None], (modes, LANES))
+    frequency = jnp.broadcast_to(frequency[:, None], (modes, LANES))
+    couple = base_coupling.reshape(25 * STRIPES, LANES)
+
+    def variables(count, place, shift):
+        return pl.BlockSpec((TILE, count * 2 * STRIPES, LANES), lambda i: (i + shift, place, 0))
+
+    half = tiles // 2
+    (sent_first,) = call(
+        pack_first,
+        [rows] * 4,
+        [(groups, 3, modes // 2, LANES)],
+        [],
+        cost=10**8,
+        grid=(half,),
+        in_specs=[variables(2, 1, 0), variables(2, 1, half), variables(1, 4, 0), variables(1, 4, half)],
+        out_specs=[pl.BlockSpec((groups, 3, TILE, LANES), lambda i: (0, 0, i, 0))],
+    )
+    first = exchange(sent_first.reshape(groups, first_rows, LANES))
+    (sent_second,) = call(
+        pack_second,
+        [rows],
+        [(groups, modes, LANES)],
+        [],
+        cost=10**8,
+        grid=(tiles,),
+        in_specs=[variables(2, 0, 0)],
+        out_specs=[pl.BlockSpec((groups, TILE, LANES), lambda i: (0, i, 0))],
+    )
+    second = exchange(sent_second)
+    first, derivative, solve, wave, frequency, couple, positions = lax.optimization_barrier(
+        (first, derivative, solve, wave, frequency, couple, positions)
+    )
+
+    grid = vmem(M, LANES)
+    spectrum = vmem(NW, 2 * NB, LANES)
+    folded = vmem(TIMES, NB, LANES)
+    turned = vmem(groups, modes // 2, LANES)
+    physical = (TIMES, NB, LANES)
+    half_physical = (TIMES, NB // 2, LANES)
+    f1, g1, f_last, g_last, mean = call(
+        functools.partial(synthesis, True),
+        [positions, first, forward, table],
+        [physical, physical, half_physical, half_physical, (8, LANES)],
+        [grid, spectrum, turned],
+        scalars=1,
+        cost=3 * 10**9,
+    )
+    s1 = lax.ppermute(f1, "modes", neighbours)
+    s_last = lax.ppermute(f_last, "modes", neighbours)
+    (back_first,) = call(
+        functools.partial(force_analysis, True),
+        [positions, f1, f1, s1, g1, derivative, backward, table, f_last, s_last, g_last, mean],
+        [(groups, first_rows + 8, LANES)],
+        [folded, folded, grid, turned],
+        scalars=1,
+        cost=3 * 10**9,
+    )
+    got_first = exchange(back_first)
+    f2, g2 = call(
+        functools.partial(synthesis, False),
+        [positions, second, forward, table],
+        [physical, physical],
+        [grid, spectrum],
+        scalars=1,
+        cost=2 * 10**9,
+    )
+    s2 = lax.ppermute(f2, "modes", neighbours)
+    (back_second,) = call(
+        functools.partial(force_analysis, False),
+        [positions, f1, f2, s2, g2, derivative, backward, table],
+        [(groups, modes, LANES)],
+        [folded, folded, grid],
+        scalars=1,
+        cost=2 * 10**9,
+    )
+    got_second = exchange(back_second)
+
+    stacked = TILE * PARTS
+    state = (STRIPES * PARTS, modes, LANES)
+    state_spec = pl.BlockSpec((STRIPES * PARTS, TILE, LANES), lambda i: (0, i, 0))
+    returned_spec = pl.BlockSpec((groups, TILE, LANES), lambda i: (0, i, 0))
+    last_spec = pl.BlockSpec((groups, TILE, LANES), lambda i: (0, tiles + i % half, 0))
+    mean_spec = pl.BlockSpec((groups, 8, LANES), lambda i: (0, first_rows // 8, 0))
+    mode_spec = pl.BlockSpec((TILE, LANES), lambda i: (i, 0))
+    all_spec = pl.BlockSpec((TILE, stride, LANES), lambda i: (i, 0, 0))
+    halves = [vmem(STRIPES, stacked, LANES, dtype=jnp.bfloat16)] * 2 + [vmem(stacked, LANES, dtype=jnp.bfloat16)] * 2
+    solve_spec = fixed(*solve.shape)
+    start, iterate, cross = call(
+        relax_first,
+        [rows, got_first, got_first, got_first, base_flow.reshape(STRIPES, LANES), couple, wave, frequency, solve],
+        [state, state, (8, LANES)],
+        halves,
+        cost=2 * 10**9,
+        grid=(tiles,),
+        in_specs=[
+            all_spec,
+            returned_spec,
+            last_spec,
+            mean_spec,
+            fixed(STRIPES, LANES),
+            fixed(*couple.shape),
+            mode_spec,
+            mode_spec,
+            solve_spec,
+        ],
+        out_specs=[state_spec, state_spec, fixed(8, LANES)],
+    )
+    (out,) = call(
+        relax_last,
+        [start, iterate, got_second, cross, couple, wave, frequency, solve],
+        [(modes, stride, LANES)],
+        [vmem(STRIPES * PARTS, TILE, LANES)] * 2 + halves,
+        cost=2 * 10**9,
+        grid=(tiles,),
+        in_specs=[
+            state_spec,
+            state_spec,
+            returned_spec,
+            fixed(8, LANES),
+            fixed(*couple.shape),
+            mode_spec,
+            mode_spec,
+            solve_spec,
+        ],
+        out_specs=[all_spec],
+    )
+    out = out.reshape(modes, 5, STRIPES, 2, LANES).transpose(0, 1, 3, 2, 4).reshape(modes, 5, 2, points)
+    return out.transpose(0, 2, 1, 3)
+
+
+def local_any(amplitudes, mode_table, slab_map, base_flow, base_coupling, slab_inverse, wall_operator):
+    points = amplitudes.shape[3]
+    fits = points == STRIPES * LANES and points // lax.axis_size("modes") == SHARE
+    fits = fits and slab_inverse.shape == (2 * STRIPES, SLAB, SLAB) and amplitudes.shape[0] % (2 * ROWS) == 0
+    chosen = local_halves if fits else local
+    return chosen(amplitudes, mode_table, slab_map, base_flow, base_coupling, slab_inverse, wall_operator)
+
+
 def solution(mesh):
     return jax.shard_map(
-        local,
+        local_any,
         mesh=mesh,
         in_specs=(
             P(("runs", "modes"), None, None, None),

time: 1140 us -> 291 us (0.26); the launches traced: 1130 us -> 290 us
  local copies, waits for them, and re-layouts: 472 us -> 18.5 us
  blocking collectives: 157 us -> 0 us
  matrix products: 127 us -> 0 us
  waiting for transfers between devices: 256 us -> 133 us
  Pallas kernels: 0 us -> 113 us
  other arithmetic: 98.3 us -> 2.86 us
  starting transfers between devices: 11.6 us -> 23.4 us
    gather x8 -> x0, local copies, waits for them, and re-layouts: 222 us -> none  [the longest x2 119 us: local(): gridded = by_mode[..., mode_at].reshape(2, field_count, point_share, NW, NB)]
    all_gather x1 -> x0, blocking collectives: 157 us -> none  [local(): lax.all_gather(spanwise_vel[0, :, 0, 0], 'modes', axis=0, tiled=True)]
    reshape x12 -> x1, local copies, waits for them, and re-layouts: 139 us -> 0.62 us  [local_halves(): couple = base_coupling.reshape(25 * STRIPES, LANES)]
    all_to_all x2 -> x4, waiting for transfers between devices: 256 us -> 127 us  [the longest x1 50.6 us: local_halves(): first = exchange(sent_first.reshape(groups, first_rows, LANES))]
    dot_general x37 -> x0, matrix products: 127 us -> none  [the longest x3 31.5 us: relaxation(): coupled = jnp.einsum('kjy,acjy->acky', matrix, iterate, precision=precise)]
    pallas_call x0 -> x8, Pallas kernels: none -> 113 us  [call(): pl.pallas_call(kernel, out_shape=[jax.ShapeDtypeStruct(shape, jnp.float32...]
    unnamed x56 -> x26, local copies, waits for them, and re-layouts: 62 us -> 4.57 us
    add x4 -> x1, other arithmetic: 31.9 us -> 0.64 us  [local_halves(): positions = mode_table[:, 0] * NB + mode_table[:, 1]]
  transfers between devices with their start and end apart: 2 -> 7, of which waited for: 1 -> 5; matrix products, arithmetic and copies ran while one was open for 6% -> 6% of each run, Pallas kernels for 0% -> 31%
where the time goes in v2:
time: 291 us; the launch traced here: 290 us
  waiting for transfers between devices  133 us (46%)
  Pallas kernels  113 us (39%)
  starting transfers between devices  23.4 us (8%)
  local copies, waits for them, and re-layouts  18.5 us (6%)
    pallas_call x8, Pallas kernels, call(): pl.pallas_call(kernel, out_shape=[jax.ShapeDtypeStruct(shape, jnp.float32...  113 us
    all_to_all x1, waiting for transfers between devices, local_halves(): first = exchange(sent_first.reshape(groups, first_rows, LANES))  50.6 us
    all_to_all x1, waiting for transfers between devices, local_halves(): got_first = exchange(back_first)  43.4 us
    all_to_all x1, waiting for transfers between devices, local_halves(): got_second = exchange(back_second)  32.6 us
    all_to_all x1, starting transfers between devices, local_halves(): first = exchange(sent_first.reshape(groups, first_rows, LANES))  6.7 us
    all_to_all x1, starting transfers between devices, local_halves(): got_first = exchange(back_first)  6.02 us
  transfers between devices with their start and end apart: 7, of which 5 were waited for; matrix products, arithmetic and copies ran while one was open for 6% of the time, Pallas kernels for 31%

profile of v2, /device:TPU:13, one launch (start us, length us, event | category | flops | bytes accessed | tf_op | source)
XLA Modules:
  0.0 290.4 jit_solution(14900098557371109497)
XLA Ops:
  0.0 6.6 %shard_map.100 = f32[16,3,128,128]{3,2,1,0:T(8,128)} custom-call(f32[256,40,128]{2,1,0:T(8,128)} %bitcast.32, f32[256,40,128]{2,1,0:T(8,128)} %bitcast.33, f32[256,40,128]{2,1,0:T(8,128)} %bitcast.34, f32[256,40,128]{2,1,0:T(8,128)} %bitcast.35), custom_call_target="tpu_custom_call" | custom-call | flops 100000000 | bytes 8388608 | tf_op jit(solution)/shard_map/pallas_call | solution.py:746
  6.6 6.7 %all-to-all-start = ((f32[16,384,128]{2,1,0:T(8,128)}), f32[16,384,128]{2,1,0:T(8,128)S(1)}, u32[]{:S(2)}, u32[]{:S(2)}) async-start(f32[16,384,128]{2,1,0:T(8,128)} %bitcast.38), calls=%async_computation | async-start | bytes 6291456 | tf_op jit(solution)/shard_map/all_to_all | solution.py:807
  14.3 0.7 copy.20
  15.7 0.8 mul.162
  16.6 0.7 mul.177
  17.3 1.8 copy.23
  19.2 0.7 mul.170
  20.0 1.8 copy.22
  21.8 0.8 copy.21
  22.6 1.9 mul.165
  24.6 1.3 mul.166
  25.9 6.7 %shard_map.104 = f32[16,256,128]{2,1,0:T(8,128)} custom-call(f32[256,40,128]{2,1,0:T(8,128)} %bitcast.36), custom_call_target="tpu_custom_call" | custom-call | flops 100000000 | bytes 8388608 | tf_op jit(solution)/shard_map/pallas_call | solution.py:746
  32.6 50.6 %all-to-all-done.r_ref = f32[16,384,128]{2,1,0:T(8,128)S(1)} async-done(((f32[16,384,128]{2,1,0:T(8,128)}), f32[16,384,128]{2,1,0:T(8,128)S(1)}, u32[]{:S(2)}, u32[]{:S(2)}) %all-to-all-start) | async-done | bytes 3145760 | tf_op jit(solution)/shard_map/all_to_all | solution.py:807
  83.2 1.7 copy-done.1
  84.9 4.9 %all-to-all-start.2 = ((f32[16,256,128]{2,1,0:T(8,128)}), f32[16,256,128]{2,1,0:T(8,128)}, u32[]{:S(2)}, u32[]{:S(2)}) async-start(f32[16,256,128]{2,1,0:T(8,128)} %shard_map.104), calls=%async_computation.2 | async-start | bytes 4194304 | tf_op jit(solution)/shard_map/all_to_all | solution.py:818
  91.7 0.9 pad_maximum_fusion.1.sw_ref
  92.6 0.7 broadcast_in_dim.55.om_ref
  93.3 0.8 broadcast_in_dim.30.kz_ref
  94.1 21.0 %shard_map.101 = (f32[17,128,128]{2,1,0:T(8,128)}, f32[17,128,128]{2,1,0:T(8,128)}, f32[17,64,128]{2,1,0:T(8,128)}, f32[17,64,128]{2,1,0:T(8,128)}, f32[8,128]{1,0:T(8,128)}) custom-call(s32[4096]{0:T(1024)} %bitcast.42, f32[16,384,128]{2,1,0:T(8,128)} %copy-done.1, bf16[512,256]{1,0:T(8,128)(2,1)} %constant.125.clone.w_ref, ...), custom_call_target="tpu_custom_call" | custom-call | flops 3000000000 | bytes 8388608 | tf_op jit(solution)/shard_map/pallas_call | solution.py:746
  115.6 3.3 %collective-permute-done.1.refs_1_ = f32[17,64,128]{2,1,0:T(8,128)S(1)} collective-permute-done((f32[17,64,128]{2,1,0:T(8,128)}, f32[17,64,128]{2,1,0:T(8,128)S(1)}, u32[]{:S(2)}, u32[]{:S(2)}) %collective-permute-start.1) | collective-permute-done | bytes 557088 | tf_op jit(solution)/shard_map/ppermute | solution.py:838
  118.9 0.9 copy-done.12
  120.1 21.4 %shard_map.102 = f32[16,392,128]{2,1,0:T(8,128)} custom-call(s32[4096]{0:T(1024)} %bitcast.43, f32[17,128,128]{2,1,0:T(8,128)} %get-tuple-element.24.vw_ref.f_ref, f32[17,128,128]{2,1,0:T(8,128)} %get-tuple-element.24.vw_ref.f_ref, f32[17,128,128]{2,1,0:T(8,128)} %copy-done.11, f32[17,128,128]{2,1,0:T(8,128)} %get-tuple-element.25.g_ref, ...), custom_call_target="tpu_custom_call" | custom-call | flops 3000000000 | bytes 8388608 | tf_op jit(solution)/shard_map/pallas_call | solution.py:746
  141.5 6.0 %all-to-all-start.1 = ((f32[16,392,128]{2,1,0:T(8,128)}), f32[16,392,128]{2,1,0:T(8,128)S(1)}, u32[]{:S(2)}, u32[]{:S(2)}) async-start(f32[16,392,128]{2,1,0:T(8,128)} %shard_map.102), calls=%async_computation.1 | async-start | bytes 6422528 | tf_op jit(solution)/shard_map/all_to_all | solution.py:847
  147.5 12.9 %shard_map.105 = (f32[17,128,128]{2,1,0:T(8,128)}, f32[17,128,128]{2,1,0:T(8,128)}) custom-call(s32[4096]{0:T(1024)} %bitcast.44, f32[16,256,128]{2,1,0:T(8,128)} %all-to-all-done.2.r_ref, bf16[512,256]{1,0:T(8,128)(2,1)} %constant.125.clone.w_ref, f32[32,8,128]{2,1,0:T(8,128)} %constant.127.clone.tab_ref), custom_call_target="tpu_custom_call" | custom-call | flops 2000000000 | bytes 8388608 | tf_op jit(solution)/shard_map/pallas_call | solution.py:746
  160.8 2.7 collective-permute-done.2.s_ref
  163.5 11.9 %shard_map.106 = f32[16,256,128]{2,1,0:T(8,128)} custom-call(s32[4096]{0:T(1024)} %bitcast.45, f32[17,128,128]{2,1,0:T(8,128)} %get-tuple-element.24.vw_ref.f_ref, f32[17,128,128]{2,1,0:T(8,128)} %get-tuple-element.36.f_ref, f32[17,128,128]{2,1,0:T(8,128)} %collective-permute-done.2.s_ref, f32[17,128,128]{2,1,0:T(8,128)} %get-tuple-element.37.g_ref, ...), custom_call_target="tpu_custom_call" | custom-call | flops 2000000000 | bytes 8388608 | tf_op jit(solution)/shard_map/pallas_call | solution.py:746
  175.4 43.4 %all-to-all-done.1.b_ref.t_ref.mean_ref = f32[16,392,128]{2,1,0:T(8,128)S(1)} async-done(((f32[16,392,128]{2,1,0:T(8,128)}), f32[16,392,128]{2,1,0:T(8,128)S(1)}, u32[]{:S(2)}, u32[]{:S(2)}) %all-to-all-start.1) | async-done | bytes 3211296 | tf_op jit(solution)/shard_map/all_to_all | solution.py:847
  218.8 1.7 copy-done
  220.5 4.9 %all-to-all-start.3 = ((f32[16,256,128]{2,1,0:T(8,128)}), f32[16,256,128]{2,1,0:T(8,128)}, u32[]{:S(2)}, u32[]{:S(2)}) async-start(f32[16,256,128]{2,1,0:T(8,128)} %shard_map.106), calls=%async_computation.3 | async-start | bytes 4194304 | tf_op jit(solution)/shard_map/all_to_all | solution.py:865
  225.4 14.9 %shard_map.103 = (f32[40,256,128]{2,1,0:T(8,128)}, f32[40,256,128]{2,1,0:T(8,128)}, f32[8,128]{1,0:T(8,128)}) custom-call(f32[256,40,128]{2,1,0:T(8,128)} %bitcast.37, f32[16,392,128]{2,1,0:T(8,128)} %copy-done, f32[16,392,128]{2,1,0:T(8,128)} %copy-done, f32[16,392,128]{2,1,0:T(8,128)} %copy-done, f32[4,128]{1,0:T(4,128)} %bitcast.48, ...), custom_call_target="tpu_custom_call" | custom-call | flops 2000000000 | bytes 8388608 | tf_op jit(solution)/shard_map/pallas_call | solution.py:746
  240.3 32.6 %all-to-all-done.3.b_ref = f32[16,256,128]{2,1,0:T(8,128)} async-done(((f32[16,256,128]{2,1,0:T(8,128)}), f32[16,256,128]{2,1,0:T(8,128)}, u32[]{:S(2)}, u32[]{:S(2)}) %all-to-all-start.3) | async-done | bytes 2097184 | tf_op jit(solution)/shard_map/all_to_all | solution.py:865
  272.9 17.5 %shard_map.107 = f32[256,40,128]{2,1,0:T(8,128)} custom-call(f32[40,256,128]{2,1,0:T(8,128)} %get-tuple-element.34.start_ref, f32[40,256,128]{2,1,0:T(8,128)} %get-tuple-element.35.first_ref, f32[16,256,128]{2,1,0:T(8,128)} %all-to-all-done.3.b_ref, f32[8,128]{1,0:T(8,128)} %get-tuple-element.38.cf_ref, f32[100,128]{1,0:T(8,128)} %reshape.250.coup_ref, ...), custom_call_target="tpu_custom_call" | custom-call | flops 2000000000 | bytes 8388608 | tf_op jit(solution)/shard_map/pallas_call | solution.py:746
  (57 shorter events, 5.0 us)
Async XLA Ops:
  6.6 6.7 %copy-start.10 = (s32[8]{0:T(128)S(1)}, s32[8]{0:T(128)}, u32[]{:S(2)}) copy-start(s32[8]{0:T(128)} %param.12) | copy-start | bytes 100
  6.6 7.1 %copy-start.2 = (f32[8,64,64]{2,1,0:T(8,128)S(1)}, f32[8,64,64]{2,1,0:T(8,128)}, u32[]{:S(2)}) copy-start(f32[8,64,64]{2,1,0:T(8,128)} %param.15) | copy-start | bytes 393220
  6.6 7.6 %copy-start.8 = (f32[64,64]{1,0:T(8,128)S(1)}, f32[64,64]{1,0:T(8,128)}, u32[]{:S(2)}) copy-start(f32[64,64]{1,0:T(8,128)} %param.16) | copy-start | bytes 49156
  6.6 8.4 %copy-start.7 = (f32[25,512]{1,0:T(8,128)S(1)}, f32[25,512]{1,0:T(8,128)}, u32[]{:S(2)}) copy-start(f32[25,512]{1,0:T(8,128)} %param.14) | copy-start | bytes 153604
  6.6 76.6 %all-to-all-start = ((f32[16,384,128]{2,1,0:T(8,128)}), f32[16,384,128]{2,1,0:T(8,128)S(1)}, u32[]{:S(2)}, u32[]{:S(2)}) async-start(f32[16,384,128]{2,1,0:T(8,128)} %bitcast.38), calls=%async_computation | async-start | bytes 6291456 | tf_op jit(solution)/shard_map/all_to_all | solution.py:807
  32.6 57.2 %copy-start.6 = (f32[2,32,32]{2,1,0:T(8,128)S(1)}, f32[2,32,32]{2,1,0:T(8,128)}, u32[]{:S(2)}) copy-start(f32[2,32,32]{2,1,0:T(8,128)} %copy.20) | copy-start | bytes 24580
  32.6 57.6 %copy-start.9 = (s32[4096,2]{0,1:T(2,128)S(1)}, s32[4096,2]{0,1:T(2,128)}, u32[]{:S(2)}) copy-start(s32[4096,2]{0,1:T(2,128)} %param.11) | copy-start | bytes 98308
  32.6 58.9 %copy-start.5 = (f32[128,128]{1,0:T(8,128)S(1)}, f32[128,128]{1,0:T(8,128)}, u32[]{:S(2)}) copy-start(f32[128,128]{1,0:T(8,128)} %mul.162) | copy-start | bytes 196612
  83.2 1.7 copy-start.1
  84.9 56.6 %all-to-all-start.2 = ((f32[16,256,128]{2,1,0:T(8,128)}), f32[16,256,128]{2,1,0:T(8,128)}, u32[]{:S(2)}, u32[]{:S(2)}) async-start(f32[16,256,128]{2,1,0:T(8,128)} %shard_map.104), calls=%async_computation.2 | async-start | bytes 4194304 | tf_op jit(solution)/shard_map/all_to_all | solution.py:818
  89.8 1.8 copy-start.3
  89.8 1.8 copy-start.4
  115.1 3.8 %collective-permute-start = (f32[17,128,128]{2,1,0:T(8,128)}, f32[17,128,128]{2,1,0:T(8,128)S(1)}, u32[]{:S(2)}, u32[]{:S(2)}) collective-permute-start(f32[17,128,128]{2,1,0:T(8,128)} %get-tuple-element.24.vw_ref.f_ref), channel_id=1, source_target_pairs={{0,1},{1,0},{2,3},{3,2},{4,5},{5,4},{6,7},{7,6},{8,9},{9,8},{10,11... | collective-permute-start | bytes 3342344 | tf_op jit(solution)/shard_map/ppermute | solution.py:837
  115.5 3.4 %collective-permute-start.1 = (f32[17,64,128]{2,1,0:T(8,128)}, f32[17,64,128]{2,1,0:T(8,128)S(1)}, u32[]{:S(2)}, u32[]{:S(2)}) collective-permute-start(f32[17,64,128]{2,1,0:T(8,128)} %get-tuple-element.27.refs_0_), channel_id=1, source_target_pairs={{0,1},{1,0},{2,3},{3,2},{4,5},{5,4},{6,7},{7,6},{8,9},{9,8},{10,11... | collective-permute-start | bytes 1671176 | tf_op jit(solution)/shard_map/ppermute | solution.py:838
  118.9 0.9 copy-start.12
  118.9 1.2 copy-start.11
  141.5 77.3 %all-to-all-start.1 = ((f32[16,392,128]{2,1,0:T(8,128)}), f32[16,392,128]{2,1,0:T(8,128)S(1)}, u32[]{:S(2)}, u32[]{:S(2)}) async-start(f32[16,392,128]{2,1,0:T(8,128)} %shard_map.102), calls=%async_computation.1 | async-start | bytes 6422528 | tf_op jit(solution)/shard_map/all_to_all | solution.py:847
  160.4 3.1 %collective-permute-start.2 = (f32[17,128,128]{2,1,0:T(8,128)}, f32[17,128,128]{2,1,0:T(8,128)}, u32[]{:S(2)}, u32[]{:S(2)}) collective-permute-start(f32[17,128,128]{2,1,0:T(8,128)} %get-tuple-element.36.f_ref), channel_id=1, source_target_pairs={{0,1},{1,0},{2,3},{3,2},{4,5},{5,4},{6,7},{7,6},{8,9},{9,8},{10,11... | collective-permute-start | bytes 3342344 | tf_op jit(solution)/shard_map/ppermute | solution.py:856
  218.8 1.7 copy-start
  220.5 52.4 %all-to-all-start.3 = ((f32[16,256,128]{2,1,0:T(8,128)}), f32[16,256,128]{2,1,0:T(8,128)}, u32[]{:S(2)}, u32[]{:S(2)}) async-start(f32[16,256,128]{2,1,0:T(8,128)} %shard_map.106), calls=%async_computation.3 | async-start | bytes 4194304 | tf_op jit(solution)/shard_map/all_to_all | solution.py:865

commit v3 on v2

--- a/solution.py
+++ b/solution.py
@@ -187,6 +187,7 @@
 STRIPES = 4
 PARTS = 10
 TILE = 32
+PACK_TILE = 64
 MIB = 1024 * 1024
 
 
@@ -209,10 +210,12 @@
 
 def block_transpose(rows, low, even):
     r0, r1, r2, r3 = rows
-    t0 = jnp.where(low, r0, roll(r2, 64))
-    t2 = jnp.where(low, roll(r0, 64), r2)
-    t1 = jnp.where(low, r1, roll(r3, 64))
-    t3 = jnp.where(low, roll(r1, 64), r3)
+    crossed = roll(jnp.where(low, r2, r0), 64)
+    t0 = jnp.where(low, r0, crossed)
+    t2 = jnp.where(low, crossed, r2)
+    crossed = roll(jnp.where(low, r3, r1), 64)
+    t1 = jnp.where(low, r1, crossed)
+    t3 = jnp.where(low, crossed, r3)
     return (
         jnp.where(even, t0, roll(t1, 32)),
         jnp.where(even, roll(t0, 96), t1),
@@ -283,7 +286,7 @@
 
 
 def pack_first(near_ref, far_ref, near_last_ref, far_last_ref, o_ref):
-    low, even = lane_masks((TILE, LANES))
+    low, even = lane_masks((PACK_TILE, LANES))
     pieces = (
         (near_ref, 0, near_ref, 2 * STRIPES),
         (far_ref, 0, far_ref, 2 * STRIPES),
@@ -295,7 +298,7 @@
 
 
 def pack_second(near_ref, o_ref):
-    low, even = lane_masks((TILE, LANES))
+    low, even = lane_masks((PACK_TILE, LANES))
     for group, value in enumerate(pack_pair(near_ref, 0, near_ref, 2 * STRIPES, low, even)):
         o_ref[group] = value
 
@@ -329,31 +332,31 @@
     return jnp.where(even, roll(near, 96), far)
 
 
-def synthesis(with_last, pos_ref, r_ref, w_ref, tab_ref, *refs):
-    if with_last:
-        f_ref, g_ref, f_last_ref, g_last_ref, mean_ref, grid_ref, spec_ref, turned_ref = refs
+def scatter(pos_ref, grid_ref, cell, source, group, row):
+    for j in range(ROWS):
+        grid_ref[pl.ds(pos_ref[cell + j], 1), :] = source[group, pl.ds(row + j, 1), :]
+
+
+def synthesis_beta(w_ref, first, second):
+    wide_sign = real_sign((NB, LANES))
+    columns = [jnp.concatenate([x, -wide_sign * roll(x, 64)], 0) for x in (first, second)]
+    high, low_part = split(jnp.concatenate(columns, 1))
+    product = dot(w_ref[...], high)
+    out = product[: 2 * NB] + product[2 * NB :] + dot(w_ref[pl.ds(0, 2 * NB), :], low_part)
+    return out[:, :LANES], out[:, LANES:]
+
+
+def synthesis(with_mean, pos_ref, r_ref, w_ref, tab_ref, *refs):
+    if with_mean:
+        f_ref, g_ref, mean_ref, grid_ref, spec_ref = refs
     else:
         f_ref, g_ref, grid_ref, spec_ref = refs
     groups = r_ref.shape[0]
     modes = M // groups
-    sign, real, even = lanes_constants()
-    wide_sign = real_sign((NB, LANES))
-    wide_even = (lane_index((NB, LANES)) & 32) == 0
+    sign, real, _ = lanes_constants()
 
     def table(j):
         return tab_ref[j]
-
-    def scatter(group, mode, source, row):
-        for j in range(ROWS):
-            cell = pos_ref[group * modes + mode + j]
-            grid_ref[pl.ds(cell, 1), :] = source[group, pl.ds(row + j, 1), :]
-
-    def beta(first, second):
-        columns = [jnp.concatenate([x, -wide_sign * roll(x, 64)], 0) for x in (first, second)]
-        high, low_part = split(jnp.concatenate(columns, 1))
-        product = dot(w_ref[...], high)
-        out = product[: 2 * NB] + product[2 * NB :] + dot(w_ref[pl.ds(0, 2 * NB), :], low_part)
-        return out[:, :LANES], out[:, LANES:]
 
     def grid(a):
         return grid_ref[pl.ds(pl.multiple_of(a * NB, NB), NB), :]
@@ -361,18 +364,18 @@
     def both_halves(i):
         group = i // (modes // ROWS)
         start = pl.multiple_of(i % (modes // ROWS) * ROWS, ROWS)
-        scatter(group, start, r_ref, start)
+        scatter(pos_ref, grid_ref, i * ROWS, r_ref, group, start)
 
     loop(groups * (modes // ROWS), 1, both_halves)
-    if with_last:
+    if with_mean:
         mean_ref[...] = grid_ref[pl.ds(0, 8), :]
 
-    def full_beta(i):
-        spec_ref[2 * i], spec_ref[2 * i + 1] = beta(grid(2 * i), grid(2 * i + 1))
-
-    loop(NW // 2, 2, full_beta)
-
-    def full_omega(out_ref, shift):
+    def beta(i):
+        spec_ref[2 * i], spec_ref[2 * i + 1] = synthesis_beta(w_ref, grid(2 * i), grid(2 * i + 1))
+
+    loop(NW // 2, 2, beta)
+
+    def omega(out_ref, shift):
         def body(i):
             rows = pl.ds(pl.multiple_of(i * 8, 8), 8)
             source = pl.ds(pl.multiple_of(shift + i * 8, 8), 8)
@@ -385,26 +388,38 @@
 
         loop(NB // 8, 2, body)
 
-    full_omega(f_ref, 0)
-    full_omega(g_ref, NB)
-    if not with_last:
-        return
+    omega(f_ref, 0)
+    omega(g_ref, NB)
+
+
+def synthesis_half(pos_ref, r_ref, w_ref, tab_ref, f_ref, g_ref, grid_ref, spec_ref, turned_ref):
+    groups = r_ref.shape[0]
+    modes = M // groups
+    sign, real, even = lanes_constants()
+    wide_even = (lane_index((NB, LANES)) & 32) == 0
+
+    def table(j):
+        return tab_ref[j]
+
+    def grid(a):
+        return grid_ref[pl.ds(pl.multiple_of(a * NB, NB), NB), :]
 
     def turn(group):
-        turned_ref[group] = roll(r_ref[group, pl.ds(modes, modes // 2), :], 96)
+        turned_ref[group] = roll(r_ref[group], 96)
         for block in range(modes // 2 // ROWS):
-            scatter(group, block * ROWS, r_ref, modes + block * ROWS)
-            scatter(group, modes // 2 + block * ROWS, turned_ref, block * ROWS)
+            cell = group * modes + block * ROWS
+            scatter(pos_ref, grid_ref, cell, r_ref, group, block * ROWS)
+            scatter(pos_ref, grid_ref, cell + modes // 2, turned_ref, group, block * ROWS)
 
     loop(groups, 1, turn)
 
-    def half_beta(i):
+    def beta(i):
         columns = [pair_left(wide_even, grid(a), grid(a + HALF)) for a in (2 * i, 2 * i + 1)]
-        spec_ref[2 * i], spec_ref[2 * i + 1] = beta(*columns)
-
-    loop(HALF // 2, 2, half_beta)
-
-    def half_omega(out_ref, shift):
+        spec_ref[2 * i], spec_ref[2 * i + 1] = synthesis_beta(w_ref, *columns)
+
+    loop(HALF // 2, 2, beta)
+
+    def omega(out_ref, shift):
         def body(i):
             rows = pl.ds(pl.multiple_of(i * 8, 8), 8)
             near = pl.ds(pl.multiple_of(shift + i * 8, 8), 8)
@@ -424,15 +439,15 @@
 
         loop(NB // 16, 2, body)
 
-    half_omega(f_last_ref, 0)
-    half_omega(g_last_ref, NB)
+    omega(f_ref, 0)
+    omega(g_ref, NB)
 
 
 def force_analysis(with_last, pos_ref, vw_ref, f_ref, s_ref, g_ref, d_ref, w_ref, tab_ref, *refs):
     if with_last:
-        f_last_ref, s_last_ref, g_last_ref, mean_ref, o_ref, k_ref, r_ref, n_ref, turned_ref = refs
+        f_last_ref, s_last_ref, g_last_ref, o_ref, k_ref, r_ref, n_ref, turned_ref = refs
     else:
-        o_ref, k_ref, r_ref, n_ref = refs
+        mean_ref, o_ref, k_ref, r_ref, n_ref = refs
     groups = o_ref.shape[0]
     modes = M // groups
     sign, real, _ = lanes_constants()
@@ -510,6 +525,8 @@
 
     loop(groups * (modes // ROWS), 1, both_halves)
     if not with_last:
+        for group in range(groups):
+            o_ref[group, pl.ds(modes, 8), :] = mean_ref[...]
         return
 
     def half_product(t, alone=False):
@@ -547,21 +564,23 @@
         here = pl.ds(modes, modes // 2)
         near = o_ref[group, here, :]
         o_ref[group, here, :] = pair_left((lane_index(near.shape) & 32) == 0, near, turned_ref[group])
-        o_ref[group, pl.ds(modes // 2 * 3, 8), :] = mean_ref[...]
 
     loop(groups, 1, turn)
 
 
-def find_rims(x_of, zh_ref, zl_ref):
+def find_rims(x_of, parts, zh_ref, zl_ref):
     lane = lane_index((TILE, LANES))
     edge = ((lane & 63) == 0) | ((lane & 63) == 63)
     for part in range(PARTS):
+        rows = pl.ds(part * TILE, TILE)
+        if part not in parts:
+            zh_ref[rows, :] = zl_ref[rows, :] = jnp.zeros((TILE, LANES), jnp.bfloat16)
+            continue
         rims = None
         for stripe in range(STRIPES):
             term = jnp.where(edge, x_of(stripe, part), 0.0)
             term = roll(term, 2 * stripe) if stripe else term
             rims = term if rims is None else rims + term
-        rows = pl.ds(part * TILE, TILE)
         zh_ref[rows, :], zl_ref[rows, :] = split(rims)
 
 
@@ -570,13 +589,18 @@
     return both[:, :LANES] + both[:, LANES:] + dot(low_part, weights[:, :LANES])
 
 
-def relax(stripe, x_of, cross, kz_ref, om_ref, coup_ref, sw_ref, rh_ref, rl_ref, zh_ref, zl_ref):
-    values = [x_of(stripe, part) for part in range(PARTS)]
+def relax(stripe, x_of, parts, cross, kz_ref, om_ref, coup_ref, sw_ref, rh_ref, rl_ref, zh_ref, zl_ref):
+    values = {part: x_of(stripe, part) for part in parts}
     rotation = kz_ref[...] * cross - om_ref[...]
     for k in range(5):
-        out_re = rotation * values[2 * k + 1]
-        out_im = -(rotation * values[2 * k])
+        out_re = jnp.zeros((TILE, LANES), jnp.float32)
+        out_im = out_re
+        if 2 * k in values:
+            out_re = rotation * values[2 * k + 1]
+            out_im = -(rotation * values[2 * k])
         for j in range(5):
+            if 2 * j not in values:
+                continue
             weight = coup_ref[pl.ds((k * 5 + j) * STRIPES + stripe, 1), :]
             out_re = out_re - weight * values[2 * j]
             out_im = out_im - weight * values[2 * j + 1]
@@ -585,13 +609,13 @@
             rh_ref[stripe, rows, :], rl_ref[stripe, rows, :] = split(out)
     high = jnp.concatenate([rh_ref[stripe], zh_ref[...]], 1)
     low_rows = jnp.concatenate([rl_ref[stripe], zl_ref[...]], 1)
-    return three_pass(high, low_rows, sw_ref[stripe])
-
-
-def relax_first(a_ref, b_ref, t_ref, mean_ref, base_ref, coup_ref, kz_ref, om_ref, sw_ref, start_ref, x_ref, cf_ref, rh_ref, rl_ref, zh_ref, zl_ref):
+    return three_pass(high, low_rows, sw_ref[stripe]).reshape(PARTS, TILE, LANES)
+
+
+def relax_first(a_ref, b_ref, mean_ref, base_ref, coup_ref, kz_ref, om_ref, sw_ref, out_ref, cf_ref, right_ref, x_ref, *halves):
+    rh_ref, rl_ref, zh_ref, zl_ref = halves
     low, even = lane_masks((TILE, LANES))
     block_of = lane_index((1, LANES)) // SHARE
-    far = pl.program_id(0) >= pl.num_programs(0) // 2
     for stripe in range(STRIPES):
         total = base_ref[pl.ds(stripe, 1), :]
         for block in range(BLOCKS):
@@ -599,74 +623,75 @@
             total = total + jnp.where(block_of == block, roll(row, SHARE * (block - 1)), 0.0)
         cf_ref[pl.ds(stripe, 1), :] = total
 
-    def x_of(stripe, part):
-        return spread(a_ref, part // 2 * 2 * STRIPES + stripe * 2 + part % 2)
-
     for stripe in range(STRIPES):
         groups = [stripe * BLOCKS + block for block in range(BLOCKS)]
         velocity = block_transpose([b_ref[group] for group in groups], low, even)
-        last = block_transpose([t_ref[group] for group in groups], low, even)
-        gained = {
-            4: velocity[0],
-            6: velocity[1],
-            5: velocity[2],
-            7: velocity[3],
-            8: jnp.where(far, last[1], last[0]),
-            9: jnp.where(far, last[3], last[2]),
-        }
+        gained = {4: velocity[0], 6: velocity[1], 5: velocity[2], 7: velocity[3]}
         for part in range(PARTS):
-            right = x_of(stripe, part)
+            value = spread(a_ref, part // 2 * 2 * STRIPES + stripe * 2 + part % 2)
+            x_ref[stripe * PARTS + part] = value
             if part in gained:
-                right = right + march_step * gained[part]
+                value = value + march_step * gained[part]
             rows = pl.ds(part * TILE, TILE)
-            rh_ref[stripe, rows, :], rl_ref[stripe, rows, :] = split(right)
+            rh_ref[stripe, rows, :], rl_ref[stripe, rows, :] = split(value)
         solved = three_pass(rh_ref[stripe], rl_ref[stripe], sw_ref[stripe, pl.ds(0, LANES), :])
-        start_ref[pl.ds(stripe * PARTS, PARTS)] = solved.reshape(PARTS, TILE, LANES)
-    find_rims(x_of, zh_ref, zl_ref)
-    for stripe in range(STRIPES):
-        here = pl.ds(stripe * PARTS, PARTS)
-        cross = cf_ref[pl.ds(stripe, 1), :]
-        new = relax(stripe, x_of, cross, kz_ref, om_ref, coup_ref, sw_ref, rh_ref, rl_ref, zh_ref, zl_ref)
-        x_ref[here] = start_ref[here] + new.reshape(PARTS, TILE, LANES)
-
-
-def relax_last(start_ref, first_ref, b_ref, cf_ref, coup_ref, kz_ref, om_ref, sw_ref, o_ref, right_ref, x_ref, rh_ref, rl_ref, zh_ref, zl_ref):
-    low, even = lane_masks((TILE, LANES))
-    gained = 4
-    for stripe in range(STRIPES):
-        here = pl.ds(stripe * PARTS, PARTS)
-        rows = [b_ref[stripe * BLOCKS + block] for block in range(BLOCKS)]
-        first_re, second_re, first_im, second_im = block_transpose(rows, low, even)
-        for part, value in enumerate((first_re, first_im, second_re, second_im)):
-            place = pl.ds(part * TILE, TILE)
-            rh_ref[stripe, place, :], rl_ref[stripe, place, :] = split(march_step * value)
-        place = pl.ds(0, gained * TILE)
-        weights = sw_ref[stripe, pl.ds(0, LANES), :]
-        added = three_pass(rh_ref[stripe, place, :], rl_ref[stripe, place, :], weights).reshape(gained, TILE, LANES)
-        with_added = pl.ds(stripe * PARTS, gained)
-        others = pl.ds(stripe * PARTS + gained, PARTS - gained)
-        right_ref[with_added] = start_ref[with_added] + added
-        x_ref[with_added] = first_ref[with_added] + added
-        right_ref[others] = start_ref[others]
-        x_ref[others] = first_ref[others]
+        right_ref[pl.ds(stripe * PARTS, PARTS)] = solved.reshape(PARTS, TILE, LANES)
 
     def x_of(stripe, part):
         return x_ref[stripe * PARTS + part]
 
-    flat = o_ref.reshape(TILE * PARTS * STRIPES, LANES)
-    for sweep in range(1, SWEEPS):
-        find_rims(x_of, zh_ref, zl_ref)
+    for sweep in range(SWEEPS):
+        target = x_ref if sweep < SWEEPS - 1 else out_ref
+        find_rims(x_of, range(PARTS), zh_ref, zl_ref)
         for stripe in range(STRIPES):
             here = pl.ds(stripe * PARTS, PARTS)
             cross = cf_ref[pl.ds(stripe, 1), :]
-            new = relax(stripe, x_of, cross, kz_ref, om_ref, coup_ref, sw_ref, rh_ref, rl_ref, zh_ref, zl_ref)
-            new = right_ref[here] + new.reshape(PARTS, TILE, LANES)
-            if sweep < SWEEPS - 1:
-                x_ref[here] = new
-                continue
+            new = relax(stripe, x_of, range(PARTS), cross, kz_ref, om_ref, coup_ref, sw_ref, *halves)
+            target[here] = right_ref[here] + new
+
+
+LATE = (0, 1, 2, 3, 8, 9)
+
+
+def relax_last(first_ref, b_ref, t_ref, cf_ref, coup_ref, kz_ref, om_ref, sw_ref, o_ref, right_ref, x_ref, *halves):
+    rh_ref, rl_ref, zh_ref, zl_ref = halves
+    low, even = lane_masks((TILE, LANES))
+    far = pl.program_id(0) >= pl.num_programs(0) // 2
+    count = len(LATE)
+    for stripe in range(STRIPES):
+        groups = [stripe * BLOCKS + block for block in range(BLOCKS)]
+        pair = block_transpose([b_ref[group] for group in groups], low, even)
+        last = block_transpose([t_ref[group] for group in groups], low, even)
+        last = (jnp.where(far, last[1], last[0]), jnp.where(far, last[3], last[2]))
+        for place, value in enumerate((pair[0], pair[2], pair[1], pair[3]) + last):
+            rows = pl.ds(place * TILE, TILE)
+            rh_ref[stripe, rows, :], rl_ref[stripe, rows, :] = split(march_step * value)
+        rows = pl.ds(0, count * TILE)
+        weights = sw_ref[stripe, pl.ds(0, LANES), :]
+        added = three_pass(rh_ref[stripe, rows, :], rl_ref[stripe, rows, :], weights)
+        right_ref[stripe] = added.reshape(count, TILE, LANES)
+
+    def right_of(stripe, part):
+        return right_ref[stripe, LATE.index(part)]
+
+    def x_of(stripe, part):
+        return x_ref[stripe * PARTS + part]
+
+    flat = o_ref.reshape(TILE * PARTS * STRIPES, LANES)
+    for sweep in range(1, SWEEPS):
+        source, parts = (right_of, LATE) if sweep == 1 else (x_of, range(PARTS))
+        find_rims(source, parts, zh_ref, zl_ref)
+        for stripe in range(STRIPES):
+            cross = cf_ref[pl.ds(stripe, 1), :]
+            new = relax(stripe, source, parts, cross, kz_ref, om_ref, coup_ref, sw_ref, *halves)
             for part in range(PARTS):
+                value = new[part] + right_of(stripe, part) if part in LATE else new[part]
+                if sweep < SWEEPS - 1:
+                    x_ref[stripe * PARTS + part] = value
+                    continue
                 offset = part // 2 * 2 * STRIPES + stripe * 2 + part % 2
-                flat[pl.ds(offset, TILE, stride=PARTS * STRIPES), :] = new[part]
+                value = value + first_ref[stripe * PARTS + part]
+                flat[pl.ds(offset, TILE, stride=PARTS * STRIPES), :] = value
 
 
 def split_host(x):
@@ -791,9 +816,9 @@
     couple = base_coupling.reshape(25 * STRIPES, LANES)
 
     def variables(count, place, shift):
-        return pl.BlockSpec((TILE, count * 2 * STRIPES, LANES), lambda i: (i + shift, place, 0))
-
-    half = tiles // 2
+        return pl.BlockSpec((PACK_TILE, count * 2 * STRIPES, LANES), lambda i: (i + shift, place, 0))
+
+    half = modes // PACK_TILE // 2
     (sent_first,) = call(
         pack_first,
         [rows] * 4,
@@ -802,7 +827,7 @@
         cost=10**8,
         grid=(half,),
         in_specs=[variables(2, 1, 0), variables(2, 1, half), variables(1, 4, 0), variables(1, 4, half)],
-        out_specs=[pl.BlockSpec((groups, 3, TILE, LANES), lambda i: (0, 0, i, 0))],
+        out_specs=[pl.BlockSpec((groups, 3, PACK_TILE, LANES), lambda i: (0, 0, i, 0))],
     )
     first = exchange(sent_first.reshape(groups, first_rows, LANES))
     (sent_second,) = call(
@@ -811,14 +836,14 @@
         [(groups, modes, LANES)],
         [],
         cost=10**8,
-        grid=(tiles,),
+        grid=(modes // PACK_TILE,),
         in_specs=[variables(2, 0, 0)],
-        out_specs=[pl.BlockSpec((groups, TILE, LANES), lambda i: (0, i, 0))],
+        out_specs=[pl.BlockSpec((groups, PACK_TILE, LANES), lambda i: (0, i, 0))],
+    )
+    sent_second, derivative, solve, wave, frequency, couple, positions = lax.optimization_barrier(
+        (sent_second, derivative, solve, wave, frequency, couple, positions)
     )
     second = exchange(sent_second)
-    first, derivative, solve, wave, frequency, couple, positions = lax.optimization_barrier(
-        (first, derivative, solve, wave, frequency, couple, positions)
-    )
 
     grid = vmem(M, LANES)
     spectrum = vmem(NW, 2 * NB, LANES)
@@ -826,41 +851,50 @@
     turned = vmem(groups, modes // 2, LANES)
     physical = (TIMES, NB, LANES)
     half_physical = (TIMES, NB // 2, LANES)
-    f1, g1, f_last, g_last, mean = call(
-        functools.partial(synthesis, True),
-        [positions, first, forward, table],
-        [physical, physical, half_physical, half_physical, (8, LANES)],
-        [grid, spectrum, turned],
-        scalars=1,
-        cost=3 * 10**9,
+    scalars = pl.BlockSpec(memory_space=pltpu.SMEM)
+
+    def spectral(kernel, received, count, place, outputs, scratch, cost):
+        block = pl.BlockSpec((groups, count, LANES), lambda i: (0, place, 0))
+        return call(
+            kernel,
+            [positions, received, forward, table],
+            outputs,
+            scratch,
+            cost=cost,
+            grid=(1,),
+            in_specs=[scalars, block, fixed(*forward.shape), fixed(*table.shape)],
+            out_specs=[fixed(*shape) for shape in outputs],
+        )
+
+    f1, g1, mean = spectral(
+        functools.partial(synthesis, True), first, modes, 0, [physical, physical, (8, LANES)], [grid, spectrum], 2 * 10**9
     )
     s1 = lax.ppermute(f1, "modes", neighbours)
+    f_last, g_last = spectral(
+        synthesis_half, first, modes // 2, 2, [half_physical] * 2, [grid, spectrum, turned], 10**9
+    )
+    s1, f_last, g_last = lax.optimization_barrier((s1, f_last, g_last))
     s_last = lax.ppermute(f_last, "modes", neighbours)
     (back_first,) = call(
+        functools.partial(force_analysis, False),
+        [positions, f1, f1, s1, g1, derivative, backward, table, mean],
+        [(groups, modes + 8, LANES)],
+        [folded, folded, grid],
+        scalars=1,
+        cost=2 * 10**9,
+    )
+    got_first = exchange(back_first)
+    f2, g2 = spectral(
+        functools.partial(synthesis, False), second, modes, 0, [physical, physical], [grid, spectrum], 2 * 10**9
+    )
+    s2 = lax.ppermute(f2, "modes", neighbours)
+    (back_second,) = call(
         functools.partial(force_analysis, True),
-        [positions, f1, f1, s1, g1, derivative, backward, table, f_last, s_last, g_last, mean],
-        [(groups, first_rows + 8, LANES)],
+        [positions, f1, f2, s2, g2, derivative, backward, table, f_last, s_last, g_last],
+        [(groups, first_rows, LANES)],
         [folded, folded, grid, turned],
         scalars=1,
         cost=3 * 10**9,
-    )
-    got_first = exchange(back_first)
-    f2, g2 = call(
-        functools.partial(synthesis, False),
-        [positions, second, forward, table],
-        [physical, physical],
-        [grid, spectrum],
-        scalars=1,
-        cost=2 * 10**9,
-    )
-    s2 = lax.ppermute(f2, "modes", neighbours)
-    (back_second,) = call(
-        functools.partial(force_analysis, False),
-        [positions, f1, f2, s2, g2, derivative, backward, table],
-        [(groups, modes, LANES)],
-        [folded, folded, grid],
-        scalars=1,
-        cost=2 * 10**9,
     )
     got_second = exchange(back_second)
 
@@ -868,49 +902,31 @@
     state = (STRIPES * PARTS, modes, LANES)
     state_spec = pl.BlockSpec((STRIPES * PARTS, TILE, LANES), lambda i: (0, i, 0))
     returned_spec = pl.BlockSpec((groups, TILE, LANES), lambda i: (0, i, 0))
-    last_spec = pl.BlockSpec((groups, TILE, LANES), lambda i: (0, tiles + i % half, 0))
-    mean_spec = pl.BlockSpec((groups, 8, LANES), lambda i: (0, first_rows // 8, 0))
+    last_spec = pl.BlockSpec((groups, TILE, LANES), lambda i: (0, tiles + i % (tiles // 2), 0))
+    mean_spec = pl.BlockSpec((groups, 8, LANES), lambda i: (0, modes // 8, 0))
     mode_spec = pl.BlockSpec((TILE, LANES), lambda i: (i, 0))
     all_spec = pl.BlockSpec((TILE, stride, LANES), lambda i: (i, 0, 0))
     halves = [vmem(STRIPES, stacked, LANES, dtype=jnp.bfloat16)] * 2 + [vmem(stacked, LANES, dtype=jnp.bfloat16)] * 2
-    solve_spec = fixed(*solve.shape)
-    start, iterate, cross = call(
+    shared_specs = [fixed(*couple.shape), mode_spec, mode_spec, fixed(*solve.shape)]
+    shared = [couple, wave, frequency, solve]
+    iterate, cross = call(
         relax_first,
-        [rows, got_first, got_first, got_first, base_flow.reshape(STRIPES, LANES), couple, wave, frequency, solve],
-        [state, state, (8, LANES)],
-        halves,
+        [rows, got_first, got_first, base_flow.reshape(STRIPES, LANES)] + shared,
+        [state, (8, LANES)],
+        [vmem(STRIPES * PARTS, TILE, LANES)] * 2 + halves,
+        cost=3 * 10**9,
+        grid=(tiles,),
+        in_specs=[all_spec, returned_spec, mean_spec, fixed(STRIPES, LANES)] + shared_specs,
+        out_specs=[state_spec, fixed(8, LANES)],
+    )
+    (out,) = call(
+        relax_last,
+        [iterate, got_second, got_second, cross] + shared,
+        [(modes, stride, LANES)],
+        [vmem(STRIPES, len(LATE), TILE, LANES), vmem(STRIPES * PARTS, TILE, LANES)] + halves,
         cost=2 * 10**9,
         grid=(tiles,),
-        in_specs=[
-            all_spec,
-            returned_spec,
-            last_spec,
-            mean_spec,
-            fixed(STRIPES, LANES),
-            fixed(*couple.shape),
-            mode_spec,
-            mode_spec,
-            solve_spec,
-        ],
-        out_specs=[state_spec, state_spec, fixed(8, LANES)],
-    )
-    (out,) = call(
-        relax_last,
-        [start, iterate, got_second, cross, couple, wave, frequency, solve],
-        [(modes, stride, LANES)],
-        [vmem(STRIPES * PARTS, TILE, LANES)] * 2 + halves,
-        cost=2 * 10**9,
-        grid=(tiles,),
-        in_specs=[
-            state_spec,
-            state_spec,
-            returned_spec,
-            fixed(8, LANES),
-            fixed(*couple.shape),
-            mode_spec,
-            mode_spec,
-            solve_spec,
-        ],
+        in_specs=[state_spec, returned_spec, last_spec, fixed(8, LANES)] + shared_specs,
         out_specs=[all_spec],
     )
     out = out.reshape(modes, 5, STRIPES, 2, LANES).transpose(0, 1, 3, 2, 4).reshape(modes, 5, 2, points)

time: 291 us -> 284 us (0.976)
  waiting for transfers between devices: 133 us -> 117 us
  Pallas kernels: 113 us -> 120 us
    all_to_all x1, waiting for transfers between devices: 43.4 us -> 10.1 us  [local_halves(): got_first = exchange(back_first)]
    all_to_all x1, waiting for transfers between devices: 32.6 us -> 46.1 us  [local_halves(): got_second = exchange(back_second)]
    all_to_all x1, waiting for transfers between devices: 0.01 us -> 11.7 us  [local_halves(): second = exchange(sent_second)]
    pallas_call x8 -> x9, Pallas kernels: 113 us -> 120 us  [call(): pl.pallas_call(kernel, out_shape=[jax.ShapeDtypeStruct(shape, jnp.float32...]
    all_to_all x1, waiting for transfers between devices: 50.6 us -> 45.5 us  [local_halves(): first = exchange(sent_first.reshape(groups, first_rows, LANES))]
  transfers between devices with their start and end apart: 7 -> 7, of which waited for: 5 -> 6; matrix products, arithmetic and copies ran while one was open for 6% -> 7% of each run, Pallas kernels for 31% -> 34%
where the time goes in v3:
time: 284 us; the launch traced here: 283 us
  Pallas kernels  120 us (42%)
  waiting for transfers between devices  117 us (41%)
  starting transfers between devices  22.3 us (8%)
  local copies, waits for them, and re-layouts  19.8 us (7%)
  other arithmetic  4.52 us (2%)
    pallas_call x9, Pallas kernels, call(): pl.pallas_call(kernel, out_shape=[jax.ShapeDtypeStruct(shape, jnp.float32...  120 us
    all_to_all x1, waiting for transfers between devices, local_halves(): got_second = exchange(back_second)  46.1 us
    all_to_all x1, waiting for transfers between devices, local_halves(): first = exchange(sent_first.reshape(groups, first_rows, LANES))  45.5 us
    all_to_all x1, waiting for transfers between devices, local_halves(): second = exchange(sent_second)  11.7 us
    all_to_all x1, waiting for transfers between devices, local_halves(): got_first = exchange(back_first)  10.1 us
    all_to_all x1, starting transfers between devices, local_halves(): first = exchange(sent_first.reshape(groups, first_rows, LANES))  6.7 us
  transfers between devices with their start and end apart: 7, of which 6 were waited for; matrix products, arithmetic and copies ran while one was open for 7% of the time, Pallas kernels for 34%

profile of v3, /device:TPU:13, one launch (start us, length us, event | category | flops | bytes accessed | tf_op | source)
XLA Modules:
  0.0 282.9 jit_solution(13265364650717094750)
XLA Ops:
  0.0 5.2 %shard_map.101 = f32[16,3,128,128]{3,2,1,0:T(8,128)} custom-call(f32[256,40,128]{2,1,0:T(8,128)} %bitcast.32, f32[256,40,128]{2,1,0:T(8,128)} %bitcast.33, f32[256,40,128]{2,1,0:T(8,128)} %bitcast.34, f32[256,40,128]{2,1,0:T(8,128)} %bitcast.35), custom_call_target="tpu_custom_call" | custom-call | flops 100000000 | bytes 8388608 | tf_op jit(solution)/shard_map/pallas_call | solution.py:771
  5.2 6.7 %all-to-all-start = ((f32[16,384,128]{2,1,0:T(8,128)}), f32[16,384,128]{2,1,0:T(8,128)S(1)}, u32[]{:S(2)}, u32[]{:S(2)}) async-start(f32[16,384,128]{2,1,0:T(8,128)} %bitcast.38), calls=%async_computation | async-start | bytes 6291456 | tf_op jit(solution)/shard_map/all_to_all | solution.py:832
  15.9 1.8 copy.23
  18.5 1.8 copy.22
  20.3 0.8 copy.21
  21.1 1.9 mul.165
  23.1 1.3 mul.166
  24.4 0.9 broadcast_multiply_fusion
  25.4 1.3 mul.160
  26.7 4.8 %shard_map.100 = f32[16,256,128]{2,1,0:T(8,128)} custom-call(f32[256,40,128]{2,1,0:T(8,128)} %bitcast.36), custom_call_target="tpu_custom_call" | custom-call | flops 100000000 | bytes 8388608 | tf_op jit(solution)/shard_map/pallas_call | solution.py:771
  32.9 0.9 broadcast_multiply_fusion.1
  33.9 0.9 pad_maximum_fusion.1.sw_ref
  35.5 0.8 broadcast_in_dim.30.kz_ref
  36.3 45.5 %all-to-all-done.r_ref = f32[16,384,128]{2,1,0:T(8,128)S(1)} async-done(((f32[16,384,128]{2,1,0:T(8,128)}), f32[16,384,128]{2,1,0:T(8,128)S(1)}, u32[]{:S(2)}, u32[]{:S(2)}) %all-to-all-start) | async-done | bytes 3145760 | tf_op jit(solution)/shard_map/all_to_all | solution.py:832
  81.8 4.9 %all-to-all-start.2 = ((f32[16,256,128]{2,1,0:T(8,128)}), f32[16,256,128]{2,1,0:T(8,128)}, u32[]{:S(2)}, u32[]{:S(2)}) async-start(f32[16,256,128]{2,1,0:T(8,128)} %shard_map.100), calls=%async_computation.2 | async-start | bytes 4194304 | tf_op jit(solution)/shard_map/all_to_all | solution.py:846
  86.7 12.9 %shard_map.102 = (f32[17,128,128]{2,1,0:T(8,128)}, f32[17,128,128]{2,1,0:T(8,128)}, f32[8,128]{1,0:T(8,128)}) custom-call(s32[4096]{0:T(1024)} %bitcast.42, f32[16,384,128]{2,1,0:T(8,128)} %copy-done.1, bf16[512,256]{1,0:T(8,128)(2,1)} %constant.125.clone.w_ref, f32[32,8,128]{2,1,0:T(8,128)} %constant.127.clone.tab_ref), custom_call_target="tpu_custom_call" | custom-call | flops 2000000000 | bytes 8388608 | tf_op jit(solution)/shard_map/pallas_call | solution.py:771
  100.0 9.6 %shard_map.103 = (f32[17,64,128]{2,1,0:T(8,128)}, f32[17,64,128]{2,1,0:T(8,128)}) custom-call(s32[4096]{0:T(1024)} %bitcast.43, f32[16,384,128]{2,1,0:T(8,128)} %copy-done.1, bf16[512,256]{1,0:T(8,128)(2,1)} %constant.125.clone.w_ref, f32[32,8,128]{2,1,0:T(8,128)} %constant.127.clone.tab_ref), custom_call_target="tpu_custom_call" | custom-call | flops 1000000000 | bytes 8388608 | tf_op jit(solution)/shard_map/pallas_call | solution.py:771
  109.6 1.0 copy-done.11
  110.6 11.9 %shard_map.104 = f32[16,264,128]{2,1,0:T(8,128)} custom-call(s32[4096]{0:T(1024)} %bitcast.44, f32[17,128,128]{2,1,0:T(8,128)} %get-tuple-element.25.vw_ref.f_ref, f32[17,128,128]{2,1,0:T(8,128)} %get-tuple-element.25.vw_ref.f_ref, f32[17,128,128]{2,1,0:T(8,128)} %copy-done.11, f32[17,128,128]{2,1,0:T(8,128)} %get-tuple-element.29.g_ref, ...), custom_call_target="tpu_custom_call" | custom-call | flops 2000000000 | bytes 8388608 | tf_op jit(solution)/shard_map/pallas_call | solution.py:771
  122.5 11.7 %all-to-all-done.2.r_ref = f32[16,256,128]{2,1,0:T(8,128)} async-done(((f32[16,256,128]{2,1,0:T(8,128)}), f32[16,256,128]{2,1,0:T(8,128)}, u32[]{:S(2)}, u32[]{:S(2)}) %all-to-all-start.2) | async-done | bytes 2097184 | tf_op jit(solution)/shard_map/all_to_all | solution.py:846
  134.2 4.9 %all-to-all-start.1 = ((f32[16,264,128]{2,1,0:T(8,128)}), f32[16,264,128]{2,1,0:T(8,128)S(1)}, u32[]{:S(2)}, u32[]{:S(2)}) async-start(f32[16,264,128]{2,1,0:T(8,128)} %shard_map.104), calls=%async_computation.1 | async-start | bytes 4325376 | tf_op jit(solution)/shard_map/all_to_all | solution.py:886
  139.2 13.1 %shard_map.106 = (f32[17,128,128]{2,1,0:T(8,128)}, f32[17,128,128]{2,1,0:T(8,128)}) custom-call(s32[4096]{0:T(1024)} %bitcast.45, f32[16,256,128]{2,1,0:T(8,128)} %all-to-all-done.2.r_ref, bf16[512,256]{1,0:T(8,128)(2,1)} %constant.125.clone.w_ref, f32[32,8,128]{2,1,0:T(8,128)} %constant.127.clone.tab_ref), custom_call_target="tpu_custom_call" | custom-call | flops 2000000000 | bytes 8388608 | tf_op jit(solution)/shard_map/pallas_call | solution.py:771
  152.8 2.6 collective-permute-done.1.s_ref
  155.8 0.8 copy-done.13
  156.6 21.3 %shard_map.107 = f32[16,384,128]{2,1,0:T(8,128)} custom-call(s32[4096]{0:T(1024)} %bitcast.46, f32[17,128,128]{2,1,0:T(8,128)} %get-tuple-element.25.vw_ref.f_ref, f32[17,128,128]{2,1,0:T(8,128)} %get-tuple-element.38.f_ref, f32[17,128,128]{2,1,0:T(8,128)} %collective-permute-done.1.s_ref, f32[17,128,128]{2,1,0:T(8,128)} %get-tuple-element.39.g_ref, ...), custom_call_target="tpu_custom_call" | custom-call | flops 3000000000 | bytes 8388608 | tf_op jit(solution)/shard_map/pallas_call | solution.py:771
  177.9 10.1 %all-to-all-done.1.b_ref.mean_ref = f32[16,264,128]{2,1,0:T(8,128)S(1)} async-done(((f32[16,264,128]{2,1,0:T(8,128)}), f32[16,264,128]{2,1,0:T(8,128)S(1)}, u32[]{:S(2)}, u32[]{:S(2)}) %all-to-all-start.1) | async-done | bytes 2162720 | tf_op jit(solution)/shard_map/all_to_all | solution.py:886
  188.0 1.3 copy-done.3
  189.3 4.9 %all-to-all-start.3 = ((f32[16,384,128]{2,1,0:T(8,128)}), f32[16,384,128]{2,1,0:T(8,128)S(1)}, u32[]{:S(2)}, u32[]{:S(2)}) async-start(f32[16,384,128]{2,1,0:T(8,128)} %shard_map.107), calls=%async_computation.3 | async-start | bytes 6291456 | tf_op jit(solution)/shard_map/all_to_all | solution.py:899
  194.2 23.8 %shard_map.105 = (f32[40,256,128]{2,1,0:T(8,128)}, f32[8,128]{1,0:T(8,128)}) custom-call(f32[256,40,128]{2,1,0:T(8,128)} %bitcast.37, f32[16,264,128]{2,1,0:T(8,128)} %copy-done.3, f32[16,264,128]{2,1,0:T(8,128)} %copy-done.3, f32[4,128]{1,0:T(4,128)} %bitcast.49, f32[100,128]{1,0:T(8,128)} %reshape.249.coup_ref, f32[256,128]{1,0:T(8,128)} %broadcast_in_dim.30.kz_ref, ...), custom_call_target="tpu_custom_call" | custom-call | flops 3000000000 | bytes 8388608 | tf_op jit(solution)/shard_map/pallas_call | solution.py:771
  218.0 46.1 %all-to-all-done.3.b_ref.t_ref = f32[16,384,128]{2,1,0:T(8,128)S(1)} async-done(((f32[16,384,128]{2,1,0:T(8,128)}), f32[16,384,128]{2,1,0:T(8,128)S(1)}, u32[]{:S(2)}, u32[]{:S(2)}) %all-to-all-start.3) | async-done | bytes 3145760 | tf_op jit(solution)/shard_map/all_to_all | solution.py:899
  264.1 1.7 copy-done
  265.8 17.0 %shard_map.108 = f32[256,40,128]{2,1,0:T(8,128)} custom-call(f32[40,256,128]{2,1,0:T(8,128)} %get-tuple-element.36.first_ref, f32[16,384,128]{2,1,0:T(8,128)} %copy-done, f32[16,384,128]{2,1,0:T(8,128)} %copy-done, f32[8,128]{1,0:T(8,128)} %get-tuple-element.42.cf_ref, f32[100,128]{1,0:T(8,128)} %reshape.249.coup_ref, f32[256,128]{1,0:T(8,128)} %broadcast_in_dim.30.kz_ref, ...), custom_call_target="tpu_custom_call" | custom-call | flops 2000000000 | bytes 8388608 | tf_op jit(solution)/shard_map/pallas_call | solution.py:771
  (60 shorter events, 8.4 us)
Async XLA Ops:
  5.2 6.7 %copy-start.10 = (s32[8]{0:T(128)S(1)}, s32[8]{0:T(128)}, u32[]{:S(2)}) copy-start(s32[8]{0:T(128)} %param.12) | copy-start | bytes 100
  5.2 7.1 %copy-start.2 = (f32[8,64,64]{2,1,0:T(8,128)S(1)}, f32[8,64,64]{2,1,0:T(8,128)}, u32[]{:S(2)}) copy-start(f32[8,64,64]{2,1,0:T(8,128)} %param.15) | copy-start | bytes 393220
  5.2 7.6 %copy-start.8 = (f32[64,64]{1,0:T(8,128)S(1)}, f32[64,64]{1,0:T(8,128)}, u32[]{:S(2)}) copy-start(f32[64,64]{1,0:T(8,128)} %param.16) | copy-start | bytes 49156
  5.2 8.4 %copy-start.7 = (f32[25,512]{1,0:T(8,128)S(1)}, f32[25,512]{1,0:T(8,128)}, u32[]{:S(2)}) copy-start(f32[25,512]{1,0:T(8,128)} %param.14) | copy-start | bytes 153604
  5.2 76.6 %all-to-all-start = ((f32[16,384,128]{2,1,0:T(8,128)}), f32[16,384,128]{2,1,0:T(8,128)S(1)}, u32[]{:S(2)}, u32[]{:S(2)}) async-start(f32[16,384,128]{2,1,0:T(8,128)} %bitcast.38), calls=%async_computation | async-start | bytes 6291456 | tf_op jit(solution)/shard_map/all_to_all | solution.py:832
  15.1 9.4 %copy-start.6 = (f32[2,32,32]{2,1,0:T(8,128)S(1)}, f32[2,32,32]{2,1,0:T(8,128)}, u32[]{:S(2)}) copy-start(f32[2,32,32]{2,1,0:T(8,128)} %copy.20) | copy-start | bytes 24580
  26.7 4.8 %copy-start.9 = (s32[4096,2]{0,1:T(2,128)S(1)}, s32[4096,2]{0,1:T(2,128)}, u32[]{:S(2)}) copy-start(s32[4096,2]{0,1:T(2,128)} %param.11) | copy-start | bytes 98308
  26.7 7.0 %copy-start.4 = (f32[4,128,128]{2,1,0:T(8,128)S(1)}, f32[4,128,128]{2,1,0:T(8,128)}, u32[]{:S(2)}) copy-start(f32[4,128,128]{2,1,0:T(8,128)} %copy.23) | copy-start | bytes 786436
  26.7 7.0 %copy-start.5 = (f32[4,128,128]{2,1,0:T(8,128)S(1)}, f32[4,128,128]{2,1,0:T(8,128)}, u32[]{:S(2)}) copy-start(f32[4,128,128]{2,1,0:T(8,128)} %copy.22) | copy-start | bytes 786436
  81.8 4.9 %copy-start.1 = (f32[16,384,128]{2,1,0:T(8,128)}, f32[16,384,128]{2,1,0:T(8,128)S(1)}, u32[]{:S(2)}) copy-start(f32[16,384,128]{2,1,0:T(8,128)S(1)} %all-to-all-done.r_ref) | copy-start | bytes 9437188
  81.8 52.4 %all-to-all-start.2 = ((f32[16,256,128]{2,1,0:T(8,128)}), f32[16,256,128]{2,1,0:T(8,128)}, u32[]{:S(2)}, u32[]{:S(2)}) async-start(f32[16,256,128]{2,1,0:T(8,128)} %shard_map.100), calls=%async_computation.2 | async-start | bytes 4194304 | tf_op jit(solution)/shard_map/all_to_all | solution.py:846
  99.6 9.9 %collective-permute-start = (f32[17,128,128]{2,1,0:T(8,128)}, f32[17,128,128]{2,1,0:T(8,128)S(1)}, u32[]{:S(2)}, u32[]{:S(2)}) collective-permute-start(f32[17,128,128]{2,1,0:T(8,128)} %get-tuple-element.25.vw_ref.f_ref), channel_id=1, source_target_pairs={{0,1},{1,0},{2,3},{3,2},{4,5},{5,4},{6,7},{7,6},{8,9},{9,8},{10,11... | collective-permute-start | bytes 3342344 | tf_op jit(solution)/shard_map/ppermute | solution.py:872
  109.6 1.0 copy-start.11
  134.2 53.7 %all-to-all-start.1 = ((f32[16,264,128]{2,1,0:T(8,128)}), f32[16,264,128]{2,1,0:T(8,128)S(1)}, u32[]{:S(2)}, u32[]{:S(2)}) async-start(f32[16,264,128]{2,1,0:T(8,128)} %shard_map.104), calls=%async_computation.1 | async-start | bytes 4325376 | tf_op jit(solution)/shard_map/all_to_all | solution.py:886
  139.2 13.4 %copy-start.12 = (f32[17,64,128]{2,1,0:T(8,128)S(1)}, f32[17,64,128]{2,1,0:T(8,128)}, u32[]{:S(2)}) copy-start(f32[17,64,128]{2,1,0:T(8,128)} %get-tuple-element.40.refs_0_) | copy-start | bytes 1671172
  152.2 3.1 %collective-permute-start.1 = (f32[17,128,128]{2,1,0:T(8,128)}, f32[17,128,128]{2,1,0:T(8,128)}, u32[]{:S(2)}, u32[]{:S(2)}) collective-permute-start(f32[17,128,128]{2,1,0:T(8,128)} %get-tuple-element.38.f_ref), channel_id=1, source_target_pairs={{0,1},{1,0},{2,3},{3,2},{4,5},{5,4},{6,7},{7,6},{8,9},{9,8},{10,11... | collective-permute-start | bytes 3342344 | tf_op jit(solution)/shard_map/ppermute | solution.py:890
  152.6 3.2 %collective-permute-start.2 = (f32[17,64,128]{2,1,0:T(8,128)S(1)}, f32[17,64,128]{2,1,0:T(8,128)S(1)}, u32[]{:S(2)}, u32[]{:S(2)}) collective-permute-start(f32[17,64,128]{2,1,0:T(8,128)S(1)} %copy-done.12), channel_id=1, source_target_pairs={{0,1},{1,0},{2,3},{3,2},{4,5},{5,4},{6,7},{7,6},{8,9},{9,8},{10,11... | collective-permute-start | bytes 1671176 | tf_op jit(solution)/shard_map/ppermute | solution.py:877
  155.8 0.8 copy-start.13
  188.0 1.3 copy-start.3
  189.3 74.8 %all-to-all-start.3 = ((f32[16,384,128]{2,1,0:T(8,128)}), f32[16,384,128]{2,1,0:T(8,128)S(1)}, u32[]{:S(2)}, u32[]{:S(2)}) async-start(f32[16,384,128]{2,1,0:T(8,128)} %shard_map.107), calls=%async_computation.3 | async-start | bytes 6291456 | tf_op jit(solution)/shard_map/all_to_all | solution.py:899
  264.1 1.7 copy-start

commit v4 on v3

--- a/solution.py
+++ b/solution.py
@@ -186,9 +186,11 @@
 BLOCKS = LANES // SHARE
 STRIPES = 4
 PARTS = 10
-TILE = 32
+TILE = 64
 PACK_TILE = 64
+FIRST_TILE = 32
 MIB = 1024 * 1024
+LAST_LIMIT = 53
 
 
 def roll(x, shift):
@@ -285,16 +287,39 @@
     return out
 
 
-def pack_first(near_ref, far_ref, near_last_ref, far_last_ref, o_ref):
-    low, even = lane_masks((PACK_TILE, LANES))
-    pieces = (
-        (near_ref, 0, near_ref, 2 * STRIPES),
-        (far_ref, 0, far_ref, 2 * STRIPES),
-        (near_last_ref, 0, far_last_ref, 0),
-    )
-    for place, piece in enumerate(pieces):
-        for group, value in enumerate(pack_pair(*piece, low, even)):
-            o_ref[group, place] = value
+def pack_first(rows_ref, o_ref, in_ref, out_ref, in_sem, out_sem):
+    tiles = in_ref.shape[0]
+    count = in_ref.shape[1]
+    wanted = pl.ds(2 * 2 * STRIPES, 3 * 2 * STRIPES)
+    low, even = lane_masks((count, LANES))
+    loads = []
+    for tile in range(tiles):
+        source = rows_ref.at[pl.ds(tile * count, count), wanted, :]
+        loads.append(pltpu.make_async_copy(source, in_ref.at[tile], in_sem.at[tile]))
+    half = tiles // 2
+    for tile in range(half):
+        loads[tile].start()
+        loads[tile + half].start()
+    stores = []
+    for tile in range(half):
+        loads[tile].wait()
+        loads[tile + half].wait()
+        near = in_ref.at[tile]
+        far = in_ref.at[tile + half]
+        pieces = (
+            (near, 0, near, 2 * STRIPES),
+            (far, 0, far, 2 * STRIPES),
+            (near, 4 * STRIPES, far, 4 * STRIPES),
+        )
+        for place, piece in enumerate(pieces):
+            for group, value in enumerate(pack_pair(*piece, low, even)):
+                out_ref[tile, place, group] = value
+            target = o_ref.at[:, pl.ds((place * half + tile) * count, count), :]
+            store = pltpu.make_async_copy(out_ref.at[tile, place], target, out_sem.at[tile, place])
+            store.start()
+            stores.append(store)
+    for store in stores:
+        store.wait()
 
 
 def pack_second(near_ref, o_ref):
@@ -612,7 +637,7 @@
     return three_pass(high, low_rows, sw_ref[stripe]).reshape(PARTS, TILE, LANES)
 
 
-def relax_first(a_ref, b_ref, mean_ref, base_ref, coup_ref, kz_ref, om_ref, sw_ref, out_ref, cf_ref, right_ref, x_ref, *halves):
+def relax_first(a_ref, b_ref, mean_ref, base_ref, coup_ref, kz_ref, om_ref, sw_ref, out_ref, right_ref, x_ref, cf_ref, *halves):
     rh_ref, rl_ref, zh_ref, zl_ref = halves
     low, even = lane_masks((TILE, LANES))
     block_of = lane_index((1, LANES)) // SHARE
@@ -622,6 +647,7 @@
             row = mean_ref[stripe * BLOCKS + block, pl.ds(0, 1), :]
             total = total + jnp.where(block_of == block, roll(row, SHARE * (block - 1)), 0.0)
         cf_ref[pl.ds(stripe, 1), :] = total
+    out_ref[0, STRIPES * PARTS, pl.ds(0, 8), :] = cf_ref[...]
 
     for stripe in range(STRIPES):
         groups = [stripe * BLOCKS + block for block in range(BLOCKS)]
@@ -641,22 +667,87 @@
         return x_ref[stripe * PARTS + part]
 
     for sweep in range(SWEEPS):
-        target = x_ref if sweep < SWEEPS - 1 else out_ref
         find_rims(x_of, range(PARTS), zh_ref, zl_ref)
         for stripe in range(STRIPES):
             here = pl.ds(stripe * PARTS, PARTS)
             cross = cf_ref[pl.ds(stripe, 1), :]
             new = relax(stripe, x_of, range(PARTS), cross, kz_ref, om_ref, coup_ref, sw_ref, *halves)
-            target[here] = right_ref[here] + new
+            if sweep < SWEEPS - 1:
+                x_ref[here] = right_ref[here] + new
+            else:
+                out_ref[0, here] = right_ref[here] + new
 
 
 LATE = (0, 1, 2, 3, 8, 9)
 
 
-def relax_last(first_ref, b_ref, t_ref, cf_ref, coup_ref, kz_ref, om_ref, sw_ref, o_ref, right_ref, x_ref, *halves):
+def relax_last(first_hbm, b_any, *refs):
+    shared_hbm, o_hbm, (first_buf, b_buf, t_buf, o_buf), shared = refs[:4], refs[4], refs[5:9], refs[9:13]
+    (in_sem, out_sem, shared_sem), scratch = refs[13:16], refs[16:]
+    coup_ref, kz_ref, om_ref, sw_ref = shared
+    tiles = first_buf.shape[0]
+    modes = tiles * TILE
+
+    def loads(i):
+        pair = b_any.at[:, pl.ds(i * TILE, TILE), :]
+        last = b_any.at[:, pl.ds(modes + i % (tiles // 2) * TILE, TILE), :]
+        return (
+            pltpu.make_async_copy(pair, b_buf.at[i], in_sem.at[0, i]),
+            pltpu.make_async_copy(last, t_buf.at[i], in_sem.at[1, i]),
+            pltpu.make_async_copy(first_hbm.at[i], first_buf.at[i], in_sem.at[2, i]),
+        )
+
+    def store(i):
+        target = o_hbm.at[pl.ds(i * TILE, TILE), :, :]
+        return pltpu.make_async_copy(o_buf.at[i], target, out_sem.at[i])
+
+    ahead = 2
+    fixed_loads = [
+        pltpu.make_async_copy(source, target, shared_sem.at[place])
+        for place, (source, target) in enumerate(zip(shared_hbm, shared))
+    ]
+    for load in fixed_loads:
+        load.start()
+    for i in range(ahead):
+        for load in loads(i):
+            load.start()
+    for load in fixed_loads:
+        load.wait()
+
+    def body(i, carry):
+        for load in loads(i):
+            load.wait()
+
+        @pl.when(i + ahead < tiles)
+        def _():
+            for load in loads(i + ahead):
+                load.start()
+
+        modes_here = pl.ds(pl.multiple_of(i * TILE, TILE), TILE)
+        relax_tile(
+            i >= tiles // 2,
+            first_buf.at[i],
+            b_buf.at[i],
+            t_buf.at[i],
+            first_buf.at[i, STRIPES * PARTS],
+            coup_ref,
+            kz_ref.at[modes_here, :],
+            om_ref.at[modes_here, :],
+            sw_ref,
+            o_buf.at[i],
+            *scratch,
+        )
+        store(i).start()
+        return carry
+
+    lax.fori_loop(0, tiles, body, 0)
+    for i in range(tiles):
+        store(i).wait()
+
+
+def relax_tile(far, first_ref, b_ref, t_ref, cf_ref, coup_ref, kz_ref, om_ref, sw_ref, o_ref, right_ref, x_ref, *halves):
     rh_ref, rl_ref, zh_ref, zl_ref = halves
     low, even = lane_masks((TILE, LANES))
-    far = pl.program_id(0) >= pl.num_programs(0) // 2
     count = len(LATE)
     for stripe in range(STRIPES):
         groups = [stripe * BLOCKS + block for block in range(BLOCKS)]
@@ -815,21 +906,28 @@
     frequency = jnp.broadcast_to(frequency[:, None], (modes, LANES))
     couple = base_coupling.reshape(25 * STRIPES, LANES)
 
+    in_hbm = pl.BlockSpec(memory_space=pltpu.HBM)
+    anywhere = pl.BlockSpec(memory_space=pl.ANY)
+
     def variables(count, place, shift):
         return pl.BlockSpec((PACK_TILE, count * 2 * STRIPES, LANES), lambda i: (i + shift, place, 0))
 
-    half = modes // PACK_TILE // 2
+    packs = modes // FIRST_TILE
     (sent_first,) = call(
         pack_first,
-        [rows] * 4,
-        [(groups, 3, modes // 2, LANES)],
-        [],
+        [rows],
+        [(groups, first_rows, LANES)],
+        [
+            vmem(packs, FIRST_TILE, 3 * 2 * STRIPES, LANES),
+            vmem(packs // 2, 3, groups, FIRST_TILE, LANES),
+            pltpu.SemaphoreType.DMA((packs,)),
+            pltpu.SemaphoreType.DMA((packs // 2, 3)),
+        ],
         cost=10**8,
-        grid=(half,),
-        in_specs=[variables(2, 1, 0), variables(2, 1, half), variables(1, 4, 0), variables(1, 4, half)],
-        out_specs=[pl.BlockSpec((groups, 3, PACK_TILE, LANES), lambda i: (0, 0, i, 0))],
-    )
-    first = exchange(sent_first.reshape(groups, first_rows, LANES))
+        in_specs=[in_hbm],
+        out_specs=[in_hbm],
+    )
+    first = exchange(sent_first)
     (sent_second,) = call(
         pack_second,
         [rows],
@@ -899,35 +997,49 @@
     got_second = exchange(back_second)
 
     stacked = TILE * PARTS
-    state = (STRIPES * PARTS, modes, LANES)
-    state_spec = pl.BlockSpec((STRIPES * PARTS, TILE, LANES), lambda i: (0, i, 0))
+    state = (tiles, STRIPES * PARTS + 1, TILE, LANES)
+    state_spec = pl.BlockSpec((1,) + state[1:], lambda i: (i, 0, 0, 0))
     returned_spec = pl.BlockSpec((groups, TILE, LANES), lambda i: (0, i, 0))
-    last_spec = pl.BlockSpec((groups, TILE, LANES), lambda i: (0, tiles + i % (tiles // 2), 0))
     mean_spec = pl.BlockSpec((groups, 8, LANES), lambda i: (0, modes // 8, 0))
     mode_spec = pl.BlockSpec((TILE, LANES), lambda i: (i, 0))
     all_spec = pl.BlockSpec((TILE, stride, LANES), lambda i: (i, 0, 0))
     halves = [vmem(STRIPES, stacked, LANES, dtype=jnp.bfloat16)] * 2 + [vmem(stacked, LANES, dtype=jnp.bfloat16)] * 2
     shared_specs = [fixed(*couple.shape), mode_spec, mode_spec, fixed(*solve.shape)]
     shared = [couple, wave, frequency, solve]
-    iterate, cross = call(
+    (iterate,) = call(
         relax_first,
         [rows, got_first, got_first, base_flow.reshape(STRIPES, LANES)] + shared,
-        [state, (8, LANES)],
-        [vmem(STRIPES * PARTS, TILE, LANES)] * 2 + halves,
+        [state],
+        [vmem(STRIPES * PARTS, TILE, LANES)] * 2 + [vmem(8, LANES)] + halves,
         cost=3 * 10**9,
         grid=(tiles,),
         in_specs=[all_spec, returned_spec, mean_spec, fixed(STRIPES, LANES)] + shared_specs,
-        out_specs=[state_spec, fixed(8, LANES)],
+        out_specs=[state_spec],
     )
     (out,) = call(
         relax_last,
-        [iterate, got_second, got_second, cross] + shared,
+        [iterate, got_second] + shared,
         [(modes, stride, LANES)],
-        [vmem(STRIPES, len(LATE), TILE, LANES), vmem(STRIPES * PARTS, TILE, LANES)] + halves,
+        [
+            vmem(*state),
+            vmem(tiles, groups, TILE, LANES),
+            vmem(tiles, groups, TILE, LANES),
+            vmem(tiles, TILE, stride, LANES),
+            vmem(*couple.shape),
+            vmem(*wave.shape),
+            vmem(*frequency.shape),
+            vmem(*solve.shape, dtype=jnp.bfloat16),
+            pltpu.SemaphoreType.DMA((3, tiles)),
+            pltpu.SemaphoreType.DMA((tiles,)),
+            pltpu.SemaphoreType.DMA((4,)),
+            vmem(STRIPES, len(LATE), TILE, LANES),
+            vmem(STRIPES * PARTS, TILE, LANES),
+        ]
+        + halves,
         cost=2 * 10**9,
-        grid=(tiles,),
-        in_specs=[state_spec, returned_spec, last_spec, fixed(8, LANES)] + shared_specs,
-        out_specs=[all_spec],
+        limit=LAST_LIMIT,
+        in_specs=[in_hbm, anywhere] + [in_hbm] * 4,
+        out_specs=[in_hbm],
     )
     out = out.reshape(modes, 5, STRIPES, 2, LANES).transpose(0, 1, 3, 2, 4).reshape(modes, 5, 2, points)
     return out.transpose(0, 2, 1, 3)

time: 284 us -> 282 us (level)
  Pallas kernels: 120 us -> 117 us
where the time goes in v4:
time: 282 us; the launch traced here: 281 us
  waiting for transfers between devices  118 us (42%)
  Pallas kernels  117 us (41%)
  starting transfers between devices  22.3 us (8%)
  local copies, waits for them, and re-layouts  18.2 us (6%)
  other arithmetic  4.5 us (2%)
    pallas_call x9, Pallas kernels, call(): pl.pallas_call(kernel, out_shape=[jax.ShapeDtypeStruct(shape, jnp.float32...  117 us
    all_to_all x1, waiting for transfers between devices, local_halves(): got_second = exchange(back_second)  47.7 us
    all_to_all x1, waiting for transfers between devices, local_halves(): first = exchange(sent_first)  45.5 us
    all_to_all x1, waiting for transfers between devices, local_halves(): second = exchange(sent_second)  11.7 us
    all_to_all x1, waiting for transfers between devices, local_halves(): got_first = exchange(back_first)  10.1 us
    all_to_all x1, starting transfers between devices, local_halves(): first = exchange(sent_first)  6.7 us
  transfers between devices with their start and end apart: 7, of which 6 were waited for; matrix products, arithmetic and copies ran while one was open for 7% of the time, Pallas kernels for 34%

profile of v4, /device:TPU:13, one launch (start us, length us, event | category | flops | bytes accessed | tf_op | source)
XLA Modules:
  0.0 280.8 jit_solution(15041644369016125242)
XLA Ops:
  0.0 5.4 %shard_map.101 = f32[16,384,128]{2,1,0:T(8,128)} custom-call(f32[256,40,128]{2,1,0:T(8,128)} %bitcast.31), custom_call_target="tpu_custom_call" | custom-call | flops 100000000 | bytes 8388608 | tf_op jit(solution)/shard_map/pallas_call | solution.py:862
  5.5 6.7 %all-to-all-start = ((f32[16,384,128]{2,1,0:T(8,128)}), f32[16,384,128]{2,1,0:T(8,128)S(1)}, u32[]{:S(2)}, u32[]{:S(2)}) async-start(f32[16,384,128]{2,1,0:T(8,128)} %shard_map.101), calls=%async_computation | async-start | bytes 6291456 | tf_op jit(solution)/shard_map/all_to_all | solution.py:930
  14.6 0.8 mul.162
  16.2 1.8 copy.23
  18.8 1.8 copy.22
  20.6 0.8 copy.21
  21.4 1.9 mul.165
  23.4 1.3 mul.166
  24.7 0.9 broadcast_multiply_fusion
  25.7 1.3 mul.160
  27.0 4.8 %shard_map.100 = f32[16,256,128]{2,1,0:T(8,128)} custom-call(f32[256,40,128]{2,1,0:T(8,128)} %bitcast.32), custom_call_target="tpu_custom_call" | custom-call | flops 100000000 | bytes 8388608 | tf_op jit(solution)/shard_map/pallas_call | solution.py:862
  33.1 0.9 broadcast_multiply_fusion.1
  34.2 0.8 pad_maximum_fusion.1.sw_ref.refs_3_
  35.0 0.8 broadcast_in_dim.55.om_ref.refs_2_
  36.5 45.5 %all-to-all-done.r_ref = f32[16,384,128]{2,1,0:T(8,128)S(1)} async-done(((f32[16,384,128]{2,1,0:T(8,128)}), f32[16,384,128]{2,1,0:T(8,128)S(1)}, u32[]{:S(2)}, u32[]{:S(2)}) %all-to-all-start) | async-done | bytes 3145760 | tf_op jit(solution)/shard_map/all_to_all | solution.py:930
  82.0 4.9 %all-to-all-start.2 = ((f32[16,256,128]{2,1,0:T(8,128)}), f32[16,256,128]{2,1,0:T(8,128)}, u32[]{:S(2)}, u32[]{:S(2)}) async-start(f32[16,256,128]{2,1,0:T(8,128)} %shard_map.100), calls=%async_computation.2 | async-start | bytes 4194304 | tf_op jit(solution)/shard_map/all_to_all | solution.py:944
  87.0 12.9 %shard_map.102 = (f32[17,128,128]{2,1,0:T(8,128)}, f32[17,128,128]{2,1,0:T(8,128)}, f32[8,128]{1,0:T(8,128)}) custom-call(s32[4096]{0:T(1024)} %bitcast.37, f32[16,384,128]{2,1,0:T(8,128)} %copy-done.5, bf16[512,256]{1,0:T(8,128)(2,1)} %constant.125.clone.w_ref, f32[32,8,128]{2,1,0:T(8,128)} %constant.127.clone.tab_ref), custom_call_target="tpu_custom_call" | custom-call | flops 2000000000 | bytes 8388608 | tf_op jit(solution)/shard_map/pallas_call | solution.py:862
  100.2 9.6 %shard_map.103 = (f32[17,64,128]{2,1,0:T(8,128)}, f32[17,64,128]{2,1,0:T(8,128)}) custom-call(s32[4096]{0:T(1024)} %bitcast.38, f32[16,384,128]{2,1,0:T(8,128)} %copy-done.5, bf16[512,256]{1,0:T(8,128)(2,1)} %constant.125.clone.w_ref, f32[32,8,128]{2,1,0:T(8,128)} %constant.127.clone.tab_ref), custom_call_target="tpu_custom_call" | custom-call | flops 1000000000 | bytes 8388608 | tf_op jit(solution)/shard_map/pallas_call | solution.py:862
  109.8 1.0 copy-done.14
  110.8 11.9 %shard_map.104 = f32[16,264,128]{2,1,0:T(8,128)} custom-call(s32[4096]{0:T(1024)} %bitcast.39, f32[17,128,128]{2,1,0:T(8,128)} %get-tuple-element.23.vw_ref.f_ref, f32[17,128,128]{2,1,0:T(8,128)} %get-tuple-element.23.vw_ref.f_ref, f32[17,128,128]{2,1,0:T(8,128)} %copy-done.14, f32[17,128,128]{2,1,0:T(8,128)} %get-tuple-element.27.g_ref, ...), custom_call_target="tpu_custom_call" | custom-call | flops 2000000000 | bytes 8388608 | tf_op jit(solution)/shard_map/pallas_call | solution.py:862
  122.8 11.7 %all-to-all-done.2.r_ref = f32[16,256,128]{2,1,0:T(8,128)} async-done(((f32[16,256,128]{2,1,0:T(8,128)}), f32[16,256,128]{2,1,0:T(8,128)}, u32[]{:S(2)}, u32[]{:S(2)}) %all-to-all-start.2) | async-done | bytes 2097184 | tf_op jit(solution)/shard_map/all_to_all | solution.py:944
  134.5 4.9 %all-to-all-start.1 = ((f32[16,264,128]{2,1,0:T(8,128)}), f32[16,264,128]{2,1,0:T(8,128)S(1)}, u32[]{:S(2)}, u32[]{:S(2)}) async-start(f32[16,264,128]{2,1,0:T(8,128)} %shard_map.104), calls=%async_computation.1 | async-start | bytes 4325376 | tf_op jit(solution)/shard_map/all_to_all | solution.py:984
  139.4 13.1 %shard_map.106 = (f32[17,128,128]{2,1,0:T(8,128)}, f32[17,128,128]{2,1,0:T(8,128)}) custom-call(s32[4096]{0:T(1024)} %bitcast.40, f32[16,256,128]{2,1,0:T(8,128)} %all-to-all-done.2.r_ref, bf16[512,256]{1,0:T(8,128)(2,1)} %constant.125.clone.w_ref, f32[32,8,128]{2,1,0:T(8,128)} %constant.127.clone.tab_ref), custom_call_target="tpu_custom_call" | custom-call | flops 2000000000 | bytes 8388608 | tf_op jit(solution)/shard_map/pallas_call | solution.py:862
  153.0 2.7 collective-permute-done.1.s_ref
  156.0 0.8 copy-done.16
  156.8 21.3 %shard_map.107 = f32[16,384,128]{2,1,0:T(8,128)} custom-call(s32[4096]{0:T(1024)} %bitcast.41, f32[17,128,128]{2,1,0:T(8,128)} %get-tuple-element.23.vw_ref.f_ref, f32[17,128,128]{2,1,0:T(8,128)} %get-tuple-element.35.f_ref, f32[17,128,128]{2,1,0:T(8,128)} %collective-permute-done.1.s_ref, f32[17,128,128]{2,1,0:T(8,128)} %get-tuple-element.36.g_ref, ...), custom_call_target="tpu_custom_call" | custom-call | flops 3000000000 | bytes 8388608 | tf_op jit(solution)/shard_map/pallas_call | solution.py:862
  178.1 10.1 %all-to-all-done.1.b_ref.mean_ref = f32[16,264,128]{2,1,0:T(8,128)S(1)} async-done(((f32[16,264,128]{2,1,0:T(8,128)}), f32[16,264,128]{2,1,0:T(8,128)S(1)}, u32[]{:S(2)}, u32[]{:S(2)}) %all-to-all-start.1) | async-done | bytes 2162720 | tf_op jit(solution)/shard_map/all_to_all | solution.py:984
  188.2 1.4 copy-done.4
  189.6 4.9 %all-to-all-start.3 = ((f32[16,384,128]{2,1,0:T(8,128)}), f32[16,384,128]{2,1,0:T(8,128)}, u32[]{:S(2)}, u32[]{:S(2)}) async-start(f32[16,384,128]{2,1,0:T(8,128)} %shard_map.107), calls=%async_computation.3 | async-start | bytes 6291456 | tf_op jit(solution)/shard_map/all_to_all | solution.py:997
  194.6 22.3 %shard_map.105.first_hbm = f32[4,41,64,128]{3,2,1,0:T(8,128)} custom-call(f32[256,40,128]{2,1,0:T(8,128)} %bitcast.33, f32[16,264,128]{2,1,0:T(8,128)} %copy-done.4, f32[16,264,128]{2,1,0:T(8,128)} %copy-done.4, f32[4,128]{1,0:T(4,128)} %bitcast.44, f32[100,128]{1,0:T(8,128)} %reshape.246.coup_ref.refs_0_, f32[256,128]{1,0:T(8,128)} %broadcast_in_dim.30.kz_ref.refs_1_, ...), custom_call_target="tpu_custom_call" | custom-call | flops 3000000000 | bytes 8388608 | tf_op jit(solution)/shard_map/pallas_call | solution.py:862
  216.8 47.7 %all-to-all-done.3.b_any = f32[16,384,128]{2,1,0:T(8,128)} async-done(((f32[16,384,128]{2,1,0:T(8,128)}), f32[16,384,128]{2,1,0:T(8,128)}, u32[]{:S(2)}, u32[]{:S(2)}) %all-to-all-start.3) | async-done | bytes 3145760 | tf_op jit(solution)/shard_map/all_to_all | solution.py:997
  264.5 16.1 %shard_map.108 = f32[256,40,128]{2,1,0:T(8,128)} custom-call(f32[4,41,64,128]{3,2,1,0:T(8,128)} %shard_map.105.first_hbm, f32[16,384,128]{2,1,0:T(8,128)} %all-to-all-done.3.b_any, f32[100,128]{1,0:T(8,128)S(1)} %copy-done.3, f32[256,128]{1,0:T(8,128)S(1)} %copy-done.2, f32[256,128]{1,0:T(8,128)S(1)} %copy-done.1, bf16[4,256,256]{2,1,0:T(8,128)(2,1)S(1)} %copy-done), custom_call_target="tpu_custom_call" | custom-call | flops 2000000000 | bytes 8388608 | tf_op jit(solution)/shard_map/pallas_call | solution.py:862
  (66 shorter events, 7.6 us)
Async XLA Ops:
  5.4 6.7 %copy-start.13 = (s32[8]{0:T(128)S(1)}, s32[8]{0:T(128)}, u32[]{:S(2)}) copy-start(s32[8]{0:T(128)} %param.12) | copy-start | bytes 100
  5.4 7.2 %copy-start.6 = (f32[8,64,64]{2,1,0:T(8,128)S(1)}, f32[8,64,64]{2,1,0:T(8,128)}, u32[]{:S(2)}) copy-start(f32[8,64,64]{2,1,0:T(8,128)} %param.15) | copy-start | bytes 393220
  5.4 7.6 %copy-start.11 = (f32[64,64]{1,0:T(8,128)S(1)}, f32[64,64]{1,0:T(8,128)}, u32[]{:S(2)}) copy-start(f32[64,64]{1,0:T(8,128)} %param.16) | copy-start | bytes 49156
  5.4 8.4 %copy-start.10 = (f32[25,512]{1,0:T(8,128)S(1)}, f32[25,512]{1,0:T(8,128)}, u32[]{:S(2)}) copy-start(f32[25,512]{1,0:T(8,128)} %param.14) | copy-start | bytes 153604
  5.5 76.6 %all-to-all-start = ((f32[16,384,128]{2,1,0:T(8,128)}), f32[16,384,128]{2,1,0:T(8,128)S(1)}, u32[]{:S(2)}, u32[]{:S(2)}) async-start(f32[16,384,128]{2,1,0:T(8,128)} %shard_map.101), calls=%async_computation | async-start | bytes 6291456 | tf_op jit(solution)/shard_map/all_to_all | solution.py:930
  15.3 9.4 %copy-start.9 = (f32[2,32,32]{2,1,0:T(8,128)S(1)}, f32[2,32,32]{2,1,0:T(8,128)}, u32[]{:S(2)}) copy-start(f32[2,32,32]{2,1,0:T(8,128)} %copy.20) | copy-start | bytes 24580
  27.0 4.8 %copy-start.12 = (s32[4096,2]{0,1:T(2,128)S(1)}, s32[4096,2]{0,1:T(2,128)}, u32[]{:S(2)}) copy-start(s32[4096,2]{0,1:T(2,128)} %param.11) | copy-start | bytes 98308
  27.0 7.0 %copy-start.7 = (f32[4,128,128]{2,1,0:T(8,128)S(1)}, f32[4,128,128]{2,1,0:T(8,128)}, u32[]{:S(2)}) copy-start(f32[4,128,128]{2,1,0:T(8,128)} %copy.23) | copy-start | bytes 786436
  27.0 7.0 %copy-start.8 = (f32[4,128,128]{2,1,0:T(8,128)S(1)}, f32[4,128,128]{2,1,0:T(8,128)}, u32[]{:S(2)}) copy-start(f32[4,128,128]{2,1,0:T(8,128)} %copy.22) | copy-start | bytes 786436
  82.0 4.9 %copy-start.5 = (f32[16,384,128]{2,1,0:T(8,128)}, f32[16,384,128]{2,1,0:T(8,128)S(1)}, u32[]{:S(2)}) copy-start(f32[16,384,128]{2,1,0:T(8,128)S(1)} %all-to-all-done.r_ref) | copy-start | bytes 9437188
  82.0 52.4 %all-to-all-start.2 = ((f32[16,256,128]{2,1,0:T(8,128)}), f32[16,256,128]{2,1,0:T(8,128)}, u32[]{:S(2)}, u32[]{:S(2)}) async-start(f32[16,256,128]{2,1,0:T(8,128)} %shard_map.100), calls=%async_computation.2 | async-start | bytes 4194304 | tf_op jit(solution)/shard_map/all_to_all | solution.py:944
  99.9 9.9 %collective-permute-start = (f32[17,128,128]{2,1,0:T(8,128)}, f32[17,128,128]{2,1,0:T(8,128)S(1)}, u32[]{:S(2)}, u32[]{:S(2)}) collective-permute-start(f32[17,128,128]{2,1,0:T(8,128)} %get-tuple-element.23.vw_ref.f_ref), channel_id=1, source_target_pairs={{0,1},{1,0},{2,3},{3,2},{4,5},{5,4},{6,7},{7,6},{8,9},{9,8},{10,11... | collective-permute-start | bytes 3342344 | tf_op jit(solution)/shard_map/ppermute | solution.py:970
  109.8 1.0 copy-start.14
  134.5 53.7 %all-to-all-start.1 = ((f32[16,264,128]{2,1,0:T(8,128)}), f32[16,264,128]{2,1,0:T(8,128)S(1)}, u32[]{:S(2)}, u32[]{:S(2)}) async-start(f32[16,264,128]{2,1,0:T(8,128)} %shard_map.104), calls=%async_computation.1 | async-start | bytes 4325376 | tf_op jit(solution)/shard_map/all_to_all | solution.py:984
  139.4 13.5 %copy-start.15 = (f32[17,64,128]{2,1,0:T(8,128)S(1)}, f32[17,64,128]{2,1,0:T(8,128)}, u32[]{:S(2)}) copy-start(f32[17,64,128]{2,1,0:T(8,128)} %get-tuple-element.37.refs_0_) | copy-start | bytes 1671172
  152.5 3.2 %collective-permute-start.1 = (f32[17,128,128]{2,1,0:T(8,128)}, f32[17,128,128]{2,1,0:T(8,128)}, u32[]{:S(2)}, u32[]{:S(2)}) collective-permute-start(f32[17,128,128]{2,1,0:T(8,128)} %get-tuple-element.35.f_ref), channel_id=1, source_target_pairs={{0,1},{1,0},{2,3},{3,2},{4,5},{5,4},{6,7},{7,6},{8,9},{9,8},{10,11... | collective-permute-start | bytes 3342344 | tf_op jit(solution)/shard_map/ppermute | solution.py:988
  152.8 3.2 %collective-permute-start.2 = (f32[17,64,128]{2,1,0:T(8,128)S(1)}, f32[17,64,128]{2,1,0:T(8,128)S(1)}, u32[]{:S(2)}, u32[]{:S(2)}) collective-permute-start(f32[17,64,128]{2,1,0:T(8,128)S(1)} %copy-done.15), channel_id=1, source_target_pairs={{0,1},{1,0},{2,3},{3,2},{4,5},{5,4},{6,7},{7,6},{8,9},{9,8},{10,11... | collective-permute-start | bytes 1671176 | tf_op jit(solution)/shard_map/ppermute | solution.py:975
  156.0 0.8 copy-start.16
  188.2 1.4 copy-start.4
  189.6 74.9 %all-to-all-start.3 = ((f32[16,384,128]{2,1,0:T(8,128)}), f32[16,384,128]{2,1,0:T(8,128)}, u32[]{:S(2)}, u32[]{:S(2)}) async-start(f32[16,384,128]{2,1,0:T(8,128)} %shard_map.107), calls=%async_computation.3 | async-start | bytes 6291456 | tf_op jit(solution)/shard_map/all_to_all | solution.py:997
  194.5 70.0 %copy-start = (bf16[4,256,256]{2,1,0:T(8,128)(2,1)S(1)}, bf16[4,256,256]{2,1,0:T(8,128)(2,1)}, u32[]{:S(2)}) copy-start(bf16[4,256,256]{2,1,0:T(8,128)(2,1)} %pad_maximum_fusion.1.sw_ref.refs_3_) | copy-start | bytes 1572868
  194.5 70.0 %copy-start.1 = (f32[256,128]{1,0:T(8,128)S(1)}, f32[256,128]{1,0:T(8,128)}, u32[]{:S(2)}) copy-start(f32[256,128]{1,0:T(8,128)} %broadcast_in_dim.55.om_ref.refs_2_) | copy-start | bytes 393220
  194.5 70.0 %copy-start.2 = (f32[256,128]{1,0:T(8,128)S(1)}, f32[256,128]{1,0:T(8,128)}, u32[]{:S(2)}) copy-start(f32[256,128]{1,0:T(8,128)} %broadcast_in_dim.30.kz_ref.refs_1_) | copy-start | bytes 393220
  194.6 70.0 %copy-start.3 = (f32[100,128]{1,0:T(8,128)S(1)}, f32[100,128]{1,0:T(8,128)}, u32[]{:S(2)}) copy-start(f32[100,128]{1,0:T(8,128)} %reshape.246.coup_ref.refs_0_) | copy-start | bytes 153604

commit v5 on v4

--- a/solution.py
+++ b/solution.py
@@ -187,10 +187,9 @@
 STRIPES = 4
 PARTS = 10
 TILE = 64
-PACK_TILE = 64
-FIRST_TILE = 32
+PACK_TILE = 32
 MIB = 1024 * 1024
-LAST_LIMIT = 53
+VMEM_LIMIT = 53
 
 
 def roll(x, shift):
@@ -287,10 +286,10 @@
     return out
 
 
-def pack_first(rows_ref, o_ref, in_ref, out_ref, in_sem, out_sem):
+def pack(first, with_last, rows_ref, o_ref, in_ref, out_ref, in_sem, out_sem):
     tiles = in_ref.shape[0]
     count = in_ref.shape[1]
-    wanted = pl.ds(2 * 2 * STRIPES, 3 * 2 * STRIPES)
+    wanted = pl.ds(first * 2 * STRIPES, in_ref.shape[2])
     low, even = lane_masks((count, LANES))
     loads = []
     for tile in range(tiles):
@@ -306,11 +305,9 @@
         loads[tile + half].wait()
         near = in_ref.at[tile]
         far = in_ref.at[tile + half]
-        pieces = (
-            (near, 0, near, 2 * STRIPES),
-            (far, 0, far, 2 * STRIPES),
-            (near, 4 * STRIPES, far, 4 * STRIPES),
-        )
+        pieces = [(near, 0, near, 2 * STRIPES), (far, 0, far, 2 * STRIPES)]
+        if with_last:
+            pieces.append((near, 8 * STRIPES, far, 8 * STRIPES))
         for place, piece in enumerate(pieces):
             for group, value in enumerate(pack_pair(*piece, low, even)):
                 out_ref[tile, place, group] = value
@@ -320,12 +317,6 @@
             stores.append(store)
     for store in stores:
         store.wait()
-
-
-def pack_second(near_ref, o_ref):
-    low, even = lane_masks((PACK_TILE, LANES))
-    for group, value in enumerate(pack_pair(near_ref, 0, near_ref, 2 * STRIPES, low, even)):
-        o_ref[group] = value
 
 
 ROWS = 128
@@ -595,17 +586,18 @@
 
 def find_rims(x_of, parts, zh_ref, zl_ref):
     lane = lane_index((TILE, LANES))
-    edge = ((lane & 63) == 0) | ((lane & 63) == 63)
+    edges = []
+    for stripe in range(STRIPES):
+        place = (lane - 2 * stripe) & (SLAB - 1)
+        edges.append((place == 0) | (place == SLAB - 1))
     for part in range(PARTS):
         rows = pl.ds(part * TILE, TILE)
         if part not in parts:
             zh_ref[rows, :] = zl_ref[rows, :] = jnp.zeros((TILE, LANES), jnp.bfloat16)
             continue
-        rims = None
-        for stripe in range(STRIPES):
-            term = jnp.where(edge, x_of(stripe, part), 0.0)
-            term = roll(term, 2 * stripe) if stripe else term
-            rims = term if rims is None else rims + term
+        rims = x_of(0, part)
+        for stripe in range(1, STRIPES):
+            rims = jnp.where(edges[stripe], roll(x_of(stripe, part), 2 * stripe), rims)
         zh_ref[rows, :], zl_ref[rows, :] = split(rims)
 
 
@@ -852,7 +844,7 @@
     return jnp.concatenate(split_device(jnp.concatenate([blocks, rims], 1)), 2)
 
 
-def call(kernel, inputs, outputs, scratch, scalars=0, cost=0, limit=60, grid=None, in_specs=None, out_specs=None):
+def call(kernel, inputs, outputs, scratch, scalars=0, cost=0, limit=VMEM_LIMIT, grid=None, in_specs=None, out_specs=None):
     whole = pl.BlockSpec(memory_space=pltpu.VMEM)
     if in_specs is None:
         in_specs = [pl.BlockSpec(memory_space=pltpu.SMEM)] * scalars + [whole] * (len(inputs) - scalars)
@@ -909,35 +901,28 @@
     in_hbm = pl.BlockSpec(memory_space=pltpu.HBM)
     anywhere = pl.BlockSpec(memory_space=pl.ANY)
 
-    def variables(count, place, shift):
-        return pl.BlockSpec((PACK_TILE, count * 2 * STRIPES, LANES), lambda i: (i + shift, place, 0))
-
-    packs = modes // FIRST_TILE
-    (sent_first,) = call(
-        pack_first,
-        [rows],
-        [(groups, first_rows, LANES)],
-        [
-            vmem(packs, FIRST_TILE, 3 * 2 * STRIPES, LANES),
-            vmem(packs // 2, 3, groups, FIRST_TILE, LANES),
-            pltpu.SemaphoreType.DMA((packs,)),
-            pltpu.SemaphoreType.DMA((packs // 2, 3)),
-        ],
-        cost=10**8,
-        in_specs=[in_hbm],
-        out_specs=[in_hbm],
-    )
-    first = exchange(sent_first)
-    (sent_second,) = call(
-        pack_second,
-        [rows],
-        [(groups, modes, LANES)],
-        [],
-        cost=10**8,
-        grid=(modes // PACK_TILE,),
-        in_specs=[variables(2, 0, 0)],
-        out_specs=[pl.BlockSpec((groups, PACK_TILE, LANES), lambda i: (0, i, 0))],
-    )
+    packs = modes // PACK_TILE
+
+    def packed(first, with_last):
+        places = 3 if with_last else 2
+        (sent,) = call(
+            functools.partial(pack, first, with_last),
+            [rows],
+            [(groups, places * modes // 2, LANES)],
+            [
+                vmem(packs, PACK_TILE, (5 if with_last else 2) * 2 * STRIPES, LANES),
+                vmem(packs // 2, places, groups, PACK_TILE, LANES),
+                pltpu.SemaphoreType.DMA((packs,)),
+                pltpu.SemaphoreType.DMA((packs // 2, places)),
+            ],
+            cost=10**8,
+            in_specs=[in_hbm],
+            out_specs=[in_hbm],
+        )
+        return sent
+
+    first = exchange(packed(2, False))
+    sent_second = packed(0, True)
     sent_second, derivative, solve, wave, frequency, couple, positions = lax.optimization_barrier(
         (sent_second, derivative, solve, wave, frequency, couple, positions)
     )
@@ -968,11 +953,6 @@
         functools.partial(synthesis, True), first, modes, 0, [physical, physical, (8, LANES)], [grid, spectrum], 2 * 10**9
     )
     s1 = lax.ppermute(f1, "modes", neighbours)
-    f_last, g_last = spectral(
-        synthesis_half, first, modes // 2, 2, [half_physical] * 2, [grid, spectrum, turned], 10**9
-    )
-    s1, f_last, g_last = lax.optimization_barrier((s1, f_last, g_last))
-    s_last = lax.ppermute(f_last, "modes", neighbours)
     (back_first,) = call(
         functools.partial(force_analysis, False),
         [positions, f1, f1, s1, g1, derivative, backward, table, mean],
@@ -986,6 +966,11 @@
         functools.partial(synthesis, False), second, modes, 0, [physical, physical], [grid, spectrum], 2 * 10**9
     )
     s2 = lax.ppermute(f2, "modes", neighbours)
+    f_last, g_last = spectral(
+        synthesis_half, second, modes // 2, 2, [half_physical] * 2, [grid, spectrum, turned], 10**9
+    )
+    s2, f_last, g_last = lax.optimization_barrier((s2, f_last, g_last))
+    s_last = lax.ppermute(f_last, "modes", neighbours)
     (back_second,) = call(
         functools.partial(force_analysis, True),
         [positions, f1, f2, s2, g2, derivative, backward, table, f_last, s_last, g_last],
@@ -1037,7 +1022,6 @@
         ]
         + halves,
         cost=2 * 10**9,
-        limit=LAST_LIMIT,
         in_specs=[in_hbm, anywhere] + [in_hbm] * 4,
         out_specs=[in_hbm],
     )

time: 282 us -> 279 us (0.989)
  waiting for transfers between devices: 118 us -> 135 us
  local copies, waits for them, and re-layouts: 18.2 us -> 4.32 us
  other arithmetic: 4.5 us -> 0.83 us
    all_to_all x1, waiting for transfers between devices: 11.7 us -> 41.1 us  [local_halves(): second = exchange(sent_second)]
    all_to_all x1, waiting for transfers between devices: 10.1 us -> 2.32 us  [local_halves(): got_first = exchange(back_first)]
    all_to_all x1, waiting for transfers between devices: 45.5 us -> 38.4 us  [local_halves(): first = exchange(packed(2, False))]
    mul x5, local copies, waits for them, and re-layouts: 4.97 us -> 0.84 us  [solve_matrices(): blocks = same[None, :, None, :, None] * turned[:, :, :, None, :]]
  transfers between devices with their start and end apart: 7 -> 7, of which waited for: 6 -> 6; matrix products, arithmetic and copies ran while one was open for 7% -> 1% of each run, Pallas kernels for 34% -> 34%
where the time goes in v5:
time: 279 us; the launch traced here: 278 us
  waiting for transfers between devices  135 us (48%)
  Pallas kernels  115 us (41%)
  starting transfers between devices  22.3 us (8%)
  local copies, waits for them, and re-layouts  4.32 us (2%)
    pallas_call x9, Pallas kernels, call(): pl.pallas_call(kernel, out_shape=[jax.ShapeDtypeStruct(shape, jnp.float32...  115 us
    all_to_all x1, waiting for transfers between devices, local_halves(): got_second = exchange(back_second)  48.6 us
    all_to_all x1, waiting for transfers between devices, local_halves(): second = exchange(sent_second)  41.1 us
    all_to_all x1, waiting for transfers between devices, local_halves(): first = exchange(packed(2, False))  38.4 us
    all_to_all x1, starting transfers between devices, local_halves(): first = exchange(packed(2, False))  6.7 us
  transfers between devices with their start and end apart: 7, of which 6 were waited for; matrix products, arithmetic and copies ran while one was open for 1% of the time, Pallas kernels for 34%

profile of v5, /device:TPU:13, one launch (start us, length us, event | category | flops | bytes accessed | tf_op | source)
XLA Modules:
  0.0 278.2 jit_solution(3355106811791020022)
XLA Ops:
  0.0 3.9 %shard_map.101 = f32[16,256,128]{2,1,0:T(8,128)} custom-call(f32[256,40,128]{2,1,0:T(8,128)} %bitcast.37), custom_call_target="tpu_custom_call" | custom-call | flops 100000000 | bytes 8388608 | tf_op jit(solution)/shard_map/pallas_call | solution.py:854
  4.0 6.7 %all-to-all-start = ((f32[16,256,128]{2,1,0:T(8,128)}), f32[16,256,128]{2,1,0:T(8,128)}, u32[]{:S(2)}, u32[]{:S(2)}) async-start(f32[16,256,128]{2,1,0:T(8,128)} %shard_map.101), calls=%async_computation | async-start | bytes 4194304 | tf_op jit(solution)/shard_map/all_to_all | solution.py:924
  10.7 0.3 slice_reduce_fusion.1
  11.8 0.1 mul.162
  12.1 0.1 copy.23
  12.4 0.1 copy.22
  12.7 0.2 mul.165
  12.8 0.3 mul.166
  13.2 0.1 broadcast_multiply_fusion
  13.3 0.3 mul.160
  13.6 5.6 %shard_map.100 = f32[16,384,128]{2,1,0:T(8,128)} custom-call(f32[256,40,128]{2,1,0:T(8,128)} %bitcast.38), custom_call_target="tpu_custom_call" | custom-call | flops 100000000 | bytes 8388608 | tf_op jit(solution)/shard_map/pallas_call | solution.py:854
  19.8 38.4 %all-to-all-done.r_ref = f32[16,256,128]{2,1,0:T(8,128)} async-done(((f32[16,256,128]{2,1,0:T(8,128)}), f32[16,256,128]{2,1,0:T(8,128)}, u32[]{:S(2)}, u32[]{:S(2)}) %all-to-all-start) | async-done | bytes 2097184 | tf_op jit(solution)/shard_map/all_to_all | solution.py:924
  58.2 4.9 %all-to-all-start.2 = ((f32[16,384,128]{2,1,0:T(8,128)}), f32[16,384,128]{2,1,0:T(8,128)}, u32[]{:S(2)}, u32[]{:S(2)}) async-start(f32[16,384,128]{2,1,0:T(8,128)} %shard_map.100), calls=%async_computation.2 | async-start | bytes 6291456 | tf_op jit(solution)/shard_map/all_to_all | solution.py:929
  63.1 13.0 %shard_map.102 = (f32[17,128,128]{2,1,0:T(8,128)}, f32[17,128,128]{2,1,0:T(8,128)}, f32[8,128]{1,0:T(8,128)S(1)}) custom-call(s32[4096]{0:T(1024)S(1)} %bitcast.31, f32[16,256,128]{2,1,0:T(8,128)} %all-to-all-done.r_ref, bf16[512,256]{1,0:T(8,128)(2,1)S(1)} %copy-done.1, f32[32,8,128]{2,1,0:T(8,128)S(1)} %copy-done.2), custom_call_target="tpu_custom_call" | custom-call | flops 2000000000 | bytes 8388608 | tf_op jit(solution)/shard_map/pallas_call | solution.py:854
  76.2 0.4 collective-permute-start
  76.5 2.6 collective-permute-done.s_ref
  79.1 1.0 copy-done.10
  80.2 11.9 %shard_map.103 = f32[16,264,128]{2,1,0:T(8,128)} custom-call(s32[4096]{0:T(1024)S(1)} %bitcast.32, f32[17,128,128]{2,1,0:T(8,128)} %get-tuple-element.23.vw_ref.f_ref, f32[17,128,128]{2,1,0:T(8,128)} %get-tuple-element.23.vw_ref.f_ref, f32[17,128,128]{2,1,0:T(8,128)} %copy-done.10, f32[17,128,128]{2,1,0:T(8,128)} %get-tuple-element.24.g_ref, ...), custom_call_target="tpu_custom_call" | custom-call | flops 2000000000 | bytes 8388608 | tf_op jit(solution)/shard_map/pallas_call | solution.py:854
  92.0 41.1 %all-to-all-done.2.r_ref = f32[16,384,128]{2,1,0:T(8,128)} async-done(((f32[16,384,128]{2,1,0:T(8,128)}), f32[16,384,128]{2,1,0:T(8,128)}, u32[]{:S(2)}, u32[]{:S(2)}) %all-to-all-start.2) | async-done | bytes 3145760 | tf_op jit(solution)/shard_map/all_to_all | solution.py:929
  133.1 4.9 %all-to-all-start.1 = ((f32[16,264,128]{2,1,0:T(8,128)}), f32[16,264,128]{2,1,0:T(8,128)}, u32[]{:S(2)}, u32[]{:S(2)}) async-start(f32[16,264,128]{2,1,0:T(8,128)} %shard_map.103), calls=%async_computation.1 | async-start | bytes 4325376 | tf_op jit(solution)/shard_map/all_to_all | solution.py:964
  138.0 12.9 %shard_map.105 = (f32[17,128,128]{2,1,0:T(8,128)}, f32[17,128,128]{2,1,0:T(8,128)}) custom-call(s32[4096]{0:T(1024)S(1)} %bitcast.33, f32[16,384,128]{2,1,0:T(8,128)} %all-to-all-done.2.r_ref, bf16[512,256]{1,0:T(8,128)(2,1)S(1)} %copy-done.1, f32[32,8,128]{2,1,0:T(8,128)S(1)} %copy-done.2), custom_call_target="tpu_custom_call" | custom-call | flops 2000000000 | bytes 8388608 | tf_op jit(solution)/shard_map/pallas_call | solution.py:854
  150.9 0.4 collective-permute-start.1
  151.3 9.5 %shard_map.106 = (f32[17,64,128]{2,1,0:T(8,128)S(1)}, f32[17,64,128]{2,1,0:T(8,128)}) custom-call(s32[4096]{0:T(1024)S(1)} %bitcast.34, f32[16,384,128]{2,1,0:T(8,128)} %all-to-all-done.2.r_ref, bf16[512,256]{1,0:T(8,128)(2,1)S(1)} %copy-done.1, f32[32,8,128]{2,1,0:T(8,128)S(1)} %copy-done.2), custom_call_target="tpu_custom_call" | custom-call | flops 1000000000 | bytes 8388608 | tf_op jit(solution)/shard_map/pallas_call | solution.py:854
  160.8 0.2 collective-permute-start.2
  161.0 1.8 collective-permute-done.2.refs_1_
  162.8 0.8 copy-done.11
  163.6 21.0 %shard_map.107 = f32[16,384,128]{2,1,0:T(8,128)} custom-call(s32[4096]{0:T(1024)S(1)} %bitcast.35, f32[17,128,128]{2,1,0:T(8,128)} %get-tuple-element.23.vw_ref.f_ref, f32[17,128,128]{2,1,0:T(8,128)} %get-tuple-element.32.f_ref, f32[17,128,128]{2,1,0:T(8,128)} %copy-done.9, f32[17,128,128]{2,1,0:T(8,128)} %get-tuple-element.36.g_ref, ...), custom_call_target="tpu_custom_call" | custom-call | flops 3000000000 | bytes 8388608 | tf_op jit(solution)/shard_map/pallas_call | solution.py:854
  184.6 2.3 all-to-all-done.1.b_ref.mean_ref
  186.9 4.9 %all-to-all-start.3 = ((f32[16,384,128]{2,1,0:T(8,128)}), f32[16,384,128]{2,1,0:T(8,128)}, u32[]{:S(2)}, u32[]{:S(2)}) async-start(f32[16,384,128]{2,1,0:T(8,128)} %shard_map.107), calls=%async_computation.3 | async-start | bytes 6291456 | tf_op jit(solution)/shard_map/all_to_all | solution.py:982
  191.8 21.4 %shard_map.104.first_hbm = f32[4,41,64,128]{3,2,1,0:T(8,128)} custom-call(f32[256,40,128]{2,1,0:T(8,128)} %bitcast.39, f32[16,264,128]{2,1,0:T(8,128)} %all-to-all-done.1.b_ref.mean_ref, f32[16,264,128]{2,1,0:T(8,128)} %all-to-all-done.1.b_ref.mean_ref, f32[4,128]{1,0:T(4,128)S(1)} %bitcast.36, f32[100,128]{1,0:T(8,128)S(1)} %reshape.246.coup_ref.refs_0_, ...), custom_call_target="tpu_custom_call" | custom-call | flops 3000000000 | bytes 8388608 | tf_op jit(solution)/shard_map/pallas_call | solution.py:854
  213.2 48.6 %all-to-all-done.3.b_any = f32[16,384,128]{2,1,0:T(8,128)} async-done(((f32[16,384,128]{2,1,0:T(8,128)}), f32[16,384,128]{2,1,0:T(8,128)}, u32[]{:S(2)}, u32[]{:S(2)}) %all-to-all-start.3) | async-done | bytes 3145760 | tf_op jit(solution)/shard_map/all_to_all | solution.py:982
  261.8 16.2 %shard_map.108 = f32[256,40,128]{2,1,0:T(8,128)} custom-call(f32[4,41,64,128]{3,2,1,0:T(8,128)} %shard_map.104.first_hbm, f32[16,384,128]{2,1,0:T(8,128)} %all-to-all-done.3.b_any, f32[100,128]{1,0:T(8,128)S(1)} %reshape.246.coup_ref.refs_0_, f32[256,128]{1,0:T(8,128)S(1)} %broadcast_in_dim.30.kz_ref.refs_1_, ...), custom_call_target="tpu_custom_call" | custom-call | flops 2000000000 | bytes 8388608 | tf_op jit(solution)/shard_map/pallas_call | solution.py:854
  (56 shorter events, 1.8 us)
Async XLA Ops:
  3.9 6.7 %copy-start.8 = (s32[8]{0:T(128)S(1)}, s32[8]{0:T(128)}, u32[]{:S(2)}) copy-start(s32[8]{0:T(128)} %param.12) | copy-start | bytes 100
  3.9 6.8 %copy-start.4 = (f32[8,64,64]{2,1,0:T(8,128)S(1)}, f32[8,64,64]{2,1,0:T(8,128)}, u32[]{:S(2)}) copy-start(f32[8,64,64]{2,1,0:T(8,128)} %param.15) | copy-start | bytes 393220
  3.9 7.3 %copy-start.6 = (f32[64,64]{1,0:T(8,128)S(1)}, f32[64,64]{1,0:T(8,128)}, u32[]{:S(2)}) copy-start(f32[64,64]{1,0:T(8,128)} %param.16) | copy-start | bytes 49156
  4.0 7.8 %copy-start.5 = (f32[25,512]{1,0:T(8,128)S(1)}, f32[25,512]{1,0:T(8,128)}, u32[]{:S(2)}) copy-start(f32[25,512]{1,0:T(8,128)} %param.14) | copy-start | bytes 153604
  4.0 54.2 %all-to-all-start = ((f32[16,256,128]{2,1,0:T(8,128)}), f32[16,256,128]{2,1,0:T(8,128)}, u32[]{:S(2)}, u32[]{:S(2)}) async-start(f32[16,256,128]{2,1,0:T(8,128)} %shard_map.101), calls=%async_computation | async-start | bytes 4194304 | tf_op jit(solution)/shard_map/all_to_all | solution.py:924
  13.6 5.6 %copy-start.7 = (s32[4096,2]{0,1:T(2,128)S(1)}, s32[4096,2]{0,1:T(2,128)}, u32[]{:S(2)}) copy-start(s32[4096,2]{0,1:T(2,128)} %param.11) | copy-start | bytes 98308
  19.7 43.4 %copy-start.1 = (bf16[512,256]{1,0:T(8,128)(2,1)S(1)}, bf16[512,256]{1,0:T(8,128)(2,1)}, u32[]{:S(2)}) copy-start(bf16[512,256]{1,0:T(8,128)(2,1)} %constant.125.clone.w_ref) | copy-start | bytes 786436
  19.7 43.4 %copy-start.2 = (f32[32,8,128]{2,1,0:T(8,128)S(1)}, f32[32,8,128]{2,1,0:T(8,128)}, u32[]{:S(2)}) copy-start(f32[32,8,128]{2,1,0:T(8,128)} %constant.127.clone.tab_ref) | copy-start | bytes 393220
  58.2 74.9 %all-to-all-start.2 = ((f32[16,384,128]{2,1,0:T(8,128)}), f32[16,384,128]{2,1,0:T(8,128)}, u32[]{:S(2)}, u32[]{:S(2)}) async-start(f32[16,384,128]{2,1,0:T(8,128)} %shard_map.100), calls=%async_computation.2 | async-start | bytes 6291456 | tf_op jit(solution)/shard_map/all_to_all | solution.py:929
  63.1 17.0 %copy-start.3 = (bf16[512,128]{1,0:T(8,128)(2,1)S(1)}, bf16[512,128]{1,0:T(8,128)(2,1)}, u32[]{:S(2)}) copy-start(bf16[512,128]{1,0:T(8,128)(2,1)} %constant.126.clone.w_ref) | copy-start | bytes 393220
  76.2 3.0 %collective-permute-start = (f32[17,128,128]{2,1,0:T(8,128)}, f32[17,128,128]{2,1,0:T(8,128)S(1)}, u32[]{:S(2)}, u32[]{:S(2)}) collective-permute-start(f32[17,128,128]{2,1,0:T(8,128)} %get-tuple-element.23.vw_ref.f_ref), channel_id=1, source_target_pairs={{0,1},{1,0},{2,3},{3,2},{4,5},{5,4},{6,7},{7,6},{8,9},{9,8},{10,11... | collective-permute-start | bytes 3342344 | tf_op jit(solution)/shard_map/ppermute | solution.py:955
  79.1 1.0 copy-start.10
  133.1 53.8 %all-to-all-start.1 = ((f32[16,264,128]{2,1,0:T(8,128)}), f32[16,264,128]{2,1,0:T(8,128)}, u32[]{:S(2)}, u32[]{:S(2)}) async-start(f32[16,264,128]{2,1,0:T(8,128)} %shard_map.103), calls=%async_computation.1 | async-start | bytes 4325376 | tf_op jit(solution)/shard_map/all_to_all | solution.py:964
  150.9 9.9 %collective-permute-start.1 = (f32[17,128,128]{2,1,0:T(8,128)}, f32[17,128,128]{2,1,0:T(8,128)S(1)}, u32[]{:S(2)}, u32[]{:S(2)}) collective-permute-start(f32[17,128,128]{2,1,0:T(8,128)} %get-tuple-element.32.f_ref), channel_id=1, source_target_pairs={{0,1},{1,0},{2,3},{3,2},{4,5},{5,4},{6,7},{7,6},{8,9},{9,8},{10,11... | collective-permute-start | bytes 3342344 | tf_op jit(solution)/shard_map/ppermute | solution.py:968
  160.8 2.0 copy-start.9
  160.8 2.0 collective-permute-start.2
  162.8 0.8 copy-start.11
  184.6 7.2 %copy-start = (f32[512]{0:T(512)S(1)}, f32[512]{0:T(512)}, u32[]{:S(2)}) copy-start(f32[512]{0:T(512)} %param.13) | copy-start | bytes 6148
  186.9 74.9 %all-to-all-start.3 = ((f32[16,384,128]{2,1,0:T(8,128)}), f32[16,384,128]{2,1,0:T(8,128)}, u32[]{:S(2)}, u32[]{:S(2)}) async-start(f32[16,384,128]{2,1,0:T(8,128)} %shard_map.107), calls=%async_computation.3 | async-start | bytes 6291456 | tf_op jit(solution)/shard_map/all_to_all | solution.py:982

commit v6 on v5

--- a/solution.py
+++ b/solution.py
@@ -609,6 +609,7 @@
 def relax(stripe, x_of, parts, cross, kz_ref, om_ref, coup_ref, sw_ref, rh_ref, rl_ref, zh_ref, zl_ref):
     values = {part: x_of(stripe, part) for part in parts}
     rotation = kz_ref[...] * cross - om_ref[...]
+    outs = []
     for k in range(5):
         out_re = jnp.zeros((TILE, LANES), jnp.float32)
         out_im = out_re
@@ -621,11 +622,9 @@
             weight = coup_ref[pl.ds((k * 5 + j) * STRIPES + stripe, 1), :]
             out_re = out_re - weight * values[2 * j]
             out_im = out_im - weight * values[2 * j + 1]
-        for part, out in ((2 * k, out_re), (2 * k + 1, out_im)):
-            rows = pl.ds(part * TILE, TILE)
-            rh_ref[stripe, rows, :], rl_ref[stripe, rows, :] = split(out)
-    high = jnp.concatenate([rh_ref[stripe], zh_ref[...]], 1)
-    low_rows = jnp.concatenate([rl_ref[stripe], zl_ref[...]], 1)
+        outs += [split(out_re), split(out_im)]
+    high = jnp.concatenate([jnp.concatenate([out[0] for out in outs], 0), zh_ref[...]], 1)
+    low_rows = jnp.concatenate([jnp.concatenate([out[1] for out in outs], 0), zl_ref[...]], 1)
     return three_pass(high, low_rows, sw_ref[stripe]).reshape(PARTS, TILE, LANES)
 
 
@@ -746,12 +745,9 @@
         pair = block_transpose([b_ref[group] for group in groups], low, even)
         last = block_transpose([t_ref[group] for group in groups], low, even)
         last = (jnp.where(far, last[1], last[0]), jnp.where(far, last[3], last[2]))
-        for place, value in enumerate((pair[0], pair[2], pair[1], pair[3]) + last):
-            rows = pl.ds(place * TILE, TILE)
-            rh_ref[stripe, rows, :], rl_ref[stripe, rows, :] = split(march_step * value)
-        rows = pl.ds(0, count * TILE)
+        late = jnp.concatenate((pair[0], pair[2], pair[1], pair[3]) + last, 0)
         weights = sw_ref[stripe, pl.ds(0, LANES), :]
-        added = three_pass(rh_ref[stripe, rows, :], rl_ref[stripe, rows, :], weights)
+        added = three_pass(*split(march_step * late), weights)
         right_ref[stripe] = added.reshape(count, TILE, LANES)
 
     def right_of(stripe, part):

time: 279 us -> 278 us (level)
  Pallas kernels: 115 us -> 111 us
  waiting for transfers between devices: 135 us -> 138 us
    pallas_call x9, Pallas kernels: 115 us -> 111 us  [call(): pl.pallas_call(kernel, out_shape=[jax.ShapeDtypeStruct(shape, jnp.float32...]
    all_to_all x1, waiting for transfers between devices: 48.6 us -> 52 us  [local_halves(): got_second = exchange(back_second)]
  transfers between devices with their start and end apart: 7 -> 7, of which waited for: 6 -> 6; matrix products, arithmetic and copies ran while one was open for 1% -> 1% of each run, Pallas kernels for 34% -> 33%
where the time goes in v6:
time: 278 us; the launch traced here: 277 us
  waiting for transfers between devices  138 us (50%)
  Pallas kernels  111 us (40%)
  starting transfers between devices  22.3 us (8%)
  local copies, waits for them, and re-layouts  4.32 us (2%)
    pallas_call x9, Pallas kernels, call(): pl.pallas_call(kernel, out_shape=[jax.ShapeDtypeStruct(shape, jnp.float32...  111 us
    all_to_all x1, waiting for transfers between devices, local_halves(): got_second = exchange(back_second)  52 us
    all_to_all x1, waiting for transfers between devices, local_halves(): second = exchange(sent_second)  41.1 us
    all_to_all x1, waiting for transfers between devices, local_halves(): first = exchange(packed(2, False))  38.4 us
    all_to_all x1, starting transfers between devices, local_halves(): first = exchange(packed(2, False))  6.7 us
  transfers between devices with their start and end apart: 7, of which 6 were waited for; matrix products, arithmetic and copies ran while one was open for 1% of the time, Pallas kernels for 33%

profile of v6, /device:TPU:13, one launch (start us, length us, event | category | flops | bytes accessed | tf_op | source)
XLA Modules:
  0.0 277.1 jit_solution(5800745464549832102)
XLA Ops:
  0.0 3.9 %shard_map.101 = f32[16,256,128]{2,1,0:T(8,128)} custom-call(f32[256,40,128]{2,1,0:T(8,128)} %bitcast.37), custom_call_target="tpu_custom_call" | custom-call | flops 100000000 | bytes 8388608 | tf_op jit(solution)/shard_map/pallas_call | solution.py:850
  4.0 6.7 %all-to-all-start = ((f32[16,256,128]{2,1,0:T(8,128)}), f32[16,256,128]{2,1,0:T(8,128)}, u32[]{:S(2)}, u32[]{:S(2)}) async-start(f32[16,256,128]{2,1,0:T(8,128)} %shard_map.101), calls=%async_computation | async-start | bytes 4194304 | tf_op jit(solution)/shard_map/all_to_all | solution.py:920
  10.7 0.3 slice_reduce_fusion.1
  11.8 0.1 mul.162
  12.1 0.1 copy.23
  12.4 0.1 copy.22
  12.7 0.2 mul.165
  12.8 0.3 mul.166
  13.2 0.1 broadcast_multiply_fusion
  13.3 0.3 mul.160
  13.6 5.6 %shard_map.100 = f32[16,384,128]{2,1,0:T(8,128)} custom-call(f32[256,40,128]{2,1,0:T(8,128)} %bitcast.38), custom_call_target="tpu_custom_call" | custom-call | flops 100000000 | bytes 8388608 | tf_op jit(solution)/shard_map/pallas_call | solution.py:850
  19.8 38.4 %all-to-all-done.r_ref = f32[16,256,128]{2,1,0:T(8,128)} async-done(((f32[16,256,128]{2,1,0:T(8,128)}), f32[16,256,128]{2,1,0:T(8,128)}, u32[]{:S(2)}, u32[]{:S(2)}) %all-to-all-start) | async-done | bytes 2097184 | tf_op jit(solution)/shard_map/all_to_all | solution.py:920
  58.2 4.9 %all-to-all-start.2 = ((f32[16,384,128]{2,1,0:T(8,128)}), f32[16,384,128]{2,1,0:T(8,128)}, u32[]{:S(2)}, u32[]{:S(2)}) async-start(f32[16,384,128]{2,1,0:T(8,128)} %shard_map.100), calls=%async_computation.2 | async-start | bytes 6291456 | tf_op jit(solution)/shard_map/all_to_all | solution.py:925
  63.1 13.0 %shard_map.102 = (f32[17,128,128]{2,1,0:T(8,128)}, f32[17,128,128]{2,1,0:T(8,128)}, f32[8,128]{1,0:T(8,128)S(1)}) custom-call(s32[4096]{0:T(1024)S(1)} %bitcast.31, f32[16,256,128]{2,1,0:T(8,128)} %all-to-all-done.r_ref, bf16[512,256]{1,0:T(8,128)(2,1)S(1)} %copy-done.1, f32[32,8,128]{2,1,0:T(8,128)S(1)} %copy-done.2), custom_call_target="tpu_custom_call" | custom-call | flops 2000000000 | bytes 8388608 | tf_op jit(solution)/shard_map/pallas_call | solution.py:850
  76.2 0.4 collective-permute-start
  76.5 2.6 collective-permute-done.s_ref
  79.1 1.0 copy-done.10
  80.2 11.9 %shard_map.103 = f32[16,264,128]{2,1,0:T(8,128)} custom-call(s32[4096]{0:T(1024)S(1)} %bitcast.32, f32[17,128,128]{2,1,0:T(8,128)} %get-tuple-element.23.vw_ref.f_ref, f32[17,128,128]{2,1,0:T(8,128)} %get-tuple-element.23.vw_ref.f_ref, f32[17,128,128]{2,1,0:T(8,128)} %copy-done.10, f32[17,128,128]{2,1,0:T(8,128)} %get-tuple-element.24.g_ref, ...), custom_call_target="tpu_custom_call" | custom-call | flops 2000000000 | bytes 8388608 | tf_op jit(solution)/shard_map/pallas_call | solution.py:850
  92.0 41.1 %all-to-all-done.2.r_ref = f32[16,384,128]{2,1,0:T(8,128)} async-done(((f32[16,384,128]{2,1,0:T(8,128)}), f32[16,384,128]{2,1,0:T(8,128)}, u32[]{:S(2)}, u32[]{:S(2)}) %all-to-all-start.2) | async-done | bytes 3145760 | tf_op jit(solution)/shard_map/all_to_all | solution.py:925
  133.1 4.9 %all-to-all-start.1 = ((f32[16,264,128]{2,1,0:T(8,128)}), f32[16,264,128]{2,1,0:T(8,128)}, u32[]{:S(2)}, u32[]{:S(2)}) async-start(f32[16,264,128]{2,1,0:T(8,128)} %shard_map.103), calls=%async_computation.1 | async-start | bytes 4325376 | tf_op jit(solution)/shard_map/all_to_all | solution.py:960
  138.0 12.9 %shard_map.105 = (f32[17,128,128]{2,1,0:T(8,128)}, f32[17,128,128]{2,1,0:T(8,128)}) custom-call(s32[4096]{0:T(1024)S(1)} %bitcast.33, f32[16,384,128]{2,1,0:T(8,128)} %all-to-all-done.2.r_ref, bf16[512,256]{1,0:T(8,128)(2,1)S(1)} %copy-done.1, f32[32,8,128]{2,1,0:T(8,128)S(1)} %copy-done.2), custom_call_target="tpu_custom_call" | custom-call | flops 2000000000 | bytes 8388608 | tf_op jit(solution)/shard_map/pallas_call | solution.py:850
  150.9 0.4 collective-permute-start.1
  151.3 9.5 %shard_map.106 = (f32[17,64,128]{2,1,0:T(8,128)S(1)}, f32[17,64,128]{2,1,0:T(8,128)}) custom-call(s32[4096]{0:T(1024)S(1)} %bitcast.34, f32[16,384,128]{2,1,0:T(8,128)} %all-to-all-done.2.r_ref, bf16[512,256]{1,0:T(8,128)(2,1)S(1)} %copy-done.1, f32[32,8,128]{2,1,0:T(8,128)S(1)} %copy-done.2), custom_call_target="tpu_custom_call" | custom-call | flops 1000000000 | bytes 8388608 | tf_op jit(solution)/shard_map/pallas_call | solution.py:850
  160.8 0.2 collective-permute-start.2
  161.0 1.8 collective-permute-done.2.refs_1_
  162.8 0.8 copy-done.11
  163.6 21.0 %shard_map.107 = f32[16,384,128]{2,1,0:T(8,128)} custom-call(s32[4096]{0:T(1024)S(1)} %bitcast.35, f32[17,128,128]{2,1,0:T(8,128)} %get-tuple-element.23.vw_ref.f_ref, f32[17,128,128]{2,1,0:T(8,128)} %get-tuple-element.32.f_ref, f32[17,128,128]{2,1,0:T(8,128)} %copy-done.9, f32[17,128,128]{2,1,0:T(8,128)} %get-tuple-element.36.g_ref, ...), custom_call_target="tpu_custom_call" | custom-call | flops 3000000000 | bytes 8388608 | tf_op jit(solution)/shard_map/pallas_call | solution.py:850
  184.6 2.3 all-to-all-done.1.b_ref.mean_ref
  186.9 4.9 %all-to-all-start.3 = ((f32[16,384,128]{2,1,0:T(8,128)}), f32[16,384,128]{2,1,0:T(8,128)}, u32[]{:S(2)}, u32[]{:S(2)}) async-start(f32[16,384,128]{2,1,0:T(8,128)} %shard_map.107), calls=%async_computation.3 | async-start | bytes 6291456 | tf_op jit(solution)/shard_map/all_to_all | solution.py:978
  191.8 18.0 %shard_map.104.first_hbm = f32[4,41,64,128]{3,2,1,0:T(8,128)} custom-call(f32[256,40,128]{2,1,0:T(8,128)} %bitcast.39, f32[16,264,128]{2,1,0:T(8,128)} %all-to-all-done.1.b_ref.mean_ref, f32[16,264,128]{2,1,0:T(8,128)} %all-to-all-done.1.b_ref.mean_ref, f32[4,128]{1,0:T(4,128)S(1)} %bitcast.36, f32[100,128]{1,0:T(8,128)S(1)} %reshape.246.coup_ref.refs_0_, ...), custom_call_target="tpu_custom_call" | custom-call | flops 3000000000 | bytes 8388608 | tf_op jit(solution)/shard_map/pallas_call | solution.py:850
  209.8 52.0 %all-to-all-done.3.b_any = f32[16,384,128]{2,1,0:T(8,128)} async-done(((f32[16,384,128]{2,1,0:T(8,128)}), f32[16,384,128]{2,1,0:T(8,128)}, u32[]{:S(2)}, u32[]{:S(2)}) %all-to-all-start.3) | async-done | bytes 3145760 | tf_op jit(solution)/shard_map/all_to_all | solution.py:978
  261.8 15.1 %shard_map.108 = f32[256,40,128]{2,1,0:T(8,128)} custom-call(f32[4,41,64,128]{3,2,1,0:T(8,128)} %shard_map.104.first_hbm, f32[16,384,128]{2,1,0:T(8,128)} %all-to-all-done.3.b_any, f32[100,128]{1,0:T(8,128)S(1)} %reshape.246.coup_ref.refs_0_, f32[256,128]{1,0:T(8,128)S(1)} %broadcast_in_dim.30.kz_ref.refs_1_, ...), custom_call_target="tpu_custom_call" | custom-call | flops 2000000000 | bytes 8388608 | tf_op jit(solution)/shard_map/pallas_call | solution.py:850
  (56 shorter events, 1.8 us)
Async XLA Ops:
  3.9 6.7 %copy-start.8 = (s32[8]{0:T(128)S(1)}, s32[8]{0:T(128)}, u32[]{:S(2)}) copy-start(s32[8]{0:T(128)} %param.12) | copy-start | bytes 100
  3.9 6.8 %copy-start.4 = (f32[8,64,64]{2,1,0:T(8,128)S(1)}, f32[8,64,64]{2,1,0:T(8,128)}, u32[]{:S(2)}) copy-start(f32[8,64,64]{2,1,0:T(8,128)} %param.15) | copy-start | bytes 393220
  3.9 7.3 %copy-start.6 = (f32[64,64]{1,0:T(8,128)S(1)}, f32[64,64]{1,0:T(8,128)}, u32[]{:S(2)}) copy-start(f32[64,64]{1,0:T(8,128)} %param.16) | copy-start | bytes 49156
  4.0 7.8 %copy-start.5 = (f32[25,512]{1,0:T(8,128)S(1)}, f32[25,512]{1,0:T(8,128)}, u32[]{:S(2)}) copy-start(f32[25,512]{1,0:T(8,128)} %param.14) | copy-start | bytes 153604
  4.0 54.2 %all-to-all-start = ((f32[16,256,128]{2,1,0:T(8,128)}), f32[16,256,128]{2,1,0:T(8,128)}, u32[]{:S(2)}, u32[]{:S(2)}) async-start(f32[16,256,128]{2,1,0:T(8,128)} %shard_map.101), calls=%async_computation | async-start | bytes 4194304 | tf_op jit(solution)/shard_map/all_to_all | solution.py:920
  13.6 5.6 %copy-start.7 = (s32[4096,2]{0,1:T(2,128)S(1)}, s32[4096,2]{0,1:T(2,128)}, u32[]{:S(2)}) copy-start(s32[4096,2]{0,1:T(2,128)} %param.11) | copy-start | bytes 98308
  19.7 43.4 %copy-start.1 = (bf16[512,256]{1,0:T(8,128)(2,1)S(1)}, bf16[512,256]{1,0:T(8,128)(2,1)}, u32[]{:S(2)}) copy-start(bf16[512,256]{1,0:T(8,128)(2,1)} %constant.125.clone.w_ref) | copy-start | bytes 786436
  19.7 43.4 %copy-start.2 = (f32[32,8,128]{2,1,0:T(8,128)S(1)}, f32[32,8,128]{2,1,0:T(8,128)}, u32[]{:S(2)}) copy-start(f32[32,8,128]{2,1,0:T(8,128)} %constant.127.clone.tab_ref) | copy-start | bytes 393220
  58.2 74.9 %all-to-all-start.2 = ((f32[16,384,128]{2,1,0:T(8,128)}), f32[16,384,128]{2,1,0:T(8,128)}, u32[]{:S(2)}, u32[]{:S(2)}) async-start(f32[16,384,128]{2,1,0:T(8,128)} %shard_map.100), calls=%async_computation.2 | async-start | bytes 6291456 | tf_op jit(solution)/shard_map/all_to_all | solution.py:925
  63.1 17.0 %copy-start.3 = (bf16[512,128]{1,0:T(8,128)(2,1)S(1)}, bf16[512,128]{1,0:T(8,128)(2,1)}, u32[]{:S(2)}) copy-start(bf16[512,128]{1,0:T(8,128)(2,1)} %constant.126.clone.w_ref) | copy-start | bytes 393220
  76.2 3.0 %collective-permute-start = (f32[17,128,128]{2,1,0:T(8,128)}, f32[17,128,128]{2,1,0:T(8,128)S(1)}, u32[]{:S(2)}, u32[]{:S(2)}) collective-permute-start(f32[17,128,128]{2,1,0:T(8,128)} %get-tuple-element.23.vw_ref.f_ref), channel_id=1, source_target_pairs={{0,1},{1,0},{2,3},{3,2},{4,5},{5,4},{6,7},{7,6},{8,9},{9,8},{10,11... | collective-permute-start | bytes 3342344 | tf_op jit(solution)/shard_map/ppermute | solution.py:951
  79.1 1.0 copy-start.10
  133.1 53.8 %all-to-all-start.1 = ((f32[16,264,128]{2,1,0:T(8,128)}), f32[16,264,128]{2,1,0:T(8,128)}, u32[]{:S(2)}, u32[]{:S(2)}) async-start(f32[16,264,128]{2,1,0:T(8,128)} %shard_map.103), calls=%async_computation.1 | async-start | bytes 4325376 | tf_op jit(solution)/shard_map/all_to_all | solution.py:960
  150.9 9.9 %collective-permute-start.1 = (f32[17,128,128]{2,1,0:T(8,128)}, f32[17,128,128]{2,1,0:T(8,128)S(1)}, u32[]{:S(2)}, u32[]{:S(2)}) collective-permute-start(f32[17,128,128]{2,1,0:T(8,128)} %get-tuple-element.32.f_ref), channel_id=1, source_target_pairs={{0,1},{1,0},{2,3},{3,2},{4,5},{5,4},{6,7},{7,6},{8,9},{9,8},{10,11... | collective-permute-start | bytes 3342344 | tf_op jit(solution)/shard_map/ppermute | solution.py:964
  160.8 2.0 copy-start.9
  160.8 2.0 collective-permute-start.2
  162.8 0.8 copy-start.11
  184.6 7.2 %copy-start = (f32[512]{0:T(512)S(1)}, f32[512]{0:T(512)}, u32[]{:S(2)}) copy-start(f32[512]{0:T(512)} %param.13) | copy-start | bytes 6148
  186.9 74.9 %all-to-all-start.3 = ((f32[16,384,128]{2,1,0:T(8,128)}), f32[16,384,128]{2,1,0:T(8,128)}, u32[]{:S(2)}, u32[]{:S(2)}) async-start(f32[16,384,128]{2,1,0:T(8,128)} %shard_map.107), calls=%async_computation.3 | async-start | bytes 6291456 | tf_op jit(solution)/shard_map/all_to_all | solution.py:978
